TPU v7x, 32 devices: a whole 2x2x4 slice. The times are simulated.
32 devices in a mesh: grp: 4 (over z), gx: 4 (over y, x), gy: 2 (over core).
Axes of the slice: x: 2, y: 2, z: 4, core: 2. Of those that a mesh axis runs over, the one named last changes fastest.
Arguments:
- fluid_temp: float32 [64, 256, 1024], P('gx', 'gy', 'grp'), may hold values from -6 to 6
- active: int32 [64, 256, 1024], P('gx', 'gy', 'grp'), may hold values 0 or 1
- fin_temp: float32 [256, 128, 512], P('grp', 'gx', 'gy'), may hold values from -6 to 6
- fin_source: float32 [256, 128, 512], P('grp', 'gx', 'gy'), may hold values from -6 to 6
- wall_owner: int32 [4, 2, 2048, 1], P('gx', 'gy'), may hold values from 0 to 3, as said below
- wall_target: int32 [4, 2, 2048], P('gx', 'gy'), may hold values from 0 to 8191, as said below
Outputs:
- fluid_new: float32 [64, 256, 1024], P('gx', 'gy', 'grp')
- fin_new: float32 [256, 128, 512], P('grp', 'gx', 'gy')
Inputs may be any that keep to these rules, and one draw needn't show every extreme that they name: `wall_owner`: among the 2048 wall cells of one column block (a, b), exactly 1024 name the owner a and at most 1024 name any one owner; in every draw one owner is named by exactly 1024 wall cells of every column block. `wall_target`: wall cell w = i * 128 + j names a root cell (2 * i + di) * 256 + 2 * j + dj of the 2 x 2 patch beneath it, di and dj being 0 or 1; the first wall cell of a block names its patch's first root cell, the last one its patch's last.
All inputs are finite; a program needn't handle non-finite values. No bound on the sum of `active` on one device may be relied on, other than what follows from the above.
Results may differ from a plain program's by a relative error of at most 0.00002.
Values sent between devices are 32-bit elements; how exact they have to be, the bound alone decides.
No kernel may reach another device: no remote copies, remote signals or barrier semaphores. Data moves between devices by JAX's collectives and lax.ppermute only.
A program may use at most 64 MiB of HBM per device.

v0:
```python
import jax
import jax.numpy as jnp
from jax import lax
from jax.experimental import pallas as pl
from jax.experimental.pallas import tpu as pltpu
from jax.sharding import PartitionSpec as P


FLUID_DIFFUSION = 1.0
FIN_CONDUCTION = 1.0
HEAT_COEF = 1.0
DIAG = 1.0 + 6.0 * FIN_CONDUCTION
SPECTRAL = 6.0 * FIN_CONDUCTION / DIAG
OMEGA = 1.0 / (1.0 - SPECTRAL * SPECTRAL / 2.0)
FLUID_SCALE = 1.0 / (1.0 + 6.0 * FLUID_DIFFUSION)
LANES = 128
PAD = 8
ROWS = 32
HIGHEST = lax.Precision.HIGHEST


def iota(shape, axis):
    return lax.broadcasted_iota(jnp.int32, shape, axis)


def repeat(count, body, step=8):
    def trip(k, carry):
        for j in range(step):
            body(k * step + j)
        return carry

    lax.fori_loop(0, count // step, trip, 0)


def tiles(value):
    return [value[:, k : k + LANES] for k in range(0, value.shape[1], LANES)]


def lane_neighbours(block, low, high):
    parts = tiles(block)
    lane = iota(parts[0].shape, 1)
    down = [pltpu.roll(part, 1, axis=1) for part in parts]
    up = [pltpu.roll(part, LANES - 1, axis=1) for part in parts]
    below = [jnp.where(lane == 0, a, b) for a, b in zip([low] + down[:-1], down)]
    above = [jnp.where(lane == LANES - 1, a, b) for a, b in zip(up[1:] + [high], up)]
    return jnp.concatenate([a + b for a, b in zip(below, above)], axis=1)


def interleave_matrix(count):
    row = iota((count, count), 0)
    col = iota((count, count), 1)
    half = count // 2
    source = jnp.where(col < half, 2 * col, 2 * (col - half) + 1)
    return (row == source).astype(jnp.float32)


def dot(a, b, contract):
    return lax.dot_general(
        a, b, (contract, ((), ())), precision=HIGHEST, preferred_element_type=jnp.float32
    )


def checker_pack(plane, parity):
    rows = plane.shape[0] // 2
    top = plane[:rows]
    bottom = plane[rows:]
    colour = (iota(top.shape, 0) + iota(top.shape, 1)) & 1
    return jnp.where(colour == parity, top, pltpu.roll(bottom, 1, axis=1))


def lane_column(column, cells, rows):
    kept = jnp.zeros((rows, LANES), jnp.float32)
    lane = iota((rows, LANES), 1)
    for i in range(cells):
        kept = jnp.where(lane == i, column(i), kept)
    return kept.T[:cells]


def pack_gx(plane, row, colour, gx, senda, sendb, dims):
    cells, rows, _, depth, _, _ = dims
    half = rows // 2
    even = gx % 2 == 0
    for send, high in ((senda, even), (sendb, jnp.logical_not(even))):
        parity = jnp.where(high, (colour + cells - 1) % 2, colour)
        send[0:half, :] = checker_pack(plane(high), parity)

    def lines(d):
        senda[pl.ds(half + d, 1), :] = row(d, even)
        sendb[pl.ds(half + d, 1), :] = row(d, jnp.logical_not(even))

    repeat(depth, lines)


def pack_rest(fluid, fin, grpa, grpb, gyx, place, dims):
    cells, rows, width, depth, fin_rows, fin_width = dims
    grp, _, gy = place
    even = grp % 2 == 0
    low, high = (
        lane_column(lambda i: fluid[i + 1, PAD : PAD + rows, k : k + 1], cells, rows)
        for k in (0, width - 1)
    )
    grpa[0:cells, 0:LANES] = jnp.where(even, high, low)
    grpb[0:cells, 0:LANES] = jnp.where(even, low, high)
    up = jnp.where(even, depth, 1)
    grpa[cells : cells + fin_rows, :] = fin[up, PAD : PAD + fin_rows, :]
    grpb[cells : cells + fin_rows, :] = fin[depth + 1 - up, PAD : PAD + fin_rows, :]
    edge = PAD + (1 - gy) * (rows - 1)
    for i in range(cells):
        gyx[i : i + 1, :] = fluid[i + 1, pl.ds(edge, 1), :]
    lane = iota((fin_rows, LANES), 1)

    def columns(at, side):
        kept = jnp.zeros((fin_rows, LANES), jnp.float32)
        for d in range(depth):
            column = fin[d + 1, PAD : PAD + fin_rows, at : at + 1]
            kept = jnp.where(lane == 2 * d + side, column, kept)
        gyx[cells : cells + fin_rows, 0:LANES] = kept

    @pl.when(gy == 0)
    def _():
        columns(fin_width - 1, 1)

    @pl.when(gy != 0)
    def _():
        columns(0, 0)


def my_place():
    return [lax.axis_index(name) for name in ("grp", "gx", "gy")]


def sides_of(at, count):
    return at % 2 == 0, jnp.where((at == 0) | (at == count - 1), 0.0, 1.0)


def grp_halos(paira, pairb, grp, groups):
    even, inside = sides_of(grp, groups)
    a, b = paira[...], pairb[...] * inside
    return jnp.where(even, b, a), jnp.where(even, a, b)


def unpack_fluid(fluid, zrows, zedge, paira, pairb, low_face, high_face, side, colour, place,
                 count, dims):
    cells, rows, width, _, _, _ = dims
    half = rows // 2
    _, gx, gy = place
    even, inside = sides_of(gx, count)
    high_plane = jnp.where(even, cells + 1, 0)
    for plane, ref, on in ((high_plane, paira, 1.0), (cells + 1 - high_plane, pairb, inside)):
        packed = ref[0:half, :] * on
        fluid[plane, PAD : PAD + half, :] = packed
        fluid[plane, PAD + half : PAD + rows, :] = pltpu.roll(packed, width - 1, axis=1)
    low_on = jnp.where(gy == 0, 0.0, 1.0)
    high_on = 1.0 - low_on
    for i in range(cells):
        line = side[i : i + 1, :]
        fluid[i + 1, PAD - 1 : PAD, :] = line * low_on
        fluid[i + 1, PAD + rows : PAD + rows + 1, :] = line * high_on
    odd_row = (iota((1, rows), 1) & 1) == 1
    for k in range(cells // 2):
        for lane, face, swap in ((2 * k, high_face, colour == 1), (2 * k + 1, low_face, colour == 0)):
            first, second = face[2 * k : 2 * k + 1, :], face[2 * k + 1 : 2 * k + 2, :]
            zrows[lane : lane + 1, :] = jnp.where(odd_row == swap, second, first)
    zrows[cells:, :] = jnp.zeros((LANES - cells, rows), jnp.float32)
    zedge[...] = zrows[...].T


def fluid_sweep(fluid, active, zedge, other, colour, dims, pairs, done=None):
    _, rows, width, _, _, _ = dims
    parity = (iota((ROWS, width), 0) + iota((ROWS, width), 1)) & 1
    updating = parity == colour
    off = parity ^ colour
    end_parity = iota((1, width), 1) & 1

    first_pair, step, count = pairs

    def pair(j, carry):
        k = first_pair + step * j
        a, b = 2 * k + 1, 2 * k + 2
        for at, swap in ((PAD - 1, 1 - colour), (PAD + rows, colour)):
            line = slice(at, at + 1)
            other[line, :] = jnp.where(end_parity == swap, fluid[b, line, :], fluid[a, line, :])
        for start in range(0, rows, ROWS):
            inner = slice(PAD + start, PAD + start + ROWS)
            other[inner, :] = jnp.where(updating, fluid[b, inner, :], fluid[a, inner, :])
        for start in range(0, rows, ROWS):
            inner = slice(PAD + start, PAD + start + ROWS)
            edge = pltpu.roll(zedge[start : start + ROWS, :], LANES - 1 - 2 * k, axis=1)
            shared = (
                other[PAD + start - 1 : PAD + start + ROWS - 1, :]
                + other[PAD + start + 1 : PAD + start + ROWS + 1, :]
                + lane_neighbours(other[inner, :], edge, edge)
            )
            here_a = fluid[a, inner, :]
            here_b = fluid[b, inner, :]
            total_a = shared + fluid[a - 1, inner, :] + here_b
            total_b = shared + fluid[b + 1, inner, :] + here_a
            new_a = (here_a + FLUID_DIFFUSION * total_a) * FLUID_SCALE
            new_b = (here_b + FLUID_DIFFUSION * total_b) * FLUID_SCALE
            mask_a = active[a - 1, start : start + ROWS, :] > off
            mask_b = active[b - 1, start : start + ROWS, :] > 1 - off
            fluid[a, inner, :] = jnp.where(mask_a, new_a, here_a)
            fluid[b, inner, :] = jnp.where(mask_b, new_b, here_b)
        if done is not None:
            done(k)
        return carry

    lax.fori_loop(0, count, pair, 0)


def fin_neighbours(fin, d, hedge, fin_rows):
    inner = slice(PAD, PAD + fin_rows)
    here = fin[d + 1, inner, :]
    edge = pltpu.roll(hedge, LANES - 1 - 2 * d, axis=1)
    total = (
        fin[d, inner, :]
        + fin[d + 2, inner, :]
        + fin[d + 1, PAD - 1 : PAD + fin_rows - 1, :]
        + fin[d + 1, PAD + 1 : PAD + fin_rows + 1, :]
        + lane_neighbours(here, edge, edge)
    )
    return here, total


def solution(mesh):
    in_specs = (
        P("gx", "gy", "grp"),
        P("gx", "gy", "grp"),
        P("grp", "gx", "gy"),
        P("grp", "gx", "gy"),
        P("gx", "gy", None, None),
        P("gx", "gy", None),
    )
    out_specs = (P("gx", "gy", "grp"), P("grp", "gx", "gy"))
    count = mesh.shape["gx"]
    groups = mesh.shape["grp"]
    sides = mesh.shape["gy"]
    assert sides == 2 and groups % 2 == 0 and count % 2 == 0
    ring = count == 4
    vmem = pl.BlockSpec(memory_space=pltpu.VMEM)
    hbm = pl.BlockSpec(memory_space=pl.ANY)

    def local(fluid_temp, active, fin_temp, fin_source, wall_owner, wall_target):
        cells, rows, width = fluid_temp.shape
        depth, fin_rows, fin_width = fin_temp.shape
        assert rows == LANES and width == fin_width == 2 * rows and fin_rows == 2 * cells
        assert 2 * depth <= LANES and depth % 8 == 0 and depth >= 24 and cells % 2 == 0 and cells >= 4 and rows % ROWS == 0 and fin_rows == ROWS
        dims = (cells, rows, width, depth, fin_rows, fin_width)
        half = rows // 2
        pairs = cells // 2
        face_rows = half + depth
        wall_rows = fin_rows + cells
        small_rows = cells + fin_rows
        gx_rows = face_rows + (wall_rows if ring else 0)
        owners = wall_owner.reshape(cells, rows)
        targets = wall_target.reshape(cells, rows)
        f32 = lambda *shape: jax.ShapeDtypeStruct(shape, jnp.float32)
        params = pltpu.CompilerParams(vmem_limit_bytes=32 * 1024 * 1024)
        fluid_pad = f32(cells + 2, rows + 2 * PAD, width)
        fin_pad = f32(depth + 2, fin_rows + 2 * PAD, fin_width)
        faces = (f32(small_rows, width), f32(small_rows, width), f32(small_rows, width))

        def start_gx_kernel(fluid_hbm, fin_hbm, own_hbm, tgt_hbm, gxa, gxb, wall,
                            planes, bottom, low_rows, high_rows, root, own, tgt, sems):
            def copy(k, source, target):
                return pltpu.make_async_copy(source, target, sems.at[k])

            last = cells - 1
            copies = [
                copy(0, own_hbm, own),
                copy(1, tgt_hbm, tgt),
                copy(2, fluid_hbm.at[:, :, pl.ds(0, LANES)], bottom),
                copy(3, fin_hbm.at[0], root),
                copy(4, fluid_hbm.at[0], planes.at[0]),
                copy(5, fluid_hbm.at[last], planes.at[1]),
                copy(6, fin_hbm.at[:, pl.ds(0, PAD), :], low_rows),
                copy(7, fin_hbm.at[:, pl.ds(fin_rows - PAD, PAD), :], high_rows),
            ]
            for item in copies:
                item.start()
            for item in copies:
                item.wait()
            shape = (cells, rows)
            shift = tgt[...] - 2 * (iota(shape, 0) * fin_width + iota(shape, 1))
            row_shift = (shift >= fin_width).astype(jnp.int32)
            code = own[...] * 4 + row_shift * 2 + (shift - row_shift * fin_width)
            wall[fin_rows:, LANES:] = code.astype(jnp.float32)
            wall[fin_rows:, 0:LANES] = lane_column(lambda i: bottom[i, :, 0:1], cells, rows)
            even_rows = dot(interleave_matrix(fin_rows), root[...], ((0,), (0,)))
            wall[0:fin_rows, :] = dot(even_rows, interleave_matrix(fin_width), ((1,), (0,)))
            gx = lax.axis_index("gx")
            pack_gx(
                lambda high: planes[jnp.where(high, 1, 0)],
                lambda d, high: jnp.where(high, high_rows[d, PAD - 1 : PAD, :], low_rows[d, 0:1, :]),
                1, gx, gxa, gxb, dims,
            )
            if ring:
                gxa[face_rows:, :] = wall[...]
                gxb[face_rows:, :] = wall[...]

        fluid_hbm, fin_hbm, owners, targets = (
            pltpu.with_memory_space_constraint(v, pltpu.HBM)
            for v in (fluid_temp, fin_temp, owners, targets)
        )
        in_hbm = pl.BlockSpec(memory_space=pltpu.HBM)
        buffer = lambda *shape: pltpu.VMEM(shape, jnp.float32)
        gxa, gxb, wall = pl.pallas_call(
            start_gx_kernel,
            out_shape=(f32(gx_rows, width), f32(gx_rows, width), f32(wall_rows, width)),
            in_specs=[in_hbm] * 4,
            out_specs=(vmem,) * 3,
            scratch_shapes=[buffer(2, rows, width), buffer(cells, rows, LANES),
                            buffer(depth, PAD, fin_width), buffer(depth, PAD, fin_width),
                            buffer(fin_rows, fin_width), pltpu.VMEM((cells, rows), jnp.int32),
                            pltpu.VMEM((cells, rows), jnp.int32), pltpu.SemaphoreType.DMA((8,))],
            compiler_params=params,
            name="start_gx",
        )(fluid_hbm, fin_hbm, owners, targets)

        def start_rest_kernel(fluid_in, fin_in, fluid, fin, grpa, grpb, gyx):
            def fluid_plane(i):
                fluid[i + 1, PAD : PAD + rows, :] = fluid_in[i]

            def fin_plane(d):
                fin[d + 1, PAD : PAD + fin_rows, :] = fin_in[d]

            repeat(cells, fluid_plane, 2)
            repeat(depth, fin_plane, 8)
            clear_rows(fin)
            pack_rest(fluid, fin, grpa, grpb, gyx, my_place(), dims)

        def clear_rows(fin):
            empty = jnp.zeros((depth, PAD, fin_width), jnp.float32)
            fin[1 : depth + 1, 0:PAD, :] = empty
            fin[1 : depth + 1, PAD + fin_rows :, :] = empty

        fluid0, fin0, grpa, grpb, gyx = pl.pallas_call(
            start_rest_kernel,
            out_shape=(fluid_pad, fin_pad) + faces,
            in_specs=[vmem, vmem],
            out_specs=(vmem,) * 5,
            compiler_params=params,
            name="start_rest",
        )(fluid_temp, fin_temp)

        def pairings(axis, size):
            cores = [(g, c) for g in range(size) for c in range(sides)]
            number = {core: k for k, core in enumerate(cores)}

            def partner(g, c):
                other = g - 1 if g % 2 == 0 else g + 1
                return (other, c) if 0 <= other < size else (g, 1 - c)

            first = [(number[g, c], number[g ^ 1, c]) for g, c in cores]
            second = [(number[g, c], number[partner(g, c)]) for g, c in cores]
            return (axis, "gy"), first, second

        def exchange(axis, size, paira, pairb):
            axes, first, second = pairings(axis, size)
            return lax.ppermute(paira, axes, first), lax.ppermute(pairb, axes, second)

        def swap(side):
            return lax.ppermute(side, "gy", [(0, 1), (1, 0)])

        def mixed_with(k):
            return [(i, i ^ k) for i in range(count)]

        if ring:
            walls = [wall, lax.ppermute(wall, "gx", mixed_with(2))]
            gxa = lax.ppermute(gxa, "gx", mixed_with(1))
            gxb = lax.ppermute(gxb, "gx", mixed_with(3))
        else:
            gxa, gxb = exchange("gx", count, gxa, gxb)
            walls = [wall, lax.all_gather(wall, "gx")]
        side = swap(gyx)
        grpa, grpb = exchange("grp", groups, grpa, grpb)

        def fin_depth_halos(fin, paira, pairb):
            below, above = grp_halos(paira, pairb, lax.axis_index("grp"), groups)
            fin[0, PAD : PAD + fin_rows, :] = below[cells:, :]
            fin[depth + 1, PAD : PAD + fin_rows, :] = above[cells:, :]

        def fin_first(fin, src, first, rest, hedge, block):
            for j in range(8):
                d = block * 8 + j
                here, total = fin_neighbours(fin, d, hedge, fin_rows)
                rhs = here + src[d]
                first[d + 1, PAD : PAD + fin_rows, :] = (rhs + FIN_CONDUCTION * total) * (1.0 / DIAG)
                rest[d] = rhs * (OMEGA / DIAG) + here * (1.0 - OMEGA)

        def fin_second(first, rest, hedge, block):
            for j in range(8):
                d = block * 8 + j
                _, total = fin_neighbours(first, d, hedge, fin_rows)
                rest[d] = rest[d] + (OMEGA * FIN_CONDUCTION / DIAG) * total

        blocks = depth // 8

        def inner_blocks(body):
            def step(k, carry):
                body(k)
                return carry

            lax.fori_loop(1, blocks - 1, step, 0)

        def middle_fin_kernel(fin, src, side, first, rest):
            hedge = side[cells : cells + fin_rows, 0:LANES]
            inner_blocks(lambda k: fin_first(fin, src, first, rest, hedge, k))
            clear_rows(first)

        first, rest = pl.pallas_call(
            middle_fin_kernel,
            out_shape=(fin_pad, f32(depth, fin_rows, fin_width)),
            in_specs=[vmem] * 3,
            out_specs=(vmem,) * 2,
            compiler_params=params,
            name="middle_fin",
        )(fin0, fin_source, side)

        def middle_gx_kernel(_0, _1, _2, _3, src, act, gxa_in, gxb_in, paira, pairb, side, own,
                             other_wall, fluid, fin, first, rest, ghost_out, zedge, gxa, gxb,
                             zrows, other):
            place = my_place()
            grp, gx, _ = place
            on_wall = grp == 0
            fin_depth_halos(fin, paira, pairb)
            hedge = side[cells : cells + fin_rows, 0:LANES]
            for block in (0, blocks - 1):
                fin_first(fin, src, first, rest, hedge, block)
            own_code = own[fin_rows:, LANES:]
            if ring:
                slots = [(gx, own), (gx ^ 1, gxa_in.at[pl.ds(face_rows, wall_rows), :]),
                         (gx ^ 3, gxb_in.at[pl.ds(face_rows, wall_rows), :]), (gx ^ 2, other_wall)]
            else:
                slots = [(s, other_wall.at[s]) for s in range(count)]
            quadrants = [(a * cells, b * LANES) for a in range(2) for b in range(2)]
            ghost = jnp.zeros((cells, rows), jnp.float32)
            deposits = [jnp.zeros((cells, rows), jnp.float32) for _ in quadrants]
            mine = (4 * gx).astype(jnp.float32)
            for owner, ref in slots:
                theirs = own_code - (4 * jnp.asarray(owner, jnp.int32)).astype(jnp.float32)
                temps = ref[fin_rows:, 0:LANES]
                wanted = ref[fin_rows:, LANES:] - mine
                for q, (r, c) in enumerate(quadrants):
                    ghost = jnp.where(theirs == q, ref[r : r + cells, c : c + LANES], ghost)
                    flux = HEAT_COEF * (temps - own[r : r + cells, c : c + LANES])
                    deposits[q] = deposits[q] + jnp.where(wanted == q, flux, 0.0)
            ghost_out[...] = ghost

            @pl.when(on_wall)
            def _():
                split = jnp.concatenate(
                    [jnp.concatenate(deposits[0:2], axis=1), jnp.concatenate(deposits[2:4], axis=1)],
                    axis=0,
                )
                mixed = dot(split, interleave_matrix(fin_width), ((1,), (1,)))
                landed = dot(interleave_matrix(fin_rows), mixed, ((1,), (0,)))
                first[1, PAD : PAD + fin_rows, :] += landed * (1.0 / DIAG)
                rest[0] += landed * (OMEGA / DIAG)

            even, inside = sides_of(gx, count)
            high_row = PAD + fin_rows - 1
            row_a = jnp.where(even, high_row, PAD)
            row_b = PAD + high_row - row_a
            scale = FIN_CONDUCTION / DIAG

            def add_row(d):
                first[d + 1, pl.ds(row_a, 1), :] += gxa_in[pl.ds(half + d, 1), :] * scale
                first[d + 1, pl.ds(row_b, 1), :] += gxb_in[pl.ds(half + d, 1), :] * (scale * inside)

            repeat(depth, add_row)
            below, above = grp_halos(paira, pairb, grp, groups)
            low_face = jnp.where(on_wall, ghost, below[0:cells, 0:LANES])
            unpack_fluid(fluid, zrows, zedge, gxa_in, gxb_in, low_face, above[0:cells, 0:LANES],
                         side, 0, place, count, dims)
            fluid_sweep(fluid, act, zedge, other, 0, dims, (0, pairs - 1, 2))
            pack_gx(
                lambda high: fluid[jnp.where(high, cells, 1), PAD : PAD + rows, :],
                lambda d, high: first[d + 1, pl.ds(jnp.where(high, high_row, PAD), 1), :],
                0, gx, gxa, gxb, dims,
            )

        zrows_buffer, zedge_buffer = buffer(LANES, rows), buffer(rows, LANES)
        other_buffer = buffer(rows + 2 * PAD, width)
        fluid1, _, first, rest, ghost, zedge, gxa, gxb = pl.pallas_call(
            middle_gx_kernel,
            out_shape=(fluid_pad, fin_pad, fin_pad, f32(depth, fin_rows, fin_width), f32(cells, rows),
                       f32(rows, LANES), f32(face_rows, width), f32(face_rows, width)),
            in_specs=[vmem] * 13,
            out_specs=(vmem,) * 8,
            scratch_shapes=[zrows_buffer, other_buffer],
            input_output_aliases={0: 0, 1: 1, 2: 2, 3: 3},
            compiler_params=params,
            name="middle_gx",
        )(fluid0, fin0, first, rest, fin_source, active, gxa, gxb, grpa, grpb, side, *walls)
        gxa, gxb = exchange("gx", count, gxa, gxb)

        def middle_rest_kernel(_, act, zedge, first, fluid, grpa, grpb, gyx, other):
            fluid_sweep(fluid, act, zedge, other, 0, dims, (1, 1, pairs - 2))
            pack_rest(fluid, first, grpa, grpb, gyx, my_place(), dims)

        fluid2, grpa, grpb, gyx = pl.pallas_call(
            middle_rest_kernel,
            out_shape=(fluid_pad,) + faces,
            in_specs=[vmem] * 4,
            out_specs=(vmem,) * 4,
            scratch_shapes=[other_buffer],
            input_output_aliases={0: 0},
            compiler_params=params,
            name="middle_rest",
        )(fluid1, active, zedge, first)
        side = swap(gyx)
        grpa, grpb = exchange("grp", groups, grpa, grpb)

        def end_fin_kernel(_, first, side, rest):
            hedge = side[cells : cells + fin_rows, 0:LANES]
            inner_blocks(lambda k: fin_second(first, rest, hedge, k))

        rest = pl.pallas_call(
            end_fin_kernel,
            out_shape=f32(depth, fin_rows, fin_width),
            in_specs=[vmem] * 3,
            out_specs=vmem,
            input_output_aliases={0: 0},
            compiler_params=params,
            name="end_fin",
        )(rest, first, side)

        def end_kernel(_0, _1, _2, act, ghost, gxa, gxb, paira, pairb, side,
                       fluid, first, rest, fluid_new, fin_new,
                       zrows, zedge, other, fluid_sems, fin_sems):
            place = my_place()
            on_wall = place[0] == 0

            def fluid_copy(k):
                return pltpu.make_async_copy(
                    fluid.at[pl.ds(2 * k + 1, 2), pl.ds(PAD, rows), :],
                    fluid_new.at[pl.ds(2 * k, 2)], fluid_sems.at[k],
                )

            def fin_copy(k, start, size):
                part = pl.ds(start, size)
                return pltpu.make_async_copy(rest.at[part], fin_new.at[part], fin_sems.at[k])

            fin_depth_halos(first, paira, pairb)
            hedge = side[cells : cells + fin_rows, 0:LANES]
            for block in (0, blocks - 1):
                fin_second(first, rest, hedge, block)
            even, inside = sides_of(place[1], count)
            row_a = jnp.where(even, fin_rows - 1, 0)
            row_b = fin_rows - 1 - row_a
            scale = OMEGA * FIN_CONDUCTION / DIAG

            def add_row(d):
                rest[d, pl.ds(row_a, 1), :] += gxa[pl.ds(half + d, 1), :] * scale
                rest[d, pl.ds(row_b, 1), :] += gxb[pl.ds(half + d, 1), :] * (scale * inside)

            repeat(depth, add_row)
            fin_copies = [fin_copy(0, 0, depth)]
            fin_copies[0].start()
            below, above = grp_halos(paira, pairb, place[0], groups)
            low_face = jnp.where(on_wall, ghost[...], below[0:cells, 0:LANES])
            unpack_fluid(fluid, zrows, zedge, gxa, gxb, low_face, above[0:cells, 0:LANES], side, 1,
                         place, count, dims)
            fluid_sweep(fluid, act, zedge, other, 1, dims, (0, 1, pairs),
                        lambda k: fluid_copy(k).start())

            def finish(k, carry):
                fluid_copy(k).wait()
                return carry

            for item in fin_copies:
                item.wait()
            lax.fori_loop(0, pairs, finish, 0)

        results = pl.pallas_call(
            end_kernel,
            out_shape=(fluid_pad, fin_pad, f32(depth, fin_rows, fin_width),
                       f32(cells, rows, width), f32(depth, fin_rows, fin_width)),
            in_specs=[vmem] * 10,
            out_specs=(vmem, vmem, vmem, hbm, hbm),
            scratch_shapes=[zrows_buffer, zedge_buffer, other_buffer,
                            pltpu.SemaphoreType.DMA((pairs,)), pltpu.SemaphoreType.DMA((1,))],
            input_output_aliases={0: 0, 1: 1, 2: 2},
            compiler_params=params,
            name="end",
        )(fluid2, first, rest, active, ghost, gxa, gxb, grpa, grpb, side)
        return results[3], results[4]

    return jax.shard_map(local, mesh=mesh, in_specs=in_specs, out_specs=out_specs, check_vma=False)
```

profile of v0, /device:TPU:0, one launch (start us, length us, event | category | flops | bytes accessed | tf_op | source)
XLA Modules:
  0.0 31.4 jit_solution(4090156359044466448)
XLA Ops:
  0.6 0.0 copy-start.1
  0.6 0.0 copy-start.2
  0.7 2.5 %start_gx.1 = (f32[176,256]{1,0:T(8,128)S(1)}, f32[176,256]{1,0:T(8,128)S(1)}, f32[48,256]{1,0:T(8,128)S(1)}) custom-call(f32[16,128,256]{2,1,0:T(8,128)} %fluid_hbm.1, f32[64,32,256]{2,1,0:T(8,128)} %fin_hbm.1, s32[16,128]{1,0:T(8,128)} %bitcast.2, s32[16,128]{1,0:T(8,128)} %bitcast.3), custom_call_target="tpu_custom_call" | custom-call | tf_op jit(solution)/shard_map/start_gx/pallas_call | solution.py:307
  3.2 3.0 %collective-permute-start.1 = (f32[176,256]{1,0:T(8,128)S(1)}, f32[176,256]{1,0:T(8,128)S(1)}, u32[]{:S(2)}, u32[]{:S(2)}) collective-permute-start(f32[176,256]{1,0:T(8,128)S(1)} %get-tuple-element.30), channel_id=1, source_target_pairs={{0,2},{2,0},{4,6},{6,4},{1,3},{3,1},{5,7},{7,5},{8,10},{10,8},{12,... | collective-permute-start | bytes 540680 | tf_op jit(solution)/shard_map/ppermute | solution.py:370
  6.2 0.0 copy-start.3
  6.2 1.5 %collective-permute-start.2 = (f32[176,256]{1,0:T(8,128)S(1)}, f32[176,256]{1,0:T(8,128)S(1)}, u32[]{:S(2)}, u32[]{:S(2)}) collective-permute-start(f32[176,256]{1,0:T(8,128)S(1)} %get-tuple-element.31), channel_id=1, source_target_pairs={{0,6},{2,4},{4,2},{6,0},{1,7},{3,5},{5,3},{7,1},{8,14},{10,12},{12... | collective-permute-start | bytes 540680 | tf_op jit(solution)/shard_map/ppermute | solution.py:371
  7.7 0.0 copy-done.1
  7.7 0.0 copy-done.2
  7.7 1.4 %start_rest.1 = (f32[18,144,256]{2,1,0:T(8,128)S(1)}, f32[66,48,256]{2,1,0:T(8,128)S(1)}, f32[48,256]{1,0:T(8,128)S(1)}, f32[48,256]{1,0:T(8,128)S(1)}, f32[48,256]{1,0:T(8,128)S(1)}) custom-call(f32[16,128,256]{2,1,0:T(8,128)S(1)} %copy-done.1, f32[64,32,256]{2,1,0:T(8,128)S(1)} %copy-done.2), custom_call_target="tpu_custom_call" | custom-call | tf_op jit(solution)/shard_map/start_rest/pallas_call | solution.py:337
  9.1 0.1 collective-permute-start
  9.2 0.1 collective-permute-start.5
  9.3 2.0 %collective-permute-start.3 = (f32[48,256]{1,0:T(8,128)S(1)}, f32[48,256]{1,0:T(8,128)S(1)}, u32[]{:S(2)}, u32[]{:S(2)}) collective-permute-start(f32[48,256]{1,0:T(8,128)S(1)} %get-tuple-element.32), channel_id=1, source_target_pairs={{0,8},{1,9},{8,0},{9,1},{16,24},{17,25},{24,16},{25,17},{2,10},{3,... | collective-permute-start | bytes 147464 | tf_op jit(solution)/shard_map/ppermute | solution.py:360
  11.3 0.0 collective-permute-done.side
  11.3 0.0 collective-permute-start.4
  11.3 0.0 copy-done.3
  11.3 0.0 copy-start
  11.3 1.6 %middle_fin.1 = (f32[66,48,256]{2,1,0:T(8,128)S(1)}, f32[64,32,256]{2,1,0:T(8,128)S(1)}) custom-call(f32[66,48,256]{2,1,0:T(8,128)S(1)} %get-tuple-element.26.fin._1, f32[64,32,256]{2,1,0:T(8,128)S(1)} %copy-done.3, f32[48,256]{1,0:T(8,128)S(1)} %collective-permute-done.side), custom_call_target="tpu_custom_call" | custom-call | tf_op jit(solution)/shard_map/middle_fin/pallas_call | solution.py:411
  13.0 3.5 %collective-permute-done.5.other_wall = f32[48,256]{1,0:T(8,128)S(1)} collective-permute-done((f32[48,256]{1,0:T(8,128)S(1)}, f32[48,256]{1,0:T(8,128)S(1)}, u32[]{:S(2)}, u32[]{:S(2)}) %collective-permute-start.5) | collective-permute-done | bytes 49184 | tf_op jit(solution)/shard_map/ppermute | solution.py:369
  16.5 0.0 collective-permute-done.3.paira
  16.5 0.0 collective-permute-done.4.pairb
  16.5 0.0 collective-permute-done.1.gxa_in
  16.5 0.0 collective-permute-done.2.gxb_in
  16.5 0.0 copy-done
  16.5 2.4 %middle_gx.1 = (f32[18,144,256]{2,1,0:T(8,128)S(1)}, f32[66,48,256]{2,1,0:T(8,128)S(1)}, f32[66,48,256]{2,1,0:T(8,128)S(1)}, f32[64,32,256]{2,1,0:T(8,128)S(1)},...) custom-call(f32[18,144,256]{2,1,0:T(8,128)S(1)} %get-tuple-element.2, ...), custom_call_target="tpu_custom_call", output_to_operand_aliasing={{0}: (0, {}), {1}: (1, {}), {2}: (2, {}), {3}: (3, {})} | custom-call | tf_op jit(solution)/shard_map/middle_gx/pallas_call | solution.py:485
  18.9 1.6 %collective-permute-start.7 = (f32[128,256]{1,0:T(8,128)S(1)}, f32[128,256]{1,0:T(8,128)S(1)}, u32[]{:S(2)}, u32[]{:S(2)}) collective-permute-start(f32[128,256]{1,0:T(8,128)S(1)} %get-tuple-element.42), channel_id=1, source_target_pairs={{0,2},{1,3},{2,0},{3,1},{4,6},{5,7},{6,4},{7,5},{8,10},{9,11},{10,... | collective-permute-start | bytes 393224 | tf_op jit(solution)/shard_map/ppermute | solution.py:360
  20.4 0.0 collective-permute-start.8
  20.4 2.5 %middle_rest.1 = (f32[18,144,256]{2,1,0:T(8,128)S(1)}, f32[48,256]{1,0:T(8,128)S(1)}, f32[48,256]{1,0:T(8,128)S(1)}, f32[48,256]{1,0:T(8,128)S(1)}) custom-call(f32[18,144,256]{2,1,0:T(8,128)S(1)} %get-tuple-element.35._, s32[16,128,256]{2,1,0:T(8,128)S(1)} %copy-done, f32[128,128]{1,0:T(8,128)S(1)} %get-tuple-element.36.zedge, ...), custom_call_target="tpu_custom_call", output_to_operand_aliasing={{0}: (0, {})} | custom-call | tf_op jit(solution)/shard_map/middle_rest/pallas_call | solution.py:502
  22.9 0.6 %collective-permute-start.6 = (f32[48,256]{1,0:T(8,128)S(1)}, f32[48,256]{1,0:T(8,128)S(1)}, u32[]{:S(2)}, u32[]{:S(2)}) collective-permute-start(f32[48,256]{1,0:T(8,128)S(1)} %get-tuple-element.40), channel_id=1, source_target_pairs={{0,1},{1,0},{2,3},{3,2},{4,5},{5,4},{6,7},{7,6},{8,9},{9,8},{10,11... | collective-permute-start | bytes 147464 | tf_op jit(solution)/shard_map/ppermute | solution.py:363
  23.5 1.1 %collective-permute-start.9 = (f32[48,256]{1,0:T(8,128)S(1)}, f32[48,256]{1,0:T(8,128)S(1)}, u32[]{:S(2)}, u32[]{:S(2)}) collective-permute-start(f32[48,256]{1,0:T(8,128)S(1)} %get-tuple-element.44), channel_id=1, source_target_pairs={{0,8},{1,9},{8,0},{9,1},{16,24},{17,25},{24,16},{25,17},{2,10},{3,... | collective-permute-start | bytes 147464 | tf_op jit(solution)/shard_map/ppermute | solution.py:360
  24.6 0.0 collective-permute-start.10
  24.6 0.0 collective-permute-done.6.side
  24.6 1.5 %end_fin.1._2 = f32[64,32,256]{2,1,0:T(8,128)S(1)} custom-call(f32[64,32,256]{2,1,0:T(8,128)S(1)} %get-tuple-element.39._, f32[66,48,256]{2,1,0:T(8,128)S(1)} %get-tuple-element.37.first._1, f32[48,256]{1,0:T(8,128)S(1)} %collective-permute-done.6.side), custom_call_target="tpu_custom_call", output_to_operand_aliasing={{}: (0, {})} | custom-call | tf_op jit(solution)/shard_map/end_fin/pallas_call | solution.py:519
  26.1 1.5 %collective-permute-done.9.paira = f32[48,256]{1,0:T(8,128)S(1)} collective-permute-done((f32[48,256]{1,0:T(8,128)S(1)}, f32[48,256]{1,0:T(8,128)S(1)}, u32[]{:S(2)}, u32[]{:S(2)}) %collective-permute-start.9) | collective-permute-done | bytes 49184 | tf_op jit(solution)/shard_map/ppermute | solution.py:360
  27.6 0.0 collective-permute-done.10.pairb
  27.6 0.0 collective-permute-done.7.gxa
  27.6 0.0 collective-permute-done.8.gxb
  27.6 3.8 %end.1 = (f32[18,144,256]{2,1,0:T(8,128)S(1)}, f32[66,48,256]{2,1,0:T(8,128)S(1)}, f32[64,32,256]{2,1,0:T(8,128)S(1)}, f32[16,128,256]{2,1,0:T(8,128)}, f32[64,32,256]{2,1,0:T(8,128)}) custom-call(f32[18,144,256]{2,1,0:T(8,128)S(1)} %get-tuple-element.38._0, ...), custom_call_target="tpu_custom_call", output_to_operand_aliasing={{0}: (0, {}), {1}: (1, {}), {2}: (2, {})} | custom-call | tf_op jit(solution)/shard_map/end/pallas_call | solution.py:576
Async XLA Ops:
  0.6 7.1 %copy-start.1 = (f32[16,128,256]{2,1,0:T(8,128)S(1)}, f32[16,128,256]{2,1,0:T(8,128)}, u32[]{:S(2)}) copy-start(f32[16,128,256]{2,1,0:T(8,128)} %fluid_hbm.1) | copy-start | bytes 6291460
  0.6 7.1 %copy-start.2 = (f32[64,32,256]{2,1,0:T(8,128)S(1)}, f32[64,32,256]{2,1,0:T(8,128)}, u32[]{:S(2)}) copy-start(f32[64,32,256]{2,1,0:T(8,128)} %fin_hbm.1) | copy-start | bytes 6291460
  3.2 13.3 %collective-permute-start.1 = (f32[176,256]{1,0:T(8,128)S(1)}, f32[176,256]{1,0:T(8,128)S(1)}, u32[]{:S(2)}, u32[]{:S(2)}) collective-permute-start(f32[176,256]{1,0:T(8,128)S(1)} %get-tuple-element.30), channel_id=1, source_target_pairs={{0,2},{2,0},{4,6},{6,4},{1,3},{3,1},{5,7},{7,5},{8,10},{10,8},{12,... | collective-permute-start | bytes 540680 | tf_op jit(solution)/shard_map/ppermute | solution.py:370
  6.2 5.1 %copy-start.3 = (f32[64,32,256]{2,1,0:T(8,128)S(1)}, f32[64,32,256]{2,1,0:T(8,128)}, u32[]{:S(2)}) copy-start(f32[64,32,256]{2,1,0:T(8,128)} %src.3) | copy-start | bytes 6291460
  6.2 10.3 %collective-permute-start.2 = (f32[176,256]{1,0:T(8,128)S(1)}, f32[176,256]{1,0:T(8,128)S(1)}, u32[]{:S(2)}, u32[]{:S(2)}) collective-permute-start(f32[176,256]{1,0:T(8,128)S(1)} %get-tuple-element.31), channel_id=1, source_target_pairs={{0,6},{2,4},{4,2},{6,0},{1,7},{3,5},{5,3},{7,1},{8,14},{10,12},{12... | collective-permute-start | bytes 540680 | tf_op jit(solution)/shard_map/ppermute | solution.py:371
  9.1 2.2 %collective-permute-start = (f32[48,256]{1,0:T(8,128)S(1)}, f32[48,256]{1,0:T(8,128)S(1)}, u32[]{:S(2)}, u32[]{:S(2)}) collective-permute-start(f32[48,256]{1,0:T(8,128)S(1)} %get-tuple-element.27), channel_id=1, source_target_pairs={{0,1},{1,0},{2,3},{3,2},{4,5},{5,4},{6,7},{7,6},{8,9},{9,8},{10,11... | collective-permute-start | bytes 147464 | tf_op jit(solution)/shard_map/ppermute | solution.py:363
  9.2 7.3 %collective-permute-start.5 = (f32[48,256]{1,0:T(8,128)S(1)}, f32[48,256]{1,0:T(8,128)S(1)}, u32[]{:S(2)}, u32[]{:S(2)}) collective-permute-start(f32[48,256]{1,0:T(8,128)S(1)} %get-tuple-element.34.own), channel_id=1, source_target_pairs={{0,4},{2,6},{4,0},{6,2},{1,5},{3,7},{5,1},{7,3},{8,12},{10,14},{12... | collective-permute-start | bytes 147464 | tf_op jit(solution)/shard_map/ppermute | solution.py:369
  9.3 7.2 %collective-permute-start.3 = (f32[48,256]{1,0:T(8,128)S(1)}, f32[48,256]{1,0:T(8,128)S(1)}, u32[]{:S(2)}, u32[]{:S(2)}) collective-permute-start(f32[48,256]{1,0:T(8,128)S(1)} %get-tuple-element.32), channel_id=1, source_target_pairs={{0,8},{1,9},{8,0},{9,1},{16,24},{17,25},{24,16},{25,17},{2,10},{3,... | collective-permute-start | bytes 147464 | tf_op jit(solution)/shard_map/ppermute | solution.py:360
  11.3 5.2 %collective-permute-start.4 = (f32[48,256]{1,0:T(8,128)S(1)}, f32[48,256]{1,0:T(8,128)S(1)}, u32[]{:S(2)}, u32[]{:S(2)}) collective-permute-start(f32[48,256]{1,0:T(8,128)S(1)} %get-tuple-element.33), channel_id=1, source_target_pairs={{0,1},{1,0},{8,16},{9,17},{16,8},{17,9},{24,25},{25,24},{2,3},{3,2... | collective-permute-start | bytes 147464 | tf_op jit(solution)/shard_map/ppermute | solution.py:360
  11.3 5.2 %copy-start = (s32[16,128,256]{2,1,0:T(8,128)S(1)}, s32[16,128,256]{2,1,0:T(8,128)}, u32[]{:S(2)}) copy-start(s32[16,128,256]{2,1,0:T(8,128)} %act.5) | copy-start | bytes 6291460
  18.9 8.7 %collective-permute-start.7 = (f32[128,256]{1,0:T(8,128)S(1)}, f32[128,256]{1,0:T(8,128)S(1)}, u32[]{:S(2)}, u32[]{:S(2)}) collective-permute-start(f32[128,256]{1,0:T(8,128)S(1)} %get-tuple-element.42), channel_id=1, source_target_pairs={{0,2},{1,3},{2,0},{3,1},{4,6},{5,7},{6,4},{7,5},{8,10},{9,11},{10,... | collective-permute-start | bytes 393224 | tf_op jit(solution)/shard_map/ppermute | solution.py:360
  20.4 7.2 %collective-permute-start.8 = (f32[128,256]{1,0:T(8,128)S(1)}, f32[128,256]{1,0:T(8,128)S(1)}, u32[]{:S(2)}, u32[]{:S(2)}) collective-permute-start(f32[128,256]{1,0:T(8,128)S(1)} %get-tuple-element.43), channel_id=1, source_target_pairs={{0,1},{1,0},{2,4},{3,5},{4,2},{5,3},{6,7},{7,6},{8,9},{9,8},{10,12... | collective-permute-start | bytes 393224 | tf_op jit(solution)/shard_map/ppermute | solution.py:360
  22.9 1.7 %collective-permute-start.6 = (f32[48,256]{1,0:T(8,128)S(1)}, f32[48,256]{1,0:T(8,128)S(1)}, u32[]{:S(2)}, u32[]{:S(2)}) collective-permute-start(f32[48,256]{1,0:T(8,128)S(1)} %get-tuple-element.40), channel_id=1, source_target_pairs={{0,1},{1,0},{2,3},{3,2},{4,5},{5,4},{6,7},{7,6},{8,9},{9,8},{10,11... | collective-permute-start | bytes 147464 | tf_op jit(solution)/shard_map/ppermute | solution.py:363
  23.5 4.1 %collective-permute-start.9 = (f32[48,256]{1,0:T(8,128)S(1)}, f32[48,256]{1,0:T(8,128)S(1)}, u32[]{:S(2)}, u32[]{:S(2)}) collective-permute-start(f32[48,256]{1,0:T(8,128)S(1)} %get-tuple-element.44), channel_id=1, source_target_pairs={{0,8},{1,9},{8,0},{9,1},{16,24},{17,25},{24,16},{25,17},{2,10},{3,... | collective-permute-start | bytes 147464 | tf_op jit(solution)/shard_map/ppermute | solution.py:360
  24.6 3.0 %collective-permute-start.10 = (f32[48,256]{1,0:T(8,128)S(1)}, f32[48,256]{1,0:T(8,128)S(1)}, u32[]{:S(2)}, u32[]{:S(2)}) collective-permute-start(f32[48,256]{1,0:T(8,128)S(1)} %get-tuple-element.45), channel_id=1, source_target_pairs={{0,1},{1,0},{8,16},{9,17},{16,8},{17,9},{24,25},{25,24},{2,3},{3,2... | collective-permute-start | bytes 147464 | tf_op jit(solution)/shard_map/ppermute | solution.py:360
where the time goes:
time: 31.5 us; the launch traced here: 31.4 us
  Pallas kernels  15.7 us (50%)
  starting transfers between devices  9.95 us (32%)
  waiting for transfers between devices  5.01 us (16%)
  between operations  0.75 us (2%)
    ppermute x6, starting transfers between devices, exchange(): return (lax.ppermute(paira, axes, first), lax.ppermute(pairb, axes, second))  4.66 us
    pallas_call x1, Pallas kernels, local(): pl.pallas_call(end_kernel, out_shape=(fluid_pad, fin_pad, f32(depth, fin_...  3.77 us
    ppermute x1, waiting for transfers between devices, local(): walls = [wall, lax.ppermute(wall, 'gx', mixed_with(2))]  3.49 us
    ppermute x1, starting transfers between devices, local(): gxa = lax.ppermute(gxa, 'gx', mixed_with(1))  3.03 us
    pallas_call x1, Pallas kernels, local(): pl.pallas_call(start_gx_kernel, out_shape=(f32(gx_rows, width), f32(gx_ro...  2.54 us
    pallas_call x1, Pallas kernels, local(): pl.pallas_call(middle_rest_kernel, out_shape=(fluid_pad,) + faces, in_spe...  2.5 us
    pallas_call x1, Pallas kernels, local(): pl.pallas_call(middle_gx_kernel, out_shape=(fluid_pad, fin_pad, fin_pad,...  2.35 us
    pallas_call x1, Pallas kernels, local(): pl.pallas_call(middle_fin_kernel, out_shape=(fin_pad, f32(depth, fin_rows...  1.63 us
  transfers between devices with their start and end apart: 11, of which 2 were waited for; matrix products, arithmetic and copies ran while one was open for 0% of the time, Pallas kernels for 22%

commit v1 on v0

--- a/solution.py
+++ b/solution.py
@@ -91,16 +91,25 @@
     repeat(depth, lines)
 
 
-def pack_rest(fluid, fin, grpa, grpb, gyx, place, dims):
+def pack_rest(fluid, fin, colour, grpa, grpb, gyx, place, dims):
     cells, rows, width, depth, fin_rows, fin_width = dims
     grp, _, gy = place
     even = grp % 2 == 0
-    low, high = (
-        lane_column(lambda i: fluid[i + 1, PAD : PAD + rows, k : k + 1], cells, rows)
-        for k in (0, width - 1)
-    )
-    grpa[0:cells, 0:LANES] = jnp.where(even, high, low)
-    grpb[0:cells, 0:LANES] = jnp.where(even, low, high)
+    odd_row = (iota((rows, 1), 0) & 1) == 1
+    inner = slice(PAD, PAD + rows)
+
+    def face(lane, swap):
+        column = slice(lane, lane + 1)
+        return lane_column(
+            lambda k: jnp.where(
+                odd_row == swap, fluid[2 * k + 2, inner, column], fluid[2 * k + 1, inner, column]
+            ),
+            cells // 2, rows,
+        )
+
+    low, high = face(0, colour == 1), face(width - 1, colour == 0)
+    grpa[0 : cells // 2, 0:LANES] = jnp.where(even, high, low)
+    grpb[0 : cells // 2, 0:LANES] = jnp.where(even, low, high)
     up = jnp.where(even, depth, 1)
     grpa[cells : cells + fin_rows, :] = fin[up, PAD : PAD + fin_rows, :]
     grpb[cells : cells + fin_rows, :] = fin[depth + 1 - up, PAD : PAD + fin_rows, :]
@@ -139,28 +148,33 @@
     return jnp.where(even, b, a), jnp.where(even, a, b)
 
 
-def unpack_fluid(fluid, zrows, zedge, paira, pairb, low_face, high_face, side, colour, place,
-                 count, dims):
+def unpack_lines(fluid, side, gy, dims):
+    cells, rows, _, _, _, _ = dims
+    low_on = jnp.where(gy == 0, 0.0, 1.0)
+    high_on = 1.0 - low_on
+    for i in range(cells):
+        line = side[i : i + 1, :]
+        fluid[i + 1, PAD - 1 : PAD, :] = line * low_on
+        fluid[i + 1, PAD + rows : PAD + rows + 1, :] = line * high_on
+
+
+def unpack_fluid(fluid, zrows, zedge, paira, pairb, ghost, below, above, colour, place, count,
+                 dims):
     cells, rows, width, _, _, _ = dims
     half = rows // 2
-    _, gx, gy = place
+    grp, gx, _ = place
     even, inside = sides_of(gx, count)
     high_plane = jnp.where(even, cells + 1, 0)
     for plane, ref, on in ((high_plane, paira, 1.0), (cells + 1 - high_plane, pairb, inside)):
         packed = ref[0:half, :] * on
         fluid[plane, PAD : PAD + half, :] = packed
         fluid[plane, PAD + half : PAD + rows, :] = pltpu.roll(packed, width - 1, axis=1)
-    low_on = jnp.where(gy == 0, 0.0, 1.0)
-    high_on = 1.0 - low_on
-    for i in range(cells):
-        line = side[i : i + 1, :]
-        fluid[i + 1, PAD - 1 : PAD, :] = line * low_on
-        fluid[i + 1, PAD + rows : PAD + rows + 1, :] = line * high_on
     odd_row = (iota((1, rows), 1) & 1) == 1
     for k in range(cells // 2):
-        for lane, face, swap in ((2 * k, high_face, colour == 1), (2 * k + 1, low_face, colour == 0)):
-            first, second = face[2 * k : 2 * k + 1, :], face[2 * k + 1 : 2 * k + 2, :]
-            zrows[lane : lane + 1, :] = jnp.where(odd_row == swap, second, first)
+        first, second = ghost[2 * k : 2 * k + 1, :], ghost[2 * k + 1 : 2 * k + 2, :]
+        merged = jnp.where(odd_row == (colour == 0), second, first)
+        zrows[2 * k : 2 * k + 1, :] = above[k : k + 1, 0:rows]
+        zrows[2 * k + 1 : 2 * k + 2, :] = jnp.where(grp == 0, merged, below[k : k + 1, 0:rows])
     zrows[cells:, :] = jnp.zeros((LANES - cells, rows), jnp.float32)
     zedge[...] = zrows[...].T
 
@@ -250,8 +264,8 @@
         pairs = cells // 2
         face_rows = half + depth
         wall_rows = fin_rows + cells
+        gx_rows = face_rows + (wall_rows if ring else 0)
         small_rows = cells + fin_rows
-        gx_rows = face_rows + (wall_rows if ring else 0)
         owners = wall_owner.reshape(cells, rows)
         targets = wall_target.reshape(cells, rows)
         f32 = lambda *shape: jax.ShapeDtypeStruct(shape, jnp.float32)
@@ -327,7 +341,7 @@
             repeat(cells, fluid_plane, 2)
             repeat(depth, fin_plane, 8)
             clear_rows(fin)
-            pack_rest(fluid, fin, grpa, grpb, gyx, my_place(), dims)
+            pack_rest(fluid, fin, 0, grpa, grpb, gyx, my_place(), dims)
 
         def clear_rows(fin):
             empty = jnp.zeros((depth, PAD, fin_width), jnp.float32)
@@ -357,7 +371,9 @@
 
         def exchange(axis, size, paira, pairb):
             axes, first, second = pairings(axis, size)
-            return lax.ppermute(paira, axes, first), lax.ppermute(pairb, axes, second)
+            paira = lax.ppermute(paira, axes, first)
+            pairb = lax.ppermute(pairb, axes, second)
+            return paira, pairb
 
         def swap(side):
             return lax.ppermute(side, "gy", [(0, 1), (1, 0)])
@@ -403,7 +419,7 @@
 
             lax.fori_loop(1, blocks - 1, step, 0)
 
-        def middle_fin_kernel(fin, src, side, first, rest):
+        def middle_fin_kernel(fin, src, side, _, first, rest):
             hedge = side[cells : cells + fin_rows, 0:LANES]
             inner_blocks(lambda k: fin_first(fin, src, first, rest, hedge, k))
             clear_rows(first)
@@ -411,28 +427,43 @@
         first, rest = pl.pallas_call(
             middle_fin_kernel,
             out_shape=(fin_pad, f32(depth, fin_rows, fin_width)),
-            in_specs=[vmem] * 3,
+            in_specs=[vmem] * 4,
             out_specs=(vmem,) * 2,
             compiler_params=params,
             name="middle_fin",
-        )(fin0, fin_source, side)
-
-        def middle_gx_kernel(_0, _1, _2, _3, src, act, gxa_in, gxb_in, paira, pairb, side, own,
-                             other_wall, fluid, fin, first, rest, ghost_out, zedge, gxa, gxb,
-                             zrows, other):
-            place = my_place()
-            grp, gx, _ = place
-            on_wall = grp == 0
+        )(fin0, fin_source, side, active)
+
+        def middle_grp_kernel(_0, _1, _2, _3, src, paira, pairb, side, fluid, fin, first, rest):
             fin_depth_halos(fin, paira, pairb)
             hedge = side[cells : cells + fin_rows, 0:LANES]
             for block in (0, blocks - 1):
                 fin_first(fin, src, first, rest, hedge, block)
+            unpack_lines(fluid, side, lax.axis_index("gy"), dims)
+
+        fin_rest = f32(depth, fin_rows, fin_width)
+        fluid0, _, first, rest = pl.pallas_call(
+            middle_grp_kernel,
+            out_shape=(fluid_pad, fin_pad, fin_pad, fin_rest),
+            in_specs=[vmem] * 8,
+            out_specs=(vmem,) * 4,
+            input_output_aliases={0: 0, 1: 1, 2: 2, 3: 3},
+            compiler_params=params,
+            name="middle_grp",
+        )(fluid0, fin0, first, rest, fin_source, grpa, grpb, side)
+
+        def middle_gx_kernel(*refs):
+            (act, gxa_in, gxb_in, paira, pairb, own), refs = refs[3:9], refs[9:]
+            wall_refs, refs = refs[: len(walls) - 1], refs[len(walls) - 1 :]
+            fluid, first, rest, ghost_out, zedge, gxa, gxb, zrows, other = refs
+            place = my_place()
+            grp, gx, _ = place
+            on_wall = grp == 0
             own_code = own[fin_rows:, LANES:]
             if ring:
                 slots = [(gx, own), (gx ^ 1, gxa_in.at[pl.ds(face_rows, wall_rows), :]),
-                         (gx ^ 3, gxb_in.at[pl.ds(face_rows, wall_rows), :]), (gx ^ 2, other_wall)]
+                         (gx ^ 3, gxb_in.at[pl.ds(face_rows, wall_rows), :]), (gx ^ 2, wall_refs[0])]
             else:
-                slots = [(s, other_wall.at[s]) for s in range(count)]
+                slots = [(s, wall_refs[0].at[s]) for s in range(count)]
             quadrants = [(a * cells, b * LANES) for a in range(2) for b in range(2)]
             ghost = jnp.zeros((cells, rows), jnp.float32)
             deposits = [jnp.zeros((cells, rows), jnp.float32) for _ in quadrants]
@@ -470,9 +501,8 @@
 
             repeat(depth, add_row)
             below, above = grp_halos(paira, pairb, grp, groups)
-            low_face = jnp.where(on_wall, ghost, below[0:cells, 0:LANES])
-            unpack_fluid(fluid, zrows, zedge, gxa_in, gxb_in, low_face, above[0:cells, 0:LANES],
-                         side, 0, place, count, dims)
+            unpack_fluid(fluid, zrows, zedge, gxa_in, gxb_in, ghost, below, above, 0, place, count,
+                         dims)
             fluid_sweep(fluid, act, zedge, other, 0, dims, (0, pairs - 1, 2))
             pack_gx(
                 lambda high: fluid[jnp.where(high, cells, 1), PAD : PAD + rows, :],
@@ -482,22 +512,22 @@
 
         zrows_buffer, zedge_buffer = buffer(LANES, rows), buffer(rows, LANES)
         other_buffer = buffer(rows + 2 * PAD, width)
-        fluid1, _, first, rest, ghost, zedge, gxa, gxb = pl.pallas_call(
+        fluid1, first, rest, ghost, zedge, gxa, gxb = pl.pallas_call(
             middle_gx_kernel,
-            out_shape=(fluid_pad, fin_pad, fin_pad, f32(depth, fin_rows, fin_width), f32(cells, rows),
+            out_shape=(fluid_pad, fin_pad, fin_rest, f32(cells, rows),
                        f32(rows, LANES), f32(face_rows, width), f32(face_rows, width)),
-            in_specs=[vmem] * 13,
-            out_specs=(vmem,) * 8,
+            in_specs=[vmem] * (8 + len(walls)),
+            out_specs=(vmem,) * 7,
             scratch_shapes=[zrows_buffer, other_buffer],
-            input_output_aliases={0: 0, 1: 1, 2: 2, 3: 3},
+            input_output_aliases={0: 0, 1: 1, 2: 2},
             compiler_params=params,
             name="middle_gx",
-        )(fluid0, fin0, first, rest, fin_source, active, gxa, gxb, grpa, grpb, side, *walls)
+        )(fluid0, first, rest, active, gxa, gxb, grpa, grpb, *walls)
         gxa, gxb = exchange("gx", count, gxa, gxb)
 
         def middle_rest_kernel(_, act, zedge, first, fluid, grpa, grpb, gyx, other):
             fluid_sweep(fluid, act, zedge, other, 0, dims, (1, 1, pairs - 2))
-            pack_rest(fluid, first, grpa, grpb, gyx, my_place(), dims)
+            pack_rest(fluid, first, 1, grpa, grpb, gyx, my_place(), dims)
 
         fluid2, grpa, grpb, gyx = pl.pallas_call(
             middle_rest_kernel,
@@ -512,25 +542,25 @@
         side = swap(gyx)
         grpa, grpb = exchange("grp", groups, grpa, grpb)
 
-        def end_fin_kernel(_, first, side, rest):
+        def end_fin_kernel(_0, _1, first, side, rest, fluid):
+            unpack_lines(fluid, side, lax.axis_index("gy"), dims)
             hedge = side[cells : cells + fin_rows, 0:LANES]
             inner_blocks(lambda k: fin_second(first, rest, hedge, k))
 
-        rest = pl.pallas_call(
+        rest, fluid3 = pl.pallas_call(
             end_fin_kernel,
-            out_shape=f32(depth, fin_rows, fin_width),
-            in_specs=[vmem] * 3,
-            out_specs=vmem,
-            input_output_aliases={0: 0},
+            out_shape=(fin_rest, fluid_pad),
+            in_specs=[vmem] * 4,
+            out_specs=(vmem,) * 2,
+            input_output_aliases={0: 0, 1: 1},
             compiler_params=params,
             name="end_fin",
-        )(rest, first, side)
+        )(rest, fluid2, first, side)
 
         def end_kernel(_0, _1, _2, act, ghost, gxa, gxb, paira, pairb, side,
                        fluid, first, rest, fluid_new, fin_new,
                        zrows, zedge, other, fluid_sems, fin_sems):
             place = my_place()
-            on_wall = place[0] == 0
 
             def fluid_copy(k):
                 return pltpu.make_async_copy(
@@ -559,9 +589,7 @@
             fin_copies = [fin_copy(0, 0, depth)]
             fin_copies[0].start()
             below, above = grp_halos(paira, pairb, place[0], groups)
-            low_face = jnp.where(on_wall, ghost[...], below[0:cells, 0:LANES])
-            unpack_fluid(fluid, zrows, zedge, gxa, gxb, low_face, above[0:cells, 0:LANES], side, 1,
-                         place, count, dims)
+            unpack_fluid(fluid, zrows, zedge, gxa, gxb, ghost, below, above, 1, place, count, dims)
             fluid_sweep(fluid, act, zedge, other, 1, dims, (0, 1, pairs),
                         lambda k: fluid_copy(k).start())
 
@@ -584,7 +612,7 @@
             input_output_aliases={0: 0, 1: 1, 2: 2},
             compiler_params=params,
             name="end",
-        )(fluid2, first, rest, active, ghost, gxa, gxb, grpa, grpb, side)
+        )(fluid3, first, rest, active, ghost, gxa, gxb, grpa, grpb, side)
         return results[3], results[4]
 
     return jax.shard_map(local, mesh=mesh, in_specs=in_specs, out_specs=out_specs, check_vma=False)

time: 31.5 us -> 31.7 us (level)
  starting transfers between devices: 9.95 us -> 11.7 us
  Pallas kernels: 15.7 us -> 14.9 us
  waiting for transfers between devices: 5.01 us -> 4.28 us
    ppermute x6, starting transfers between devices: 4.66 us -> 6 us  [the longest x3 5.77 us: exchange(): paira = lax.ppermute(paira, axes, first)]
    ppermute x6, waiting for transfers between devices: 1.51 us -> 0.86 us  [the longest x3 0.85 us: exchange(): paira = lax.ppermute(paira, axes, first)]
    ppermute x1, starting transfers between devices: 0.13 us -> 0.51 us  [local(): walls = [wall, lax.ppermute(wall, 'gx', mixed_with(2))]]
    pallas_call x1, Pallas kernels: 2.5 us -> 2.15 us  [local(): pl.pallas_call(middle_rest_kernel, out_shape=(fluid_pad,) + faces, in_spe...]
    pallas_call x2 -> x3, Pallas kernels: 3.86 us -> 3.85 us  [the longest x1 1.95 us: local(): pl.pallas_call(middle_gx_kernel, out_shape=(fluid_pad, fin_pad, fin_rest,...]
  transfers between devices with their start and end apart: 11 -> 11, of which waited for: 2 -> 3; matrix products, arithmetic and copies ran while one was open for 0% -> 0% of each run, Pallas kernels for 22% -> 21%
where the time goes in v1:
time: 31.7 us; the launch traced here: 31.6 us
  Pallas kernels  14.9 us (47%)
  starting transfers between devices  11.7 us (37%)
  waiting for transfers between devices  4.28 us (14%)
  between operations  0.75 us (2%)
    ppermute x3, starting transfers between devices, exchange(): paira = lax.ppermute(paira, axes, first)  5.77 us
    pallas_call x1, Pallas kernels, local(): pl.pallas_call(end_kernel, out_shape=(fluid_pad, fin_pad, f32(depth, fin_...  3.69 us
    ppermute x1, waiting for transfers between devices, local(): walls = [wall, lax.ppermute(wall, 'gx', mixed_with(2))]  3.41 us
    ppermute x1, starting transfers between devices, local(): gxa = lax.ppermute(gxa, 'gx', mixed_with(1))  3.03 us
    pallas_call x1, Pallas kernels, local(): pl.pallas_call(start_gx_kernel, out_shape=(f32(gx_rows, width), f32(gx_ro...  2.54 us
    pallas_call x1, Pallas kernels, local(): pl.pallas_call(middle_rest_kernel, out_shape=(fluid_pad,) + faces, in_spe...  2.15 us
    pallas_call x1, Pallas kernels, local(): pl.pallas_call(middle_gx_kernel, out_shape=(fluid_pad, fin_pad, fin_rest,...  1.95 us
    pallas_call x1, Pallas kernels, local(): pl.pallas_call(middle_fin_kernel, out_shape=(fin_pad, f32(depth, fin_rows...  1.56 us
  transfers between devices with their start and end apart: 11, of which 3 were waited for; matrix products, arithmetic and copies ran while one was open for 0% of the time, Pallas kernels for 21%

profile of v1, /device:TPU:0, one launch (start us, length us, event | category | flops | bytes accessed | tf_op | source)
XLA Modules:
  0.0 31.6 jit_solution(11579611904296777218)
XLA Ops:
  0.6 0.0 copy-start.2
  0.6 0.0 copy-start.3
  0.7 2.5 %start_gx.1 = (f32[176,256]{1,0:T(8,128)S(1)}, f32[176,256]{1,0:T(8,128)S(1)}, f32[48,256]{1,0:T(8,128)S(1)}) custom-call(f32[16,128,256]{2,1,0:T(8,128)} %fluid_hbm.1, f32[64,32,256]{2,1,0:T(8,128)} %fin_hbm.1, s32[16,128]{1,0:T(8,128)} %bitcast.2, s32[16,128]{1,0:T(8,128)} %bitcast.3), custom_call_target="tpu_custom_call" | custom-call | tf_op jit(solution)/shard_map/start_gx/pallas_call | solution.py:321
  3.2 0.0 copy-start
  3.2 0.0 copy-start.1
  3.2 3.0 %collective-permute-start.3 = (f32[176,256]{1,0:T(8,128)S(1)}, f32[176,256]{1,0:T(8,128)S(1)}, u32[]{:S(2)}, u32[]{:S(2)}) collective-permute-start(f32[176,256]{1,0:T(8,128)S(1)} %get-tuple-element.40), channel_id=1, source_target_pairs={{0,2},{2,0},{4,6},{6,4},{1,3},{3,1},{5,7},{7,5},{8,10},{10,8},{12,... | collective-permute-start | bytes 540680 | tf_op jit(solution)/shard_map/ppermute | solution.py:386
  6.3 1.5 %collective-permute-start.4 = (f32[176,256]{1,0:T(8,128)S(1)}, f32[176,256]{1,0:T(8,128)S(1)}, u32[]{:S(2)}, u32[]{:S(2)}) collective-permute-start(f32[176,256]{1,0:T(8,128)S(1)} %get-tuple-element.41), channel_id=1, source_target_pairs={{0,6},{2,4},{4,2},{6,0},{1,7},{3,5},{5,3},{7,1},{8,14},{10,12},{12... | collective-permute-start | bytes 540680 | tf_op jit(solution)/shard_map/ppermute | solution.py:387
  7.7 0.0 copy-done.2
  7.8 0.0 copy-done.3
  7.8 1.1 %start_rest.1 = (f32[18,144,256]{2,1,0:T(8,128)S(1)}, f32[66,48,256]{2,1,0:T(8,128)S(1)}, f32[48,256]{1,0:T(8,128)S(1)}, f32[48,256]{1,0:T(8,128)S(1)}, f32[48,256]{1,0:T(8,128)S(1)}) custom-call(f32[16,128,256]{2,1,0:T(8,128)S(1)} %copy-done.2, f32[64,32,256]{2,1,0:T(8,128)S(1)} %copy-done.3), custom_call_target="tpu_custom_call" | custom-call | tf_op jit(solution)/shard_map/start_rest/pallas_call | solution.py:351
  8.9 0.1 collective-permute-start
  8.9 1.6 %collective-permute-start.1 = (f32[48,256]{1,0:T(8,128)S(1)}, f32[48,256]{1,0:T(8,128)S(1)}, u32[]{:S(2)}, u32[]{:S(2)}) collective-permute-start(f32[48,256]{1,0:T(8,128)S(1)} %get-tuple-element.35), channel_id=1, source_target_pairs={{0,8},{1,9},{8,0},{9,1},{16,24},{17,25},{24,16},{25,17},{2,10},{3,... | collective-permute-start | bytes 147464 | tf_op jit(solution)/shard_map/ppermute | solution.py:374
  10.6 0.2 collective-permute-start.2
  10.7 0.0 collective-permute-done.side
  10.7 0.5 %collective-permute-start.5 = (f32[48,256]{1,0:T(8,128)S(1)}, f32[48,256]{1,0:T(8,128)S(1)}, u32[]{:S(2)}, u32[]{:S(2)}) collective-permute-start(f32[48,256]{1,0:T(8,128)S(1)} %get-tuple-element.42.refs_8_), channel_id=1, source_target_pairs={{0,4},{2,6},{4,0},{6,2},{1,5},{3,7},{5,1},{7,3},{8,12},{10,14},{12... | collective-permute-start | bytes 147464 | tf_op jit(solution)/shard_map/ppermute | solution.py:385
  11.2 0.0 copy-done
  11.2 0.0 copy-done.1
  11.2 1.6 %middle_fin.1 = (f32[66,48,256]{2,1,0:T(8,128)S(1)}, f32[64,32,256]{2,1,0:T(8,128)S(1)}) custom-call(f32[66,48,256]{2,1,0:T(8,128)S(1)} %get-tuple-element.31.fin._1, f32[64,32,256]{2,1,0:T(8,128)S(1)} %copy-done.1, f32[48,256]{1,0:T(8,128)S(1)} %collective-permute-done.side, s32[16,128,256]{2,1,0:T(8,128)S(1)} %copy-done), custom_call_target="tpu_custom_call" | custom-call | tf_op jit(solution)/shard_map/middle_fin/pallas_call | solution.py:427
  12.8 0.3 collective-permute-done.1.paira.refs_6_
  13.1 0.0 collective-permute-done.2.pairb.refs_7_
  13.1 0.4 %middle_grp.1 = (f32[18,144,256]{2,1,0:T(8,128)S(1)}, f32[66,48,256]{2,1,0:T(8,128)S(1)}, f32[66,48,256]{2,1,0:T(8,128)S(1)}, f32[64,32,256]{2,1,0:T(8,128)S(1)}) custom-call(f32[18,144,256]{2,1,0:T(8,128)S(1)} %get-tuple-element.30._0, ...), custom_call_target="tpu_custom_call", output_to_operand_aliasing={{0}: (0, {}), {1}: (1, {}), {2}: (2, {}), {3}: (3, {})} | custom-call | tf_op jit(solution)/shard_map/middle_grp/pallas_call | solution.py:444
  13.5 3.4 %collective-permute-done.5.refs_9_ = f32[48,256]{1,0:T(8,128)S(1)} collective-permute-done((f32[48,256]{1,0:T(8,128)S(1)}, f32[48,256]{1,0:T(8,128)S(1)}, u32[]{:S(2)}, u32[]{:S(2)}) %collective-permute-start.5) | collective-permute-done | bytes 49184 | tf_op jit(solution)/shard_map/ppermute | solution.py:385
  16.9 0.0 collective-permute-done.3.refs_4_
  16.9 0.0 collective-permute-done.4.refs_5_
  16.9 1.9 %middle_gx.1 = (f32[18,144,256]{2,1,0:T(8,128)S(1)}, f32[66,48,256]{2,1,0:T(8,128)S(1)}, f32[64,32,256]{2,1,0:T(8,128)S(1)}, f32[16,128]{1,0:T(8,128)S(1)}, f32[...) custom-call(f32[18,144,256]{2,1,0:T(8,128)S(1)} %get-tuple-element.3, ...), custom_call_target="tpu_custom_call", output_to_operand_aliasing={{0}: (0, {}), {1}: (1, {}), {2}: (2, {})} | custom-call | tf_op jit(solution)/shard_map/middle_gx/pallas_call | solution.py:515
  18.9 1.6 %collective-permute-start.7 = (f32[128,256]{1,0:T(8,128)S(1)}, f32[128,256]{1,0:T(8,128)S(1)}, u32[]{:S(2)}, u32[]{:S(2)}) collective-permute-start(f32[128,256]{1,0:T(8,128)S(1)} %get-tuple-element.52), channel_id=1, source_target_pairs={{0,2},{1,3},{2,0},{3,1},{4,6},{5,7},{6,4},{7,5},{8,10},{9,11},{10,... | collective-permute-start | bytes 393224 | tf_op jit(solution)/shard_map/ppermute | solution.py:374
  20.4 0.0 collective-permute-start.8
  20.4 2.2 %middle_rest.1 = (f32[18,144,256]{2,1,0:T(8,128)S(1)}, f32[48,256]{1,0:T(8,128)S(1)}, f32[48,256]{1,0:T(8,128)S(1)}, f32[48,256]{1,0:T(8,128)S(1)}) custom-call(f32[18,144,256]{2,1,0:T(8,128)S(1)} %get-tuple-element.44._, s32[16,128,256]{2,1,0:T(8,128)S(1)} %copy-done, f32[128,128]{1,0:T(8,128)S(1)} %get-tuple-element.45.zedge, ...), custom_call_target="tpu_custom_call", output_to_operand_aliasing={{0}: (0, {})} | custom-call | tf_op jit(solution)/shard_map/middle_rest/pallas_call | solution.py:532
  22.6 0.6 %collective-permute-start.6 = (f32[48,256]{1,0:T(8,128)S(1)}, f32[48,256]{1,0:T(8,128)S(1)}, u32[]{:S(2)}, u32[]{:S(2)}) collective-permute-start(f32[48,256]{1,0:T(8,128)S(1)} %get-tuple-element.48), channel_id=1, source_target_pairs={{0,1},{1,0},{2,3},{3,2},{4,5},{5,4},{6,7},{7,6},{8,9},{9,8},{10,11... | collective-permute-start | bytes 147464 | tf_op jit(solution)/shard_map/ppermute | solution.py:379
  23.2 0.1 collective-permute-start.10
  23.3 2.6 %collective-permute-start.9 = (f32[48,256]{1,0:T(8,128)S(1)}, f32[48,256]{1,0:T(8,128)S(1)}, u32[]{:S(2)}, u32[]{:S(2)}) collective-permute-start(f32[48,256]{1,0:T(8,128)S(1)} %get-tuple-element.54), channel_id=1, source_target_pairs={{0,8},{1,9},{8,0},{9,1},{16,24},{17,25},{24,16},{25,17},{2,10},{3,... | collective-permute-start | bytes 147464 | tf_op jit(solution)/shard_map/ppermute | solution.py:374
  25.8 0.0 collective-permute-done.6.side
  25.8 1.5 %end_fin.1 = (f32[64,32,256]{2,1,0:T(8,128)S(1)}, f32[18,144,256]{2,1,0:T(8,128)S(1)}) custom-call(f32[64,32,256]{2,1,0:T(8,128)S(1)} %get-tuple-element.43._0, f32[18,144,256]{2,1,0:T(8,128)S(1)} %get-tuple-element.47._1, f32[66,48,256]{2,1,0:T(8,128)S(1)} %get-tuple-element.46.first._1, ...), custom_call_target="tpu_custom_call", output_to_operand_aliasing={{0}: (0, {}), {1}: (1, {})} | custom-call | tf_op jit(solution)/shard_map/end_fin/pallas_call | solution.py:550
  27.3 0.0 collective-permute-done.10.pairb
  27.3 0.6 %collective-permute-done.9.paira = f32[48,256]{1,0:T(8,128)S(1)} collective-permute-done((f32[48,256]{1,0:T(8,128)S(1)}, f32[48,256]{1,0:T(8,128)S(1)}, u32[]{:S(2)}, u32[]{:S(2)}) %collective-permute-start.9) | collective-permute-done | bytes 49184 | tf_op jit(solution)/shard_map/ppermute | solution.py:374
  27.9 0.0 collective-permute-done.7.gxa
  27.9 0.0 collective-permute-done.8.gxb
  27.9 3.7 %end.1 = (f32[18,144,256]{2,1,0:T(8,128)S(1)}, f32[66,48,256]{2,1,0:T(8,128)S(1)}, f32[64,32,256]{2,1,0:T(8,128)S(1)}, f32[16,128,256]{2,1,0:T(8,128)}, f32[64,32,256]{2,1,0:T(8,128)}) custom-call(f32[18,144,256]{2,1,0:T(8,128)S(1)} %get-tuple-element.49._0, ...), custom_call_target="tpu_custom_call", output_to_operand_aliasing={{0}: (0, {}), {1}: (1, {}), {2}: (2, {})} | custom-call | tf_op jit(solution)/shard_map/end/pallas_call | solution.py:604
Async XLA Ops:
  0.6 7.1 %copy-start.2 = (f32[16,128,256]{2,1,0:T(8,128)S(1)}, f32[16,128,256]{2,1,0:T(8,128)}, u32[]{:S(2)}) copy-start(f32[16,128,256]{2,1,0:T(8,128)} %fluid_hbm.1) | copy-start | bytes 6291460
  0.6 7.1 %copy-start.3 = (f32[64,32,256]{2,1,0:T(8,128)S(1)}, f32[64,32,256]{2,1,0:T(8,128)}, u32[]{:S(2)}) copy-start(f32[64,32,256]{2,1,0:T(8,128)} %fin_hbm.1) | copy-start | bytes 6291460
  3.2 8.0 %copy-start = (s32[16,128,256]{2,1,0:T(8,128)S(1)}, s32[16,128,256]{2,1,0:T(8,128)}, u32[]{:S(2)}) copy-start(s32[16,128,256]{2,1,0:T(8,128)} %act.3) | copy-start | bytes 6291460
  3.2 8.0 %copy-start.1 = (f32[64,32,256]{2,1,0:T(8,128)S(1)}, f32[64,32,256]{2,1,0:T(8,128)}, u32[]{:S(2)}) copy-start(f32[64,32,256]{2,1,0:T(8,128)} %src.3) | copy-start | bytes 6291460
  3.2 13.7 %collective-permute-start.3 = (f32[176,256]{1,0:T(8,128)S(1)}, f32[176,256]{1,0:T(8,128)S(1)}, u32[]{:S(2)}, u32[]{:S(2)}) collective-permute-start(f32[176,256]{1,0:T(8,128)S(1)} %get-tuple-element.40), channel_id=1, source_target_pairs={{0,2},{2,0},{4,6},{6,4},{1,3},{3,1},{5,7},{7,5},{8,10},{10,8},{12,... | collective-permute-start | bytes 540680 | tf_op jit(solution)/shard_map/ppermute | solution.py:386
  6.3 10.7 %collective-permute-start.4 = (f32[176,256]{1,0:T(8,128)S(1)}, f32[176,256]{1,0:T(8,128)S(1)}, u32[]{:S(2)}, u32[]{:S(2)}) collective-permute-start(f32[176,256]{1,0:T(8,128)S(1)} %get-tuple-element.41), channel_id=1, source_target_pairs={{0,6},{2,4},{4,2},{6,0},{1,7},{3,5},{5,3},{7,1},{8,14},{10,12},{12... | collective-permute-start | bytes 540680 | tf_op jit(solution)/shard_map/ppermute | solution.py:387
  8.9 1.9 %collective-permute-start = (f32[48,256]{1,0:T(8,128)S(1)}, f32[48,256]{1,0:T(8,128)S(1)}, u32[]{:S(2)}, u32[]{:S(2)}) collective-permute-start(f32[48,256]{1,0:T(8,128)S(1)} %get-tuple-element.32), channel_id=1, source_target_pairs={{0,1},{1,0},{2,3},{3,2},{4,5},{5,4},{6,7},{7,6},{8,9},{9,8},{10,11... | collective-permute-start | bytes 147464 | tf_op jit(solution)/shard_map/ppermute | solution.py:379
  8.9 4.2 %collective-permute-start.1 = (f32[48,256]{1,0:T(8,128)S(1)}, f32[48,256]{1,0:T(8,128)S(1)}, u32[]{:S(2)}, u32[]{:S(2)}) collective-permute-start(f32[48,256]{1,0:T(8,128)S(1)} %get-tuple-element.35), channel_id=1, source_target_pairs={{0,8},{1,9},{8,0},{9,1},{16,24},{17,25},{24,16},{25,17},{2,10},{3,... | collective-permute-start | bytes 147464 | tf_op jit(solution)/shard_map/ppermute | solution.py:374
  10.6 2.5 %collective-permute-start.2 = (f32[48,256]{1,0:T(8,128)S(1)}, f32[48,256]{1,0:T(8,128)S(1)}, u32[]{:S(2)}, u32[]{:S(2)}) collective-permute-start(f32[48,256]{1,0:T(8,128)S(1)} %get-tuple-element.36), channel_id=1, source_target_pairs={{0,1},{1,0},{8,16},{9,17},{16,8},{17,9},{24,25},{25,24},{2,3},{3,2... | collective-permute-start | bytes 147464 | tf_op jit(solution)/shard_map/ppermute | solution.py:375
  10.7 6.2 %collective-permute-start.5 = (f32[48,256]{1,0:T(8,128)S(1)}, f32[48,256]{1,0:T(8,128)S(1)}, u32[]{:S(2)}, u32[]{:S(2)}) collective-permute-start(f32[48,256]{1,0:T(8,128)S(1)} %get-tuple-element.42.refs_8_), channel_id=1, source_target_pairs={{0,4},{2,6},{4,0},{6,2},{1,5},{3,7},{5,1},{7,3},{8,12},{10,14},{12... | collective-permute-start | bytes 147464 | tf_op jit(solution)/shard_map/ppermute | solution.py:385
  18.9 9.0 %collective-permute-start.7 = (f32[128,256]{1,0:T(8,128)S(1)}, f32[128,256]{1,0:T(8,128)S(1)}, u32[]{:S(2)}, u32[]{:S(2)}) collective-permute-start(f32[128,256]{1,0:T(8,128)S(1)} %get-tuple-element.52), channel_id=1, source_target_pairs={{0,2},{1,3},{2,0},{3,1},{4,6},{5,7},{6,4},{7,5},{8,10},{9,11},{10,... | collective-permute-start | bytes 393224 | tf_op jit(solution)/shard_map/ppermute | solution.py:374
  20.4 7.5 %collective-permute-start.8 = (f32[128,256]{1,0:T(8,128)S(1)}, f32[128,256]{1,0:T(8,128)S(1)}, u32[]{:S(2)}, u32[]{:S(2)}) collective-permute-start(f32[128,256]{1,0:T(8,128)S(1)} %get-tuple-element.53), channel_id=1, source_target_pairs={{0,1},{1,0},{2,4},{3,5},{4,2},{5,3},{6,7},{7,6},{8,9},{9,8},{10,12... | collective-permute-start | bytes 393224 | tf_op jit(solution)/shard_map/ppermute | solution.py:375
  22.6 3.2 %collective-permute-start.6 = (f32[48,256]{1,0:T(8,128)S(1)}, f32[48,256]{1,0:T(8,128)S(1)}, u32[]{:S(2)}, u32[]{:S(2)}) collective-permute-start(f32[48,256]{1,0:T(8,128)S(1)} %get-tuple-element.48), channel_id=1, source_target_pairs={{0,1},{1,0},{2,3},{3,2},{4,5},{5,4},{6,7},{7,6},{8,9},{9,8},{10,11... | collective-permute-start | bytes 147464 | tf_op jit(solution)/shard_map/ppermute | solution.py:379
  23.2 4.1 %collective-permute-start.10 = (f32[48,256]{1,0:T(8,128)S(1)}, f32[48,256]{1,0:T(8,128)S(1)}, u32[]{:S(2)}, u32[]{:S(2)}) collective-permute-start(f32[48,256]{1,0:T(8,128)S(1)} %get-tuple-element.55), channel_id=1, source_target_pairs={{0,1},{1,0},{8,16},{9,17},{16,8},{17,9},{24,25},{25,24},{2,3},{3,2... | collective-permute-start | bytes 147464 | tf_op jit(solution)/shard_map/ppermute | solution.py:375
  23.3 4.6 %collective-permute-start.9 = (f32[48,256]{1,0:T(8,128)S(1)}, f32[48,256]{1,0:T(8,128)S(1)}, u32[]{:S(2)}, u32[]{:S(2)}) collective-permute-start(f32[48,256]{1,0:T(8,128)S(1)} %get-tuple-element.54), channel_id=1, source_target_pairs={{0,8},{1,9},{8,0},{9,1},{16,24},{17,25},{24,16},{25,17},{2,10},{3,... | collective-permute-start | bytes 147464 | tf_op jit(solution)/shard_map/ppermute | solution.py:374

commit v2 on v1

--- a/solution.py
+++ b/solution.py
@@ -15,7 +15,7 @@
 FLUID_SCALE = 1.0 / (1.0 + 6.0 * FLUID_DIFFUSION)
 LANES = 128
 PAD = 8
-ROWS = 32
+ROWS = 16
 HIGHEST = lax.Precision.HIGHEST
 
 
@@ -76,19 +76,13 @@
     return kept.T[:cells]
 
 
-def pack_gx(plane, row, colour, gx, senda, sendb, dims):
-    cells, rows, _, depth, _, _ = dims
+def pack_gx(plane, colour, gx, senda, sendb, dims):
+    cells, rows, _, _, _, _ = dims
     half = rows // 2
     even = gx % 2 == 0
     for send, high in ((senda, even), (sendb, jnp.logical_not(even))):
         parity = jnp.where(high, (colour + cells - 1) % 2, colour)
         send[0:half, :] = checker_pack(plane(high), parity)
-
-    def lines(d):
-        senda[pl.ds(half + d, 1), :] = row(d, even)
-        sendb[pl.ds(half + d, 1), :] = row(d, jnp.logical_not(even))
-
-    repeat(depth, lines)
 
 
 def pack_rest(fluid, fin, colour, grpa, grpb, gyx, place, dims):
@@ -179,17 +173,15 @@
     zedge[...] = zrows[...].T
 
 
-def fluid_sweep(fluid, active, zedge, other, colour, dims, pairs, done=None):
+def fluid_sweep(fluid, active, zedge, others, colour, dims, pairs, done=None):
     _, rows, width, _, _, _ = dims
     parity = (iota((ROWS, width), 0) + iota((ROWS, width), 1)) & 1
     updating = parity == colour
     off = parity ^ colour
     end_parity = iota((1, width), 1) & 1
-
-    first_pair, step, count = pairs
-
-    def pair(j, carry):
-        k = first_pair + step * j
+    first_pair, step, trips, group = pairs
+
+    def merge(k, other):
         a, b = 2 * k + 1, 2 * k + 2
         for at, swap in ((PAD - 1, 1 - colour), (PAD + rows, colour)):
             line = slice(at, at + 1)
@@ -197,6 +189,9 @@
         for start in range(0, rows, ROWS):
             inner = slice(PAD + start, PAD + start + ROWS)
             other[inner, :] = jnp.where(updating, fluid[b, inner, :], fluid[a, inner, :])
+
+    def update(k, other):
+        a, b = 2 * k + 1, 2 * k + 2
         for start in range(0, rows, ROWS):
             inner = slice(PAD + start, PAD + start + ROWS)
             edge = pltpu.roll(zedge[start : start + ROWS, :], LANES - 1 - 2 * k, axis=1)
@@ -215,11 +210,35 @@
             mask_b = active[b - 1, start : start + ROWS, :] > 1 - off
             fluid[a, inner, :] = jnp.where(mask_a, new_a, here_a)
             fluid[b, inner, :] = jnp.where(mask_b, new_b, here_b)
-        if done is not None:
-            done(k)
+
+    def trip(j, carry):
+        ks = [first_pair + step * (group * j + u) for u in range(group)]
+        for u, k in enumerate(ks):
+            merge(k, others.at[u])
+        for u, k in enumerate(ks):
+            update(k, others.at[u])
+            if done is not None:
+                done(k)
         return carry
 
-    lax.fori_loop(0, count, pair, 0)
+    lax.fori_loop(0, trips, trip, 0)
+
+
+def add_gx_rows(target, offset, rows_at, received, half, scales, depth, sends=None):
+    def block(k, carry):
+        part = pl.ds(half + 8 * k, 8)
+        for n, (row, ref, scale) in enumerate(zip(rows_at, received, scales)):
+            halo = ref[part, :] * scale
+            new = [
+                target[8 * k + j + offset, pl.ds(row, 1), :] + halo[j : j + 1, :] for j in range(8)
+            ]
+            for j in range(8):
+                target[8 * k + j + offset, pl.ds(row, 1), :] = new[j]
+            if sends is not None:
+                sends[n][part, :] = jnp.concatenate(new, axis=0)
+        return carry
+
+    lax.fori_loop(0, depth // 8, block, 0)
 
 
 def fin_neighbours(fin, d, hedge, fin_rows):
@@ -258,10 +277,12 @@
         cells, rows, width = fluid_temp.shape
         depth, fin_rows, fin_width = fin_temp.shape
         assert rows == LANES and width == fin_width == 2 * rows and fin_rows == 2 * cells
-        assert 2 * depth <= LANES and depth % 8 == 0 and depth >= 24 and cells % 2 == 0 and cells >= 4 and rows % ROWS == 0 and fin_rows == ROWS
+        assert 2 * depth <= LANES and depth % 8 == 0 and depth >= 24 and cells % 2 == 0 and cells >= 4 and rows % ROWS == 0 and fin_rows % 8 == 0
         dims = (cells, rows, width, depth, fin_rows, fin_width)
         half = rows // 2
         pairs = cells // 2
+        outer_group = max(g for g in (1, 2, 4) if pairs % g == 0)
+        inner_group = max(g for g in (1, 2, 3) if (pairs - 2) % g == 0)
         face_rows = half + depth
         wall_rows = fin_rows + cells
         gx_rows = face_rows + (wall_rows if ring else 0)
@@ -292,7 +313,7 @@
             ]
             for item in copies:
                 item.start()
-            for item in copies:
+            for item in copies[:4]:
                 item.wait()
             shape = (cells, rows)
             shift = tgt[...] - 2 * (iota(shape, 0) * fin_width + iota(shape, 1))
@@ -303,11 +324,22 @@
             even_rows = dot(interleave_matrix(fin_rows), root[...], ((0,), (0,)))
             wall[0:fin_rows, :] = dot(even_rows, interleave_matrix(fin_width), ((1,), (0,)))
             gx = lax.axis_index("gx")
-            pack_gx(
-                lambda high: planes[jnp.where(high, 1, 0)],
-                lambda d, high: jnp.where(high, high_rows[d, PAD - 1 : PAD, :], low_rows[d, 0:1, :]),
-                1, gx, gxa, gxb, dims,
-            )
+            for item in copies[4:]:
+                item.wait()
+            pack_gx(lambda high: planes[jnp.where(high, 1, 0)], 1, gx, gxa, gxb, dims)
+            even = gx % 2 == 0
+
+            def lines(k, carry):
+                part = pl.ds(half + 8 * k, 8)
+                low = jnp.concatenate([low_rows[8 * k + j, 0:1, :] for j in range(8)], axis=0)
+                high = jnp.concatenate(
+                    [high_rows[8 * k + j, PAD - 1 : PAD, :] for j in range(8)], axis=0
+                )
+                gxa[part, :] = jnp.where(even, high, low)
+                gxb[part, :] = jnp.where(even, low, high)
+                return carry
+
+            lax.fori_loop(0, depth // 8, lines, 0)
             if ring:
                 gxa[face_rows:, :] = wall[...]
                 gxb[face_rows:, :] = wall[...]
@@ -494,31 +526,26 @@
             row_a = jnp.where(even, high_row, PAD)
             row_b = PAD + high_row - row_a
             scale = FIN_CONDUCTION / DIAG
-
-            def add_row(d):
-                first[d + 1, pl.ds(row_a, 1), :] += gxa_in[pl.ds(half + d, 1), :] * scale
-                first[d + 1, pl.ds(row_b, 1), :] += gxb_in[pl.ds(half + d, 1), :] * (scale * inside)
-
-            repeat(depth, add_row)
+            add_gx_rows(first, 1, (row_a, row_b), (gxa_in, gxb_in), half, (scale, scale * inside),
+                        depth, (gxa, gxb))
             below, above = grp_halos(paira, pairb, grp, groups)
             unpack_fluid(fluid, zrows, zedge, gxa_in, gxb_in, ghost, below, above, 0, place, count,
                          dims)
-            fluid_sweep(fluid, act, zedge, other, 0, dims, (0, pairs - 1, 2))
+            fluid_sweep(fluid, act, zedge, other, 0, dims, (0, pairs - 1, 1, 2))
             pack_gx(
-                lambda high: fluid[jnp.where(high, cells, 1), PAD : PAD + rows, :],
-                lambda d, high: first[d + 1, pl.ds(jnp.where(high, high_row, PAD), 1), :],
-                0, gx, gxa, gxb, dims,
+                lambda high: fluid[jnp.where(high, cells, 1), PAD : PAD + rows, :], 0, gx, gxa, gxb,
+                dims,
             )
 
         zrows_buffer, zedge_buffer = buffer(LANES, rows), buffer(rows, LANES)
-        other_buffer = buffer(rows + 2 * PAD, width)
+        other_buffer = lambda planes: buffer(planes, rows + 2 * PAD, width)
         fluid1, first, rest, ghost, zedge, gxa, gxb = pl.pallas_call(
             middle_gx_kernel,
             out_shape=(fluid_pad, fin_pad, fin_rest, f32(cells, rows),
                        f32(rows, LANES), f32(face_rows, width), f32(face_rows, width)),
             in_specs=[vmem] * (8 + len(walls)),
             out_specs=(vmem,) * 7,
-            scratch_shapes=[zrows_buffer, other_buffer],
+            scratch_shapes=[zrows_buffer, other_buffer(2)],
             input_output_aliases={0: 0, 1: 1, 2: 2},
             compiler_params=params,
             name="middle_gx",
@@ -526,7 +553,7 @@
         gxa, gxb = exchange("gx", count, gxa, gxb)
 
         def middle_rest_kernel(_, act, zedge, first, fluid, grpa, grpb, gyx, other):
-            fluid_sweep(fluid, act, zedge, other, 0, dims, (1, 1, pairs - 2))
+            fluid_sweep(fluid, act, zedge, other, 0, dims, (1, 1, (pairs - 2) // inner_group, inner_group))
             pack_rest(fluid, first, 1, grpa, grpb, gyx, my_place(), dims)
 
         fluid2, grpa, grpb, gyx = pl.pallas_call(
@@ -534,7 +561,7 @@
             out_shape=(fluid_pad,) + faces,
             in_specs=[vmem] * 4,
             out_specs=(vmem,) * 4,
-            scratch_shapes=[other_buffer],
+            scratch_shapes=[other_buffer(inner_group)],
             input_output_aliases={0: 0},
             compiler_params=params,
             name="middle_rest",
@@ -580,17 +607,12 @@
             row_a = jnp.where(even, fin_rows - 1, 0)
             row_b = fin_rows - 1 - row_a
             scale = OMEGA * FIN_CONDUCTION / DIAG
-
-            def add_row(d):
-                rest[d, pl.ds(row_a, 1), :] += gxa[pl.ds(half + d, 1), :] * scale
-                rest[d, pl.ds(row_b, 1), :] += gxb[pl.ds(half + d, 1), :] * (scale * inside)
-
-            repeat(depth, add_row)
+            add_gx_rows(rest, 0, (row_a, row_b), (gxa, gxb), half, (scale, scale * inside), depth)
             fin_copies = [fin_copy(0, 0, depth)]
             fin_copies[0].start()
             below, above = grp_halos(paira, pairb, place[0], groups)
             unpack_fluid(fluid, zrows, zedge, gxa, gxb, ghost, below, above, 1, place, count, dims)
-            fluid_sweep(fluid, act, zedge, other, 1, dims, (0, 1, pairs),
+            fluid_sweep(fluid, act, zedge, other, 1, dims, (0, 1, pairs // outer_group, outer_group),
                         lambda k: fluid_copy(k).start())
 
             def finish(k, carry):
@@ -607,7 +629,7 @@
                        f32(cells, rows, width), f32(depth, fin_rows, fin_width)),
             in_specs=[vmem] * 10,
             out_specs=(vmem, vmem, vmem, hbm, hbm),
-            scratch_shapes=[zrows_buffer, zedge_buffer, other_buffer,
+            scratch_shapes=[zrows_buffer, zedge_buffer, other_buffer(outer_group),
                             pltpu.SemaphoreType.DMA((pairs,)), pltpu.SemaphoreType.DMA((1,))],
             input_output_aliases={0: 0, 1: 1, 2: 2},
             compiler_params=params,

time: 31.7 us -> 30 us (0.946)
  Pallas kernels: 14.9 us -> 13.1 us
    pallas_call x1, Pallas kernels: 3.69 us -> 3.08 us  [local(): pl.pallas_call(end_kernel, out_shape=(fluid_pad, fin_pad, f32(depth, fin_...]
    pallas_call x1, Pallas kernels: 1.95 us -> 1.37 us  [local(): pl.pallas_call(middle_gx_kernel, out_shape=(fluid_pad, fin_pad, fin_rest,...]
    pallas_call x1, Pallas kernels: 2.54 us -> 2.18 us  [local(): pl.pallas_call(start_gx_kernel, out_shape=(f32(gx_rows, width), f32(gx_ro...]
  transfers between devices with their start and end apart: 11 -> 11, of which waited for: 3 -> 3; matrix products, arithmetic and copies ran while one was open for 0% -> 0% of each run, Pallas kernels for 21% -> 22%
where the time goes in v2:
time: 30 us; the launch traced here: 29.8 us
  Pallas kernels  13.1 us (44%)
  starting transfers between devices  11.7 us (39%)
  waiting for transfers between devices  4.28 us (14%)
  between operations  0.75 us (2%)
    ppermute x3, starting transfers between devices, exchange(): paira = lax.ppermute(paira, axes, first)  5.77 us
    ppermute x1, waiting for transfers between devices, local(): walls = [wall, lax.ppermute(wall, 'gx', mixed_with(2))]  3.41 us
    pallas_call x1, Pallas kernels, local(): pl.pallas_call(end_kernel, out_shape=(fluid_pad, fin_pad, f32(depth, fin_...  3.08 us
    ppermute x1, starting transfers between devices, local(): gxa = lax.ppermute(gxa, 'gx', mixed_with(1))  3.03 us
    pallas_call x1, Pallas kernels, local(): pl.pallas_call(start_gx_kernel, out_shape=(f32(gx_rows, width), f32(gx_ro...  2.18 us
    pallas_call x1, Pallas kernels, local(): pl.pallas_call(middle_rest_kernel, out_shape=(fluid_pad,) + faces, in_spe...  1.93 us
    pallas_call x1, Pallas kernels, local(): pl.pallas_call(middle_fin_kernel, out_shape=(fin_pad, f32(depth, fin_rows...  1.56 us
    ppermute x1, starting transfers between devices, local(): gxb = lax.ppermute(gxb, 'gx', mixed_with(3))  1.49 us
  transfers between devices with their start and end apart: 11, of which 3 were waited for; matrix products, arithmetic and copies ran while one was open for 0% of the time, Pallas kernels for 22%

profile of v2, /device:TPU:0, one launch (start us, length us, event | category | flops | bytes accessed | tf_op | source)
XLA Modules:
  0.0 29.8 jit_solution(17272249465457946401)
XLA Ops:
  0.6 0.0 copy-start.2
  0.6 0.0 copy-start.3
  0.7 2.2 %start_gx.1 = (f32[176,256]{1,0:T(8,128)S(1)}, f32[176,256]{1,0:T(8,128)S(1)}, f32[48,256]{1,0:T(8,128)S(1)}) custom-call(f32[16,128,256]{2,1,0:T(8,128)} %fluid_hbm.1, f32[64,32,256]{2,1,0:T(8,128)} %fin_hbm.1, s32[16,128]{1,0:T(8,128)} %bitcast.2, s32[16,128]{1,0:T(8,128)} %bitcast.3), custom_call_target="tpu_custom_call" | custom-call | tf_op jit(solution)/shard_map/start_gx/pallas_call | solution.py:353
  2.8 0.0 copy-start
  2.8 0.0 copy-start.1
  2.9 3.0 %collective-permute-start.3 = (f32[176,256]{1,0:T(8,128)S(1)}, f32[176,256]{1,0:T(8,128)S(1)}, u32[]{:S(2)}, u32[]{:S(2)}) collective-permute-start(f32[176,256]{1,0:T(8,128)S(1)} %get-tuple-element.40), channel_id=1, source_target_pairs={{0,2},{2,0},{4,6},{6,4},{1,3},{3,1},{5,7},{7,5},{8,10},{10,8},{12,... | collective-permute-start | bytes 540680 | tf_op jit(solution)/shard_map/ppermute | solution.py:418
  5.9 1.5 %collective-permute-start.4 = (f32[176,256]{1,0:T(8,128)S(1)}, f32[176,256]{1,0:T(8,128)S(1)}, u32[]{:S(2)}, u32[]{:S(2)}) collective-permute-start(f32[176,256]{1,0:T(8,128)S(1)} %get-tuple-element.41), channel_id=1, source_target_pairs={{0,6},{2,4},{4,2},{6,0},{1,7},{3,5},{5,3},{7,1},{8,14},{10,12},{12... | collective-permute-start | bytes 540680 | tf_op jit(solution)/shard_map/ppermute | solution.py:419
  7.4 0.0 copy-done.2
  7.4 0.0 copy-done.3
  7.4 1.1 %start_rest.1 = (f32[18,144,256]{2,1,0:T(8,128)S(1)}, f32[66,48,256]{2,1,0:T(8,128)S(1)}, f32[48,256]{1,0:T(8,128)S(1)}, f32[48,256]{1,0:T(8,128)S(1)}, f32[48,256]{1,0:T(8,128)S(1)}) custom-call(f32[16,128,256]{2,1,0:T(8,128)S(1)} %copy-done.2, f32[64,32,256]{2,1,0:T(8,128)S(1)} %copy-done.3), custom_call_target="tpu_custom_call" | custom-call | tf_op jit(solution)/shard_map/start_rest/pallas_call | solution.py:383
  8.5 0.1 collective-permute-start
  8.6 1.6 %collective-permute-start.1 = (f32[48,256]{1,0:T(8,128)S(1)}, f32[48,256]{1,0:T(8,128)S(1)}, u32[]{:S(2)}, u32[]{:S(2)}) collective-permute-start(f32[48,256]{1,0:T(8,128)S(1)} %get-tuple-element.35), channel_id=1, source_target_pairs={{0,8},{1,9},{8,0},{9,1},{16,24},{17,25},{24,16},{25,17},{2,10},{3,... | collective-permute-start | bytes 147464 | tf_op jit(solution)/shard_map/ppermute | solution.py:406
  10.2 0.2 collective-permute-start.2
  10.4 0.0 collective-permute-done.side
  10.4 0.5 %collective-permute-start.5 = (f32[48,256]{1,0:T(8,128)S(1)}, f32[48,256]{1,0:T(8,128)S(1)}, u32[]{:S(2)}, u32[]{:S(2)}) collective-permute-start(f32[48,256]{1,0:T(8,128)S(1)} %get-tuple-element.42.refs_8_), channel_id=1, source_target_pairs={{0,4},{2,6},{4,0},{6,2},{1,5},{3,7},{5,1},{7,3},{8,12},{10,14},{12... | collective-permute-start | bytes 147464 | tf_op jit(solution)/shard_map/ppermute | solution.py:417
  10.9 0.0 copy-done
  10.9 0.0 copy-done.1
  10.9 1.6 %middle_fin.1 = (f32[66,48,256]{2,1,0:T(8,128)S(1)}, f32[64,32,256]{2,1,0:T(8,128)S(1)}) custom-call(f32[66,48,256]{2,1,0:T(8,128)S(1)} %get-tuple-element.31.fin._1, f32[64,32,256]{2,1,0:T(8,128)S(1)} %copy-done.1, f32[48,256]{1,0:T(8,128)S(1)} %collective-permute-done.side, s32[16,128,256]{2,1,0:T(8,128)S(1)} %copy-done), custom_call_target="tpu_custom_call" | custom-call | tf_op jit(solution)/shard_map/middle_fin/pallas_call | solution.py:459
  12.4 0.3 collective-permute-done.1.paira.refs_6_
  12.7 0.0 collective-permute-done.2.pairb.refs_7_
  12.7 0.4 %middle_grp.1 = (f32[18,144,256]{2,1,0:T(8,128)S(1)}, f32[66,48,256]{2,1,0:T(8,128)S(1)}, f32[66,48,256]{2,1,0:T(8,128)S(1)}, f32[64,32,256]{2,1,0:T(8,128)S(1)}) custom-call(f32[18,144,256]{2,1,0:T(8,128)S(1)} %get-tuple-element.30._0, ...), custom_call_target="tpu_custom_call", output_to_operand_aliasing={{0}: (0, {}), {1}: (1, {}), {2}: (2, {}), {3}: (3, {})} | custom-call | tf_op jit(solution)/shard_map/middle_grp/pallas_call | solution.py:476
  13.2 3.4 %collective-permute-done.5.refs_9_ = f32[48,256]{1,0:T(8,128)S(1)} collective-permute-done((f32[48,256]{1,0:T(8,128)S(1)}, f32[48,256]{1,0:T(8,128)S(1)}, u32[]{:S(2)}, u32[]{:S(2)}) %collective-permute-start.5) | collective-permute-done | bytes 49184 | tf_op jit(solution)/shard_map/ppermute | solution.py:417
  16.6 0.0 collective-permute-done.3.refs_4_
  16.6 0.0 collective-permute-done.4.refs_5_
  16.6 1.4 %middle_gx.1 = (f32[18,144,256]{2,1,0:T(8,128)S(1)}, f32[66,48,256]{2,1,0:T(8,128)S(1)}, f32[64,32,256]{2,1,0:T(8,128)S(1)}, f32[16,128]{1,0:T(8,128)S(1)}, f32[...) custom-call(f32[18,144,256]{2,1,0:T(8,128)S(1)} %get-tuple-element.3, ...), custom_call_target="tpu_custom_call", output_to_operand_aliasing={{0}: (0, {}), {1}: (1, {}), {2}: (2, {})} | custom-call | tf_op jit(solution)/shard_map/middle_gx/pallas_call | solution.py:542
  17.9 1.6 %collective-permute-start.7 = (f32[128,256]{1,0:T(8,128)S(1)}, f32[128,256]{1,0:T(8,128)S(1)}, u32[]{:S(2)}, u32[]{:S(2)}) collective-permute-start(f32[128,256]{1,0:T(8,128)S(1)} %get-tuple-element.52), channel_id=1, source_target_pairs={{0,2},{1,3},{2,0},{3,1},{4,6},{5,7},{6,4},{7,5},{8,10},{9,11},{10,... | collective-permute-start | bytes 393224 | tf_op jit(solution)/shard_map/ppermute | solution.py:406
  19.5 0.0 collective-permute-start.8
  19.5 1.9 %middle_rest.1 = (f32[18,144,256]{2,1,0:T(8,128)S(1)}, f32[48,256]{1,0:T(8,128)S(1)}, f32[48,256]{1,0:T(8,128)S(1)}, f32[48,256]{1,0:T(8,128)S(1)}) custom-call(f32[18,144,256]{2,1,0:T(8,128)S(1)} %get-tuple-element.44._, s32[16,128,256]{2,1,0:T(8,128)S(1)} %copy-done, f32[128,128]{1,0:T(8,128)S(1)} %get-tuple-element.45.zedge, ...), custom_call_target="tpu_custom_call", output_to_operand_aliasing={{0}: (0, {})} | custom-call | tf_op jit(solution)/shard_map/middle_rest/pallas_call | solution.py:559
  21.4 0.6 %collective-permute-start.6 = (f32[48,256]{1,0:T(8,128)S(1)}, f32[48,256]{1,0:T(8,128)S(1)}, u32[]{:S(2)}, u32[]{:S(2)}) collective-permute-start(f32[48,256]{1,0:T(8,128)S(1)} %get-tuple-element.48), channel_id=1, source_target_pairs={{0,1},{1,0},{2,3},{3,2},{4,5},{5,4},{6,7},{7,6},{8,9},{9,8},{10,11... | collective-permute-start | bytes 147464 | tf_op jit(solution)/shard_map/ppermute | solution.py:411
  22.0 0.1 collective-permute-start.10
  22.1 2.6 %collective-permute-start.9 = (f32[48,256]{1,0:T(8,128)S(1)}, f32[48,256]{1,0:T(8,128)S(1)}, u32[]{:S(2)}, u32[]{:S(2)}) collective-permute-start(f32[48,256]{1,0:T(8,128)S(1)} %get-tuple-element.54), channel_id=1, source_target_pairs={{0,8},{1,9},{8,0},{9,1},{16,24},{17,25},{24,16},{25,17},{2,10},{3,... | collective-permute-start | bytes 147464 | tf_op jit(solution)/shard_map/ppermute | solution.py:406
  24.7 0.0 collective-permute-done.6.side
  24.7 1.5 %end_fin.1 = (f32[64,32,256]{2,1,0:T(8,128)S(1)}, f32[18,144,256]{2,1,0:T(8,128)S(1)}) custom-call(f32[64,32,256]{2,1,0:T(8,128)S(1)} %get-tuple-element.43._0, f32[18,144,256]{2,1,0:T(8,128)S(1)} %get-tuple-element.47._1, f32[66,48,256]{2,1,0:T(8,128)S(1)} %get-tuple-element.46.first._1, ...), custom_call_target="tpu_custom_call", output_to_operand_aliasing={{0}: (0, {}), {1}: (1, {})} | custom-call | tf_op jit(solution)/shard_map/end_fin/pallas_call | solution.py:577
  26.2 0.0 collective-permute-done.10.pairb
  26.2 0.6 %collective-permute-done.9.paira = f32[48,256]{1,0:T(8,128)S(1)} collective-permute-done((f32[48,256]{1,0:T(8,128)S(1)}, f32[48,256]{1,0:T(8,128)S(1)}, u32[]{:S(2)}, u32[]{:S(2)}) %collective-permute-start.9) | collective-permute-done | bytes 49184 | tf_op jit(solution)/shard_map/ppermute | solution.py:406
  26.7 0.0 collective-permute-done.7.gxa
  26.7 0.0 collective-permute-done.8.gxb
  26.7 3.1 %end.1 = (f32[18,144,256]{2,1,0:T(8,128)S(1)}, f32[66,48,256]{2,1,0:T(8,128)S(1)}, f32[64,32,256]{2,1,0:T(8,128)S(1)}, f32[16,128,256]{2,1,0:T(8,128)}, f32[64,32,256]{2,1,0:T(8,128)}) custom-call(f32[18,144,256]{2,1,0:T(8,128)S(1)} %get-tuple-element.49._0, ...), custom_call_target="tpu_custom_call", output_to_operand_aliasing={{0}: (0, {}), {1}: (1, {}), {2}: (2, {})} | custom-call | tf_op jit(solution)/shard_map/end/pallas_call | solution.py:626
Async XLA Ops:
  0.6 6.8 %copy-start.2 = (f32[16,128,256]{2,1,0:T(8,128)S(1)}, f32[16,128,256]{2,1,0:T(8,128)}, u32[]{:S(2)}) copy-start(f32[16,128,256]{2,1,0:T(8,128)} %fluid_hbm.1) | copy-start | bytes 6291460
  0.6 6.8 %copy-start.3 = (f32[64,32,256]{2,1,0:T(8,128)S(1)}, f32[64,32,256]{2,1,0:T(8,128)}, u32[]{:S(2)}) copy-start(f32[64,32,256]{2,1,0:T(8,128)} %fin_hbm.1) | copy-start | bytes 6291460
  2.8 8.0 %copy-start = (s32[16,128,256]{2,1,0:T(8,128)S(1)}, s32[16,128,256]{2,1,0:T(8,128)}, u32[]{:S(2)}) copy-start(s32[16,128,256]{2,1,0:T(8,128)} %act.3) | copy-start | bytes 6291460
  2.8 8.0 %copy-start.1 = (f32[64,32,256]{2,1,0:T(8,128)S(1)}, f32[64,32,256]{2,1,0:T(8,128)}, u32[]{:S(2)}) copy-start(f32[64,32,256]{2,1,0:T(8,128)} %src.3) | copy-start | bytes 6291460
  2.9 13.7 %collective-permute-start.3 = (f32[176,256]{1,0:T(8,128)S(1)}, f32[176,256]{1,0:T(8,128)S(1)}, u32[]{:S(2)}, u32[]{:S(2)}) collective-permute-start(f32[176,256]{1,0:T(8,128)S(1)} %get-tuple-element.40), channel_id=1, source_target_pairs={{0,2},{2,0},{4,6},{6,4},{1,3},{3,1},{5,7},{7,5},{8,10},{10,8},{12,... | collective-permute-start | bytes 540680 | tf_op jit(solution)/shard_map/ppermute | solution.py:418
  5.9 10.7 %collective-permute-start.4 = (f32[176,256]{1,0:T(8,128)S(1)}, f32[176,256]{1,0:T(8,128)S(1)}, u32[]{:S(2)}, u32[]{:S(2)}) collective-permute-start(f32[176,256]{1,0:T(8,128)S(1)} %get-tuple-element.41), channel_id=1, source_target_pairs={{0,6},{2,4},{4,2},{6,0},{1,7},{3,5},{5,3},{7,1},{8,14},{10,12},{12... | collective-permute-start | bytes 540680 | tf_op jit(solution)/shard_map/ppermute | solution.py:419
  8.5 1.9 %collective-permute-start = (f32[48,256]{1,0:T(8,128)S(1)}, f32[48,256]{1,0:T(8,128)S(1)}, u32[]{:S(2)}, u32[]{:S(2)}) collective-permute-start(f32[48,256]{1,0:T(8,128)S(1)} %get-tuple-element.32), channel_id=1, source_target_pairs={{0,1},{1,0},{2,3},{3,2},{4,5},{5,4},{6,7},{7,6},{8,9},{9,8},{10,11... | collective-permute-start | bytes 147464 | tf_op jit(solution)/shard_map/ppermute | solution.py:411
  8.6 4.2 %collective-permute-start.1 = (f32[48,256]{1,0:T(8,128)S(1)}, f32[48,256]{1,0:T(8,128)S(1)}, u32[]{:S(2)}, u32[]{:S(2)}) collective-permute-start(f32[48,256]{1,0:T(8,128)S(1)} %get-tuple-element.35), channel_id=1, source_target_pairs={{0,8},{1,9},{8,0},{9,1},{16,24},{17,25},{24,16},{25,17},{2,10},{3,... | collective-permute-start | bytes 147464 | tf_op jit(solution)/shard_map/ppermute | solution.py:406
  10.2 2.5 %collective-permute-start.2 = (f32[48,256]{1,0:T(8,128)S(1)}, f32[48,256]{1,0:T(8,128)S(1)}, u32[]{:S(2)}, u32[]{:S(2)}) collective-permute-start(f32[48,256]{1,0:T(8,128)S(1)} %get-tuple-element.36), channel_id=1, source_target_pairs={{0,1},{1,0},{8,16},{9,17},{16,8},{17,9},{24,25},{25,24},{2,3},{3,2... | collective-permute-start | bytes 147464 | tf_op jit(solution)/shard_map/ppermute | solution.py:407
  10.4 6.2 %collective-permute-start.5 = (f32[48,256]{1,0:T(8,128)S(1)}, f32[48,256]{1,0:T(8,128)S(1)}, u32[]{:S(2)}, u32[]{:S(2)}) collective-permute-start(f32[48,256]{1,0:T(8,128)S(1)} %get-tuple-element.42.refs_8_), channel_id=1, source_target_pairs={{0,4},{2,6},{4,0},{6,2},{1,5},{3,7},{5,1},{7,3},{8,12},{10,14},{12... | collective-permute-start | bytes 147464 | tf_op jit(solution)/shard_map/ppermute | solution.py:417
  17.9 8.8 %collective-permute-start.7 = (f32[128,256]{1,0:T(8,128)S(1)}, f32[128,256]{1,0:T(8,128)S(1)}, u32[]{:S(2)}, u32[]{:S(2)}) collective-permute-start(f32[128,256]{1,0:T(8,128)S(1)} %get-tuple-element.52), channel_id=1, source_target_pairs={{0,2},{1,3},{2,0},{3,1},{4,6},{5,7},{6,4},{7,5},{8,10},{9,11},{10,... | collective-permute-start | bytes 393224 | tf_op jit(solution)/shard_map/ppermute | solution.py:406
  19.5 7.2 %collective-permute-start.8 = (f32[128,256]{1,0:T(8,128)S(1)}, f32[128,256]{1,0:T(8,128)S(1)}, u32[]{:S(2)}, u32[]{:S(2)}) collective-permute-start(f32[128,256]{1,0:T(8,128)S(1)} %get-tuple-element.53), channel_id=1, source_target_pairs={{0,1},{1,0},{2,4},{3,5},{4,2},{5,3},{6,7},{7,6},{8,9},{9,8},{10,12... | collective-permute-start | bytes 393224 | tf_op jit(solution)/shard_map/ppermute | solution.py:407
  21.4 3.2 %collective-permute-start.6 = (f32[48,256]{1,0:T(8,128)S(1)}, f32[48,256]{1,0:T(8,128)S(1)}, u32[]{:S(2)}, u32[]{:S(2)}) collective-permute-start(f32[48,256]{1,0:T(8,128)S(1)} %get-tuple-element.48), channel_id=1, source_target_pairs={{0,1},{1,0},{2,3},{3,2},{4,5},{5,4},{6,7},{7,6},{8,9},{9,8},{10,11... | collective-permute-start | bytes 147464 | tf_op jit(solution)/shard_map/ppermute | solution.py:411
  22.0 4.1 %collective-permute-start.10 = (f32[48,256]{1,0:T(8,128)S(1)}, f32[48,256]{1,0:T(8,128)S(1)}, u32[]{:S(2)}, u32[]{:S(2)}) collective-permute-start(f32[48,256]{1,0:T(8,128)S(1)} %get-tuple-element.55), channel_id=1, source_target_pairs={{0,1},{1,0},{8,16},{9,17},{16,8},{17,9},{24,25},{25,24},{2,3},{3,2... | collective-permute-start | bytes 147464 | tf_op jit(solution)/shard_map/ppermute | solution.py:407
  22.1 4.6 %collective-permute-start.9 = (f32[48,256]{1,0:T(8,128)S(1)}, f32[48,256]{1,0:T(8,128)S(1)}, u32[]{:S(2)}, u32[]{:S(2)}) collective-permute-start(f32[48,256]{1,0:T(8,128)S(1)} %get-tuple-element.54), channel_id=1, source_target_pairs={{0,8},{1,9},{8,0},{9,1},{16,24},{17,25},{24,16},{25,17},{2,10},{3,... | collective-permute-start | bytes 147464 | tf_op jit(solution)/shard_map/ppermute | solution.py:406

commit v3 on v2

--- a/solution.py
+++ b/solution.py
@@ -173,13 +173,12 @@
     zedge[...] = zrows[...].T
 
 
-def fluid_sweep(fluid, active, zedge, others, colour, dims, pairs, done=None):
+def neighbour_sums(fluid, others, sums, colour, dims, pairs):
     _, rows, width, _, _, _ = dims
-    parity = (iota((ROWS, width), 0) + iota((ROWS, width), 1)) & 1
-    updating = parity == colour
-    off = parity ^ colour
+    updating = ((iota((ROWS, width), 0) + iota((ROWS, width), 1)) & 1) == colour
     end_parity = iota((1, width), 1) & 1
     first_pair, step, trips, group = pairs
+    empty = jnp.zeros((ROWS, LANES), jnp.float32)
 
     def merge(k, other):
         a, b = 2 * k + 1, 2 * k + 2
@@ -190,16 +189,41 @@
             inner = slice(PAD + start, PAD + start + ROWS)
             other[inner, :] = jnp.where(updating, fluid[b, inner, :], fluid[a, inner, :])
 
-    def update(k, other):
+    def add(other, total):
+        for start in range(0, rows, ROWS):
+            inner = slice(PAD + start, PAD + start + ROWS)
+            total[start : start + ROWS, :] = (
+                other[PAD + start - 1 : PAD + start + ROWS - 1, :]
+                + other[PAD + start + 1 : PAD + start + ROWS + 1, :]
+                + lane_neighbours(other[inner, :], empty, empty)
+            )
+
+    def trip(j, carry):
+        ns = [group * j + u for u in range(group)]
+        for u, n in enumerate(ns):
+            merge(first_pair + step * n, others.at[u])
+        for u, n in enumerate(ns):
+            add(others.at[u], sums.at[n])
+        return carry
+
+    lax.fori_loop(0, trips, trip, 0)
+
+
+def fluid_update(fluid, active, zedge, sums, colour, dims, pairs, done=None):
+    _, rows, width, _, _, _ = dims
+    off = ((iota((ROWS, width), 0) + iota((ROWS, width), 1)) & 1) ^ colour
+    lane = iota((ROWS, LANES), 1)
+    first_pair, step, trips, group = pairs
+
+    def update(k, total):
         a, b = 2 * k + 1, 2 * k + 2
         for start in range(0, rows, ROWS):
             inner = slice(PAD + start, PAD + start + ROWS)
             edge = pltpu.roll(zedge[start : start + ROWS, :], LANES - 1 - 2 * k, axis=1)
-            shared = (
-                other[PAD + start - 1 : PAD + start + ROWS - 1, :]
-                + other[PAD + start + 1 : PAD + start + ROWS + 1, :]
-                + lane_neighbours(other[inner, :], edge, edge)
-            )
+            parts = tiles(total[start : start + ROWS, :])
+            parts[0] = parts[0] + jnp.where(lane == 0, edge, 0.0)
+            parts[-1] = parts[-1] + jnp.where(lane == LANES - 1, edge, 0.0)
+            shared = jnp.concatenate(parts, axis=1)
             here_a = fluid[a, inner, :]
             here_b = fluid[b, inner, :]
             total_a = shared + fluid[a - 1, inner, :] + here_b
@@ -212,13 +236,11 @@
             fluid[b, inner, :] = jnp.where(mask_b, new_b, here_b)
 
     def trip(j, carry):
-        ks = [first_pair + step * (group * j + u) for u in range(group)]
-        for u, k in enumerate(ks):
-            merge(k, others.at[u])
-        for u, k in enumerate(ks):
-            update(k, others.at[u])
+        for u in range(group):
+            n = group * j + u
+            update(first_pair + step * n, sums.at[n])
             if done is not None:
-                done(k)
+                done(first_pair + step * n)
         return carry
 
     lax.fori_loop(0, trips, trip, 0)
@@ -465,28 +487,33 @@
             name="middle_fin",
         )(fin0, fin_source, side, active)
 
-        def middle_grp_kernel(_0, _1, _2, _3, src, paira, pairb, side, fluid, fin, first, rest):
+        def middle_grp_kernel(_0, _1, _2, _3, src, paira, pairb, side, fluid, fin, first, rest,
+                              sums, others):
             fin_depth_halos(fin, paira, pairb)
             hedge = side[cells : cells + fin_rows, 0:LANES]
             for block in (0, blocks - 1):
                 fin_first(fin, src, first, rest, hedge, block)
             unpack_lines(fluid, side, lax.axis_index("gy"), dims)
+            neighbour_sums(fluid, others, sums, 0, dims, outer_pairs)
 
         fin_rest = f32(depth, fin_rows, fin_width)
-        fluid0, _, first, rest = pl.pallas_call(
+        other_buffer = lambda planes: buffer(planes, rows + 2 * PAD, width)
+        outer_pairs = (0, pairs - 1, 1, 2)
+        fluid0, _, first, rest, sums = pl.pallas_call(
             middle_grp_kernel,
-            out_shape=(fluid_pad, fin_pad, fin_pad, fin_rest),
+            out_shape=(fluid_pad, fin_pad, fin_pad, fin_rest, f32(2, rows, width)),
             in_specs=[vmem] * 8,
-            out_specs=(vmem,) * 4,
+            out_specs=(vmem,) * 5,
+            scratch_shapes=[other_buffer(2)],
             input_output_aliases={0: 0, 1: 1, 2: 2, 3: 3},
             compiler_params=params,
             name="middle_grp",
         )(fluid0, fin0, first, rest, fin_source, grpa, grpb, side)
 
         def middle_gx_kernel(*refs):
-            (act, gxa_in, gxb_in, paira, pairb, own), refs = refs[3:9], refs[9:]
+            (act, sums, gxa_in, gxb_in, paira, pairb, own), refs = refs[3:10], refs[10:]
             wall_refs, refs = refs[: len(walls) - 1], refs[len(walls) - 1 :]
-            fluid, first, rest, ghost_out, zedge, gxa, gxb, zrows, other = refs
+            fluid, first, rest, ghost_out, zedge, gxa, gxb, zrows = refs
             place = my_place()
             grp, gx, _ = place
             on_wall = grp == 0
@@ -531,29 +558,30 @@
             below, above = grp_halos(paira, pairb, grp, groups)
             unpack_fluid(fluid, zrows, zedge, gxa_in, gxb_in, ghost, below, above, 0, place, count,
                          dims)
-            fluid_sweep(fluid, act, zedge, other, 0, dims, (0, pairs - 1, 1, 2))
+            fluid_update(fluid, act, zedge, sums, 0, dims, outer_pairs)
             pack_gx(
                 lambda high: fluid[jnp.where(high, cells, 1), PAD : PAD + rows, :], 0, gx, gxa, gxb,
                 dims,
             )
 
         zrows_buffer, zedge_buffer = buffer(LANES, rows), buffer(rows, LANES)
-        other_buffer = lambda planes: buffer(planes, rows + 2 * PAD, width)
         fluid1, first, rest, ghost, zedge, gxa, gxb = pl.pallas_call(
             middle_gx_kernel,
             out_shape=(fluid_pad, fin_pad, fin_rest, f32(cells, rows),
                        f32(rows, LANES), f32(face_rows, width), f32(face_rows, width)),
-            in_specs=[vmem] * (8 + len(walls)),
+            in_specs=[vmem] * (9 + len(walls)),
             out_specs=(vmem,) * 7,
-            scratch_shapes=[zrows_buffer, other_buffer(2)],
+            scratch_shapes=[zrows_buffer],
             input_output_aliases={0: 0, 1: 1, 2: 2},
             compiler_params=params,
             name="middle_gx",
-        )(fluid0, first, rest, active, gxa, gxb, grpa, grpb, *walls)
+        )(fluid0, first, rest, active, sums, gxa, gxb, grpa, grpb, *walls)
         gxa, gxb = exchange("gx", count, gxa, gxb)
 
-        def middle_rest_kernel(_, act, zedge, first, fluid, grpa, grpb, gyx, other):
-            fluid_sweep(fluid, act, zedge, other, 0, dims, (1, 1, (pairs - 2) // inner_group, inner_group))
+        def middle_rest_kernel(_, act, zedge, first, fluid, grpa, grpb, gyx, others, sums):
+            inner_pairs = (1, 1, (pairs - 2) // inner_group, inner_group)
+            neighbour_sums(fluid, others, sums, 0, dims, inner_pairs)
+            fluid_update(fluid, act, zedge, sums, 0, dims, inner_pairs)
             pack_rest(fluid, first, 1, grpa, grpb, gyx, my_place(), dims)
 
         fluid2, grpa, grpb, gyx = pl.pallas_call(
@@ -561,7 +589,7 @@
             out_shape=(fluid_pad,) + faces,
             in_specs=[vmem] * 4,
             out_specs=(vmem,) * 4,
-            scratch_shapes=[other_buffer(inner_group)],
+            scratch_shapes=[other_buffer(inner_group), buffer(pairs - 2, rows, width)],
             input_output_aliases={0: 0},
             compiler_params=params,
             name="middle_rest",
@@ -569,24 +597,27 @@
         side = swap(gyx)
         grpa, grpb = exchange("grp", groups, grpa, grpb)
 
-        def end_fin_kernel(_0, _1, first, side, rest, fluid):
+        def end_fin_kernel(_0, _1, first, side, rest, fluid, sums, others):
             unpack_lines(fluid, side, lax.axis_index("gy"), dims)
             hedge = side[cells : cells + fin_rows, 0:LANES]
             inner_blocks(lambda k: fin_second(first, rest, hedge, k))
-
-        rest, fluid3 = pl.pallas_call(
+            neighbour_sums(fluid, others, sums, 1, dims, all_pairs)
+
+        all_pairs = (0, 1, pairs // outer_group, outer_group)
+        rest, fluid3, sums = pl.pallas_call(
             end_fin_kernel,
-            out_shape=(fin_rest, fluid_pad),
+            out_shape=(fin_rest, fluid_pad, f32(pairs, rows, width)),
             in_specs=[vmem] * 4,
-            out_specs=(vmem,) * 2,
+            out_specs=(vmem,) * 3,
+            scratch_shapes=[other_buffer(outer_group)],
             input_output_aliases={0: 0, 1: 1},
             compiler_params=params,
             name="end_fin",
         )(rest, fluid2, first, side)
 
-        def end_kernel(_0, _1, _2, act, ghost, gxa, gxb, paira, pairb, side,
+        def end_kernel(_0, _1, _2, act, ghost, gxa, gxb, paira, pairb, side, sums,
                        fluid, first, rest, fluid_new, fin_new,
-                       zrows, zedge, other, fluid_sems, fin_sems):
+                       zrows, zedge, fluid_sems, fin_sems):
             place = my_place()
 
             def fluid_copy(k):
@@ -612,8 +643,8 @@
             fin_copies[0].start()
             below, above = grp_halos(paira, pairb, place[0], groups)
             unpack_fluid(fluid, zrows, zedge, gxa, gxb, ghost, below, above, 1, place, count, dims)
-            fluid_sweep(fluid, act, zedge, other, 1, dims, (0, 1, pairs // outer_group, outer_group),
-                        lambda k: fluid_copy(k).start())
+            fluid_update(fluid, act, zedge, sums, 1, dims, all_pairs,
+                         lambda k: fluid_copy(k).start())
 
             def finish(k, carry):
                 fluid_copy(k).wait()
@@ -627,14 +658,14 @@
             end_kernel,
             out_shape=(fluid_pad, fin_pad, f32(depth, fin_rows, fin_width),
                        f32(cells, rows, width), f32(depth, fin_rows, fin_width)),
-            in_specs=[vmem] * 10,
+            in_specs=[vmem] * 11,
             out_specs=(vmem, vmem, vmem, hbm, hbm),
-            scratch_shapes=[zrows_buffer, zedge_buffer, other_buffer(outer_group),
+            scratch_shapes=[zrows_buffer, zedge_buffer,
                             pltpu.SemaphoreType.DMA((pairs,)), pltpu.SemaphoreType.DMA((1,))],
             input_output_aliases={0: 0, 1: 1, 2: 2},
             compiler_params=params,
             name="end",
-        )(fluid3, first, rest, active, ghost, gxa, gxb, grpa, grpb, side)
+        )(fluid3, first, rest, active, ghost, gxa, gxb, grpa, grpb, side, sums)
         return results[3], results[4]
 
     return jax.shard_map(local, mesh=mesh, in_specs=in_specs, out_specs=out_specs, check_vma=False)

time: 30 us -> 29.3 us (0.977)
  waiting for transfers between devices: 4.28 us -> 3.55 us
    pallas_call x1, Pallas kernels: 1.48 us -> 2.16 us  [local(): pl.pallas_call(end_fin_kernel, out_shape=(fin_rest, fluid_pad, f32(pairs,...]
    ppermute x3, waiting for transfers between devices: 0.85 us -> 0.29 us  [exchange(): paira = lax.ppermute(paira, axes, first)]
    pallas_call x1, Pallas kernels: 3.08 us -> 2.68 us  [local(): pl.pallas_call(end_kernel, out_shape=(fluid_pad, fin_pad, f32(depth, fin_...]
  transfers between devices with their start and end apart: 11 -> 11, of which waited for: 3 -> 2; matrix products, arithmetic and copies ran while one was open for 0% -> 0% of each run, Pallas kernels for 22% -> 25%
where the time goes in v3:
time: 29.3 us; the launch traced here: 29.2 us
  Pallas kernels  13.2 us (45%)
  starting transfers between devices  11.7 us (40%)
  waiting for transfers between devices  3.55 us (12%)
  between operations  0.76 us (3%)
    ppermute x3, starting transfers between devices, exchange(): paira = lax.ppermute(paira, axes, first)  5.76 us
    ppermute x1, waiting for transfers between devices, local(): walls = [wall, lax.ppermute(wall, 'gx', mixed_with(2))]  3.25 us
    ppermute x1, starting transfers between devices, local(): gxa = lax.ppermute(gxa, 'gx', mixed_with(1))  3.03 us
    pallas_call x1, Pallas kernels, local(): pl.pallas_call(end_kernel, out_shape=(fluid_pad, fin_pad, f32(depth, fin_...  2.68 us
    pallas_call x1, Pallas kernels, local(): pl.pallas_call(start_gx_kernel, out_shape=(f32(gx_rows, width), f32(gx_ro...  2.18 us
    pallas_call x1, Pallas kernels, local(): pl.pallas_call(end_fin_kernel, out_shape=(fin_rest, fluid_pad, f32(pairs,...  2.16 us
    pallas_call x1, Pallas kernels, local(): pl.pallas_call(middle_rest_kernel, out_shape=(fluid_pad,) + faces, in_spe...  1.83 us
    pallas_call x1, Pallas kernels, local(): pl.pallas_call(middle_fin_kernel, out_shape=(fin_pad, f32(depth, fin_rows...  1.56 us
  transfers between devices with their start and end apart: 11, of which 2 were waited for; matrix products, arithmetic and copies ran while one was open for 0% of the time, Pallas kernels for 25%

profile of v3, /device:TPU:0, one launch (start us, length us, event | category | flops | bytes accessed | tf_op | source)
XLA Modules:
  0.0 29.2 jit_solution(6059008778260480333)
XLA Ops:
  0.6 0.0 copy-start.2
  0.6 0.0 copy-start.3
  0.7 2.2 %start_gx.1 = (f32[176,256]{1,0:T(8,128)S(1)}, f32[176,256]{1,0:T(8,128)S(1)}, f32[48,256]{1,0:T(8,128)S(1)}) custom-call(f32[16,128,256]{2,1,0:T(8,128)} %fluid_hbm.1, f32[64,32,256]{2,1,0:T(8,128)} %fin_hbm.1, s32[16,128]{1,0:T(8,128)} %bitcast.2, s32[16,128]{1,0:T(8,128)} %bitcast.3), custom_call_target="tpu_custom_call" | custom-call | tf_op jit(solution)/shard_map/start_gx/pallas_call | solution.py:375
  2.8 0.0 copy-start
  2.8 0.0 copy-start.1
  2.9 3.0 %collective-permute-start.3 = (f32[176,256]{1,0:T(8,128)S(1)}, f32[176,256]{1,0:T(8,128)S(1)}, u32[]{:S(2)}, u32[]{:S(2)}) collective-permute-start(f32[176,256]{1,0:T(8,128)S(1)} %get-tuple-element.43), channel_id=1, source_target_pairs={{0,2},{2,0},{4,6},{6,4},{1,3},{3,1},{5,7},{7,5},{8,10},{10,8},{12,... | collective-permute-start | bytes 540680 | tf_op jit(solution)/shard_map/ppermute | solution.py:440
  5.9 1.5 %collective-permute-start.4 = (f32[176,256]{1,0:T(8,128)S(1)}, f32[176,256]{1,0:T(8,128)S(1)}, u32[]{:S(2)}, u32[]{:S(2)}) collective-permute-start(f32[176,256]{1,0:T(8,128)S(1)} %get-tuple-element.44), channel_id=1, source_target_pairs={{0,6},{2,4},{4,2},{6,0},{1,7},{3,5},{5,3},{7,1},{8,14},{10,12},{12... | collective-permute-start | bytes 540680 | tf_op jit(solution)/shard_map/ppermute | solution.py:441
  7.4 0.0 copy-done.2
  7.4 0.0 copy-done.3
  7.4 1.1 %start_rest.1 = (f32[18,144,256]{2,1,0:T(8,128)S(1)}, f32[66,48,256]{2,1,0:T(8,128)S(1)}, f32[48,256]{1,0:T(8,128)S(1)}, f32[48,256]{1,0:T(8,128)S(1)}, f32[48,256]{1,0:T(8,128)S(1)}) custom-call(f32[16,128,256]{2,1,0:T(8,128)S(1)} %copy-done.2, f32[64,32,256]{2,1,0:T(8,128)S(1)} %copy-done.3), custom_call_target="tpu_custom_call" | custom-call | tf_op jit(solution)/shard_map/start_rest/pallas_call | solution.py:405
  8.5 0.1 collective-permute-start
  8.6 1.6 %collective-permute-start.1 = (f32[48,256]{1,0:T(8,128)S(1)}, f32[48,256]{1,0:T(8,128)S(1)}, u32[]{:S(2)}, u32[]{:S(2)}) collective-permute-start(f32[48,256]{1,0:T(8,128)S(1)} %get-tuple-element.37), channel_id=1, source_target_pairs={{0,8},{1,9},{8,0},{9,1},{16,24},{17,25},{24,16},{25,17},{2,10},{3,... | collective-permute-start | bytes 147464 | tf_op jit(solution)/shard_map/ppermute | solution.py:428
  10.2 0.2 collective-permute-start.2
  10.4 0.0 collective-permute-done.side
  10.4 0.5 %collective-permute-start.5 = (f32[48,256]{1,0:T(8,128)S(1)}, f32[48,256]{1,0:T(8,128)S(1)}, u32[]{:S(2)}, u32[]{:S(2)}) collective-permute-start(f32[48,256]{1,0:T(8,128)S(1)} %get-tuple-element.45.refs_9_), channel_id=1, source_target_pairs={{0,4},{2,6},{4,0},{6,2},{1,5},{3,7},{5,1},{7,3},{8,12},{10,14},{12... | collective-permute-start | bytes 147464 | tf_op jit(solution)/shard_map/ppermute | solution.py:439
  10.9 0.0 copy-done
  10.9 0.0 copy-done.1
  10.9 1.6 %middle_fin.1 = (f32[66,48,256]{2,1,0:T(8,128)S(1)}, f32[64,32,256]{2,1,0:T(8,128)S(1)}) custom-call(f32[66,48,256]{2,1,0:T(8,128)S(1)} %get-tuple-element.33.fin._1, f32[64,32,256]{2,1,0:T(8,128)S(1)} %copy-done.1, f32[48,256]{1,0:T(8,128)S(1)} %collective-permute-done.side, s32[16,128,256]{2,1,0:T(8,128)S(1)} %copy-done), custom_call_target="tpu_custom_call" | custom-call | tf_op jit(solution)/shard_map/middle_fin/pallas_call | solution.py:481
  12.4 0.3 collective-permute-done.1.paira.refs_7_
  12.7 0.0 collective-permute-done.2.pairb.refs_8_
  12.7 0.6 %middle_grp.1 = (f32[18,144,256]{2,1,0:T(8,128)S(1)}, f32[66,48,256]{2,1,0:T(8,128)S(1)}, f32[66,48,256]{2,1,0:T(8,128)S(1)}, f32[64,32,256]{2,1,0:T(8,128)S(1)}, f32[2,128,256]{2,1,0:T(8,128)S(1)}) custom-call(f32[18,144,256]{2,1,0:T(8,128)S(1)} %get-tuple-element.32._0, ...), custom_call_target="tpu_custom_call", output_to_operand_aliasing={{0}: (0, {}), {1}: (1, {}), {2}: (2, {}), {3}: (3, {})} | custom-call | tf_op jit(solution)/shard_map/middle_grp/pallas_call | solution.py:502
  13.3 3.2 %collective-permute-done.5.refs_10_ = f32[48,256]{1,0:T(8,128)S(1)} collective-permute-done((f32[48,256]{1,0:T(8,128)S(1)}, f32[48,256]{1,0:T(8,128)S(1)}, u32[]{:S(2)}, u32[]{:S(2)}) %collective-permute-start.5) | collective-permute-done | bytes 49184 | tf_op jit(solution)/shard_map/ppermute | solution.py:439
  16.6 0.0 collective-permute-done.3.refs_5_
  16.6 0.0 collective-permute-done.4.refs_6_
  16.6 1.1 %middle_gx.1 = (f32[18,144,256]{2,1,0:T(8,128)S(1)}, f32[66,48,256]{2,1,0:T(8,128)S(1)}, f32[64,32,256]{2,1,0:T(8,128)S(1)}, f32[16,128]{1,0:T(8,128)S(1)}, f32[...) custom-call(f32[18,144,256]{2,1,0:T(8,128)S(1)} %get-tuple-element.3, ...), custom_call_target="tpu_custom_call", output_to_operand_aliasing={{0}: (0, {}), {1}: (1, {}), {2}: (2, {})} | custom-call | tf_op jit(solution)/shard_map/middle_gx/pallas_call | solution.py:568
  17.7 1.5 %collective-permute-start.7 = (f32[128,256]{1,0:T(8,128)S(1)}, f32[128,256]{1,0:T(8,128)S(1)}, u32[]{:S(2)}, u32[]{:S(2)}) collective-permute-start(f32[128,256]{1,0:T(8,128)S(1)} %get-tuple-element.55), channel_id=1, source_target_pairs={{0,2},{1,3},{2,0},{3,1},{4,6},{5,7},{6,4},{7,5},{8,10},{9,11},{10,... | collective-permute-start | bytes 393224 | tf_op jit(solution)/shard_map/ppermute | solution.py:428
  19.2 0.0 collective-permute-start.8
  19.2 1.8 %middle_rest.1 = (f32[18,144,256]{2,1,0:T(8,128)S(1)}, f32[48,256]{1,0:T(8,128)S(1)}, f32[48,256]{1,0:T(8,128)S(1)}, f32[48,256]{1,0:T(8,128)S(1)}) custom-call(f32[18,144,256]{2,1,0:T(8,128)S(1)} %get-tuple-element.47._, s32[16,128,256]{2,1,0:T(8,128)S(1)} %copy-done, f32[128,128]{1,0:T(8,128)S(1)} %get-tuple-element.48.zedge, ...), custom_call_target="tpu_custom_call", output_to_operand_aliasing={{0}: (0, {})} | custom-call | tf_op jit(solution)/shard_map/middle_rest/pallas_call | solution.py:587
  21.1 0.6 %collective-permute-start.6 = (f32[48,256]{1,0:T(8,128)S(1)}, f32[48,256]{1,0:T(8,128)S(1)}, u32[]{:S(2)}, u32[]{:S(2)}) collective-permute-start(f32[48,256]{1,0:T(8,128)S(1)} %get-tuple-element.51), channel_id=1, source_target_pairs={{0,1},{1,0},{2,3},{3,2},{4,5},{5,4},{6,7},{7,6},{8,9},{9,8},{10,11... | collective-permute-start | bytes 147464 | tf_op jit(solution)/shard_map/ppermute | solution.py:433
  21.7 0.1 collective-permute-start.10
  21.7 2.6 %collective-permute-start.9 = (f32[48,256]{1,0:T(8,128)S(1)}, f32[48,256]{1,0:T(8,128)S(1)}, u32[]{:S(2)}, u32[]{:S(2)}) collective-permute-start(f32[48,256]{1,0:T(8,128)S(1)} %get-tuple-element.57), channel_id=1, source_target_pairs={{0,8},{1,9},{8,0},{9,1},{16,24},{17,25},{24,16},{25,17},{2,10},{3,... | collective-permute-start | bytes 147464 | tf_op jit(solution)/shard_map/ppermute | solution.py:428
  24.3 0.0 collective-permute-done.6.side
  24.3 2.2 %end_fin.1 = (f32[64,32,256]{2,1,0:T(8,128)S(1)}, f32[18,144,256]{2,1,0:T(8,128)S(1)}, f32[8,128,256]{2,1,0:T(8,128)S(1)}) custom-call(f32[64,32,256]{2,1,0:T(8,128)S(1)} %get-tuple-element.46._0, f32[18,144,256]{2,1,0:T(8,128)S(1)} %get-tuple-element.50._1, ...), custom_call_target="tpu_custom_call", output_to_operand_aliasing={{0}: (0, {}), {1}: (1, {})} | custom-call | tf_op jit(solution)/shard_map/end_fin/pallas_call | solution.py:607
  26.5 0.0 collective-permute-done.10.pairb
  26.5 0.0 collective-permute-done.9.paira
  26.5 0.0 collective-permute-done.7.gxa
  26.5 0.0 collective-permute-done.8.gxb
  26.5 2.7 %end.1 = (f32[18,144,256]{2,1,0:T(8,128)S(1)}, f32[66,48,256]{2,1,0:T(8,128)S(1)}, f32[64,32,256]{2,1,0:T(8,128)S(1)}, f32[16,128,256]{2,1,0:T(8,128)}, f32[64,32,256]{2,1,0:T(8,128)}) custom-call(f32[18,144,256]{2,1,0:T(8,128)S(1)} %get-tuple-element.52._0, ...), custom_call_target="tpu_custom_call", output_to_operand_aliasing={{0}: (0, {}), {1}: (1, {}), {2}: (2, {})} | custom-call | tf_op jit(solution)/shard_map/end/pallas_call | solution.py:657
Async XLA Ops:
  0.6 6.8 %copy-start.2 = (f32[16,128,256]{2,1,0:T(8,128)S(1)}, f32[16,128,256]{2,1,0:T(8,128)}, u32[]{:S(2)}) copy-start(f32[16,128,256]{2,1,0:T(8,128)} %fluid_hbm.1) | copy-start | bytes 6291460
  0.6 6.8 %copy-start.3 = (f32[64,32,256]{2,1,0:T(8,128)S(1)}, f32[64,32,256]{2,1,0:T(8,128)}, u32[]{:S(2)}) copy-start(f32[64,32,256]{2,1,0:T(8,128)} %fin_hbm.1) | copy-start | bytes 6291460
  2.8 8.0 %copy-start = (s32[16,128,256]{2,1,0:T(8,128)S(1)}, s32[16,128,256]{2,1,0:T(8,128)}, u32[]{:S(2)}) copy-start(s32[16,128,256]{2,1,0:T(8,128)} %act.3) | copy-start | bytes 6291460
  2.8 8.0 %copy-start.1 = (f32[64,32,256]{2,1,0:T(8,128)S(1)}, f32[64,32,256]{2,1,0:T(8,128)}, u32[]{:S(2)}) copy-start(f32[64,32,256]{2,1,0:T(8,128)} %src.3) | copy-start | bytes 6291460
  2.9 13.7 %collective-permute-start.3 = (f32[176,256]{1,0:T(8,128)S(1)}, f32[176,256]{1,0:T(8,128)S(1)}, u32[]{:S(2)}, u32[]{:S(2)}) collective-permute-start(f32[176,256]{1,0:T(8,128)S(1)} %get-tuple-element.43), channel_id=1, source_target_pairs={{0,2},{2,0},{4,6},{6,4},{1,3},{3,1},{5,7},{7,5},{8,10},{10,8},{12,... | collective-permute-start | bytes 540680 | tf_op jit(solution)/shard_map/ppermute | solution.py:440
  5.9 10.7 %collective-permute-start.4 = (f32[176,256]{1,0:T(8,128)S(1)}, f32[176,256]{1,0:T(8,128)S(1)}, u32[]{:S(2)}, u32[]{:S(2)}) collective-permute-start(f32[176,256]{1,0:T(8,128)S(1)} %get-tuple-element.44), channel_id=1, source_target_pairs={{0,6},{2,4},{4,2},{6,0},{1,7},{3,5},{5,3},{7,1},{8,14},{10,12},{12... | collective-permute-start | bytes 540680 | tf_op jit(solution)/shard_map/ppermute | solution.py:441
  8.5 1.9 %collective-permute-start = (f32[48,256]{1,0:T(8,128)S(1)}, f32[48,256]{1,0:T(8,128)S(1)}, u32[]{:S(2)}, u32[]{:S(2)}) collective-permute-start(f32[48,256]{1,0:T(8,128)S(1)} %get-tuple-element.34), channel_id=1, source_target_pairs={{0,1},{1,0},{2,3},{3,2},{4,5},{5,4},{6,7},{7,6},{8,9},{9,8},{10,11... | collective-permute-start | bytes 147464 | tf_op jit(solution)/shard_map/ppermute | solution.py:433
  8.6 4.2 %collective-permute-start.1 = (f32[48,256]{1,0:T(8,128)S(1)}, f32[48,256]{1,0:T(8,128)S(1)}, u32[]{:S(2)}, u32[]{:S(2)}) collective-permute-start(f32[48,256]{1,0:T(8,128)S(1)} %get-tuple-element.37), channel_id=1, source_target_pairs={{0,8},{1,9},{8,0},{9,1},{16,24},{17,25},{24,16},{25,17},{2,10},{3,... | collective-permute-start | bytes 147464 | tf_op jit(solution)/shard_map/ppermute | solution.py:428
  10.2 2.5 %collective-permute-start.2 = (f32[48,256]{1,0:T(8,128)S(1)}, f32[48,256]{1,0:T(8,128)S(1)}, u32[]{:S(2)}, u32[]{:S(2)}) collective-permute-start(f32[48,256]{1,0:T(8,128)S(1)} %get-tuple-element.38), channel_id=1, source_target_pairs={{0,1},{1,0},{8,16},{9,17},{16,8},{17,9},{24,25},{25,24},{2,3},{3,2... | collective-permute-start | bytes 147464 | tf_op jit(solution)/shard_map/ppermute | solution.py:429
  10.4 6.2 %collective-permute-start.5 = (f32[48,256]{1,0:T(8,128)S(1)}, f32[48,256]{1,0:T(8,128)S(1)}, u32[]{:S(2)}, u32[]{:S(2)}) collective-permute-start(f32[48,256]{1,0:T(8,128)S(1)} %get-tuple-element.45.refs_9_), channel_id=1, source_target_pairs={{0,4},{2,6},{4,0},{6,2},{1,5},{3,7},{5,1},{7,3},{8,12},{10,14},{12... | collective-permute-start | bytes 147464 | tf_op jit(solution)/shard_map/ppermute | solution.py:439
  17.7 8.8 %collective-permute-start.7 = (f32[128,256]{1,0:T(8,128)S(1)}, f32[128,256]{1,0:T(8,128)S(1)}, u32[]{:S(2)}, u32[]{:S(2)}) collective-permute-start(f32[128,256]{1,0:T(8,128)S(1)} %get-tuple-element.55), channel_id=1, source_target_pairs={{0,2},{1,3},{2,0},{3,1},{4,6},{5,7},{6,4},{7,5},{8,10},{9,11},{10,... | collective-permute-start | bytes 393224 | tf_op jit(solution)/shard_map/ppermute | solution.py:428
  19.2 7.3 %collective-permute-start.8 = (f32[128,256]{1,0:T(8,128)S(1)}, f32[128,256]{1,0:T(8,128)S(1)}, u32[]{:S(2)}, u32[]{:S(2)}) collective-permute-start(f32[128,256]{1,0:T(8,128)S(1)} %get-tuple-element.56), channel_id=1, source_target_pairs={{0,1},{1,0},{2,4},{3,5},{4,2},{5,3},{6,7},{7,6},{8,9},{9,8},{10,12... | collective-permute-start | bytes 393224 | tf_op jit(solution)/shard_map/ppermute | solution.py:429
  21.1 3.2 %collective-permute-start.6 = (f32[48,256]{1,0:T(8,128)S(1)}, f32[48,256]{1,0:T(8,128)S(1)}, u32[]{:S(2)}, u32[]{:S(2)}) collective-permute-start(f32[48,256]{1,0:T(8,128)S(1)} %get-tuple-element.51), channel_id=1, source_target_pairs={{0,1},{1,0},{2,3},{3,2},{4,5},{5,4},{6,7},{7,6},{8,9},{9,8},{10,11... | collective-permute-start | bytes 147464 | tf_op jit(solution)/shard_map/ppermute | solution.py:433
  21.7 4.8 %collective-permute-start.10 = (f32[48,256]{1,0:T(8,128)S(1)}, f32[48,256]{1,0:T(8,128)S(1)}, u32[]{:S(2)}, u32[]{:S(2)}) collective-permute-start(f32[48,256]{1,0:T(8,128)S(1)} %get-tuple-element.58), channel_id=1, source_target_pairs={{0,1},{1,0},{8,16},{9,17},{16,8},{17,9},{24,25},{25,24},{2,3},{3,2... | collective-permute-start | bytes 147464 | tf_op jit(solution)/shard_map/ppermute | solution.py:429
  21.7 4.8 %collective-permute-start.9 = (f32[48,256]{1,0:T(8,128)S(1)}, f32[48,256]{1,0:T(8,128)S(1)}, u32[]{:S(2)}, u32[]{:S(2)}) collective-permute-start(f32[48,256]{1,0:T(8,128)S(1)} %get-tuple-element.57), channel_id=1, source_target_pairs={{0,8},{1,9},{8,0},{9,1},{16,24},{17,25},{24,16},{25,17},{2,10},{3,... | collective-permute-start | bytes 147464 | tf_op jit(solution)/shard_map/ppermute | solution.py:428

commit v4 on v3

--- a/solution.py
+++ b/solution.py
@@ -199,11 +199,11 @@
             )
 
     def trip(j, carry):
-        ns = [group * j + u for u in range(group)]
-        for u, n in enumerate(ns):
-            merge(first_pair + step * n, others.at[u])
-        for u, n in enumerate(ns):
-            add(others.at[u], sums.at[n])
+        ks = [first_pair + step * (group * j + u) for u in range(group)]
+        for u, k in enumerate(ks):
+            merge(k, others.at[u])
+        for u, k in enumerate(ks):
+            add(others.at[u], sums.at[k])
         return carry
 
     lax.fori_loop(0, trips, trip, 0)
@@ -237,10 +237,10 @@
 
     def trip(j, carry):
         for u in range(group):
-            n = group * j + u
-            update(first_pair + step * n, sums.at[n])
+            k = first_pair + step * (group * j + u)
+            update(k, sums.at[k])
             if done is not None:
-                done(first_pair + step * n)
+                done(k)
         return carry
 
     lax.fori_loop(0, trips, trip, 0)
@@ -494,17 +494,19 @@
             for block in (0, blocks - 1):
                 fin_first(fin, src, first, rest, hedge, block)
             unpack_lines(fluid, side, lax.axis_index("gy"), dims)
-            neighbour_sums(fluid, others, sums, 0, dims, outer_pairs)
+            neighbour_sums(fluid, others, sums, 0, dims, all_pairs)
 
         fin_rest = f32(depth, fin_rows, fin_width)
         other_buffer = lambda planes: buffer(planes, rows + 2 * PAD, width)
         outer_pairs = (0, pairs - 1, 1, 2)
+        all_pairs = (0, 1, pairs // outer_group, outer_group)
+        inner_pairs = (1, 1, (pairs - 2) // inner_group, inner_group)
         fluid0, _, first, rest, sums = pl.pallas_call(
             middle_grp_kernel,
-            out_shape=(fluid_pad, fin_pad, fin_pad, fin_rest, f32(2, rows, width)),
+            out_shape=(fluid_pad, fin_pad, fin_pad, fin_rest, f32(pairs, rows, width)),
             in_specs=[vmem] * 8,
             out_specs=(vmem,) * 5,
-            scratch_shapes=[other_buffer(2)],
+            scratch_shapes=[other_buffer(outer_group)],
             input_output_aliases={0: 0, 1: 1, 2: 2, 3: 3},
             compiler_params=params,
             name="middle_grp",
@@ -578,44 +580,47 @@
         )(fluid0, first, rest, active, sums, gxa, gxb, grpa, grpb, *walls)
         gxa, gxb = exchange("gx", count, gxa, gxb)
 
-        def middle_rest_kernel(_, act, zedge, first, fluid, grpa, grpb, gyx, others, sums):
-            inner_pairs = (1, 1, (pairs - 2) // inner_group, inner_group)
-            neighbour_sums(fluid, others, sums, 0, dims, inner_pairs)
+        def middle_rest_kernel(_, act, zedge, first, sums, fluid, grpa, grpb, gyx):
             fluid_update(fluid, act, zedge, sums, 0, dims, inner_pairs)
             pack_rest(fluid, first, 1, grpa, grpb, gyx, my_place(), dims)
 
         fluid2, grpa, grpb, gyx = pl.pallas_call(
             middle_rest_kernel,
             out_shape=(fluid_pad,) + faces,
-            in_specs=[vmem] * 4,
+            in_specs=[vmem] * 5,
             out_specs=(vmem,) * 4,
-            scratch_shapes=[other_buffer(inner_group), buffer(pairs - 2, rows, width)],
             input_output_aliases={0: 0},
             compiler_params=params,
             name="middle_rest",
-        )(fluid1, active, zedge, first)
+        )(fluid1, active, zedge, first, sums)
         side = swap(gyx)
         grpa, grpb = exchange("grp", groups, grpa, grpb)
 
-        def end_fin_kernel(_0, _1, first, side, rest, fluid, sums, others):
+        def end_fin_kernel(_0, _1, first, side, rest, fluid, sums, fin_new, others, sem):
             unpack_lines(fluid, side, lax.axis_index("gy"), dims)
             hedge = side[cells : cells + fin_rows, 0:LANES]
             inner_blocks(lambda k: fin_second(first, rest, hedge, k))
+            copy = fin_copy(rest, fin_new, sem.at[0], inner_depths, inner_rows)
+            copy.start()
             neighbour_sums(fluid, others, sums, 1, dims, all_pairs)
-
-        all_pairs = (0, 1, pairs // outer_group, outer_group)
-        rest, fluid3, sums = pl.pallas_call(
+            copy.wait()
+
+        def fin_copy(rest, fin_new, sem, depths, lines):
+            return pltpu.make_async_copy(rest.at[depths, lines], fin_new.at[depths, lines], sem)
+
+        inner_depths, inner_rows = pl.ds(8, depth - 16), pl.ds(PAD, fin_rows - 2 * PAD)
+        rest, fluid3, sums, fin_new = pl.pallas_call(
             end_fin_kernel,
-            out_shape=(fin_rest, fluid_pad, f32(pairs, rows, width)),
+            out_shape=(fin_rest, fluid_pad, f32(pairs, rows, width), fin_rest),
             in_specs=[vmem] * 4,
-            out_specs=(vmem,) * 3,
-            scratch_shapes=[other_buffer(outer_group)],
+            out_specs=(vmem, vmem, vmem, hbm),
+            scratch_shapes=[other_buffer(outer_group), pltpu.SemaphoreType.DMA((1,))],
             input_output_aliases={0: 0, 1: 1},
             compiler_params=params,
             name="end_fin",
         )(rest, fluid2, first, side)
 
-        def end_kernel(_0, _1, _2, act, ghost, gxa, gxb, paira, pairb, side, sums,
+        def end_kernel(_0, _1, _2, _3, act, ghost, gxa, gxb, paira, pairb, side, sums,
                        fluid, first, rest, fluid_new, fin_new,
                        zrows, zedge, fluid_sems, fin_sems):
             place = my_place()
@@ -626,21 +631,24 @@
                     fluid_new.at[pl.ds(2 * k, 2)], fluid_sems.at[k],
                 )
 
-            def fin_copy(k, start, size):
-                part = pl.ds(start, size)
-                return pltpu.make_async_copy(rest.at[part], fin_new.at[part], fin_sems.at[k])
-
-            fin_depth_halos(first, paira, pairb)
-            hedge = side[cells : cells + fin_rows, 0:LANES]
-            for block in (0, blocks - 1):
-                fin_second(first, rest, hedge, block)
             even, inside = sides_of(place[1], count)
             row_a = jnp.where(even, fin_rows - 1, 0)
             row_b = fin_rows - 1 - row_a
             scale = OMEGA * FIN_CONDUCTION / DIAG
             add_gx_rows(rest, 0, (row_a, row_b), (gxa, gxb), half, (scale, scale * inside), depth)
-            fin_copies = [fin_copy(0, 0, depth)]
-            fin_copies[0].start()
+            whole = pl.ds(0, fin_rows)
+            parts = ((inner_depths, pl.ds(0, PAD)), (inner_depths, pl.ds(fin_rows - PAD, PAD)),
+                     (pl.ds(0, 8), whole), (pl.ds(depth - 8, 8), whole))
+            fin_copies = [
+                fin_copy(rest, fin_new, fin_sems.at[k], *part) for k, part in enumerate(parts)
+            ]
+            for item in fin_copies[:2]:
+                item.start()
+            fin_depth_halos(first, paira, pairb)
+            hedge = side[cells : cells + fin_rows, 0:LANES]
+            for block, item in ((0, fin_copies[2]), (blocks - 1, fin_copies[3])):
+                fin_second(first, rest, hedge, block)
+                item.start()
             below, above = grp_halos(paira, pairb, place[0], groups)
             unpack_fluid(fluid, zrows, zedge, gxa, gxb, ghost, below, above, 1, place, count, dims)
             fluid_update(fluid, act, zedge, sums, 1, dims, all_pairs,
@@ -658,14 +666,14 @@
             end_kernel,
             out_shape=(fluid_pad, fin_pad, f32(depth, fin_rows, fin_width),
                        f32(cells, rows, width), f32(depth, fin_rows, fin_width)),
-            in_specs=[vmem] * 11,
+            in_specs=[vmem] * 3 + [hbm] + [vmem] * 8,
             out_specs=(vmem, vmem, vmem, hbm, hbm),
             scratch_shapes=[zrows_buffer, zedge_buffer,
-                            pltpu.SemaphoreType.DMA((pairs,)), pltpu.SemaphoreType.DMA((1,))],
-            input_output_aliases={0: 0, 1: 1, 2: 2},
+                            pltpu.SemaphoreType.DMA((pairs,)), pltpu.SemaphoreType.DMA((4,))],
+            input_output_aliases={0: 0, 1: 1, 2: 2, 3: 4},
             compiler_params=params,
             name="end",
-        )(fluid3, first, rest, active, ghost, gxa, gxb, grpa, grpb, side, sums)
+        )(fluid3, first, rest, fin_new, active, ghost, gxa, gxb, grpa, grpb, side, sums)
         return results[3], results[4]
 
     return jax.shard_map(local, mesh=mesh, in_specs=in_specs, out_specs=out_specs, check_vma=False)

time: 29.3 us -> 28.5 us (0.973)
  waiting for transfers between devices: 3.55 us -> 3.03 us
  Pallas kernels: 13.2 us -> 12.9 us
    pallas_call x1, Pallas kernels: 1.83 us -> 1.26 us  [local(): pl.pallas_call(middle_rest_kernel, out_shape=(fluid_pad,) + faces, in_spe...]
    pallas_call x1, Pallas kernels: 0.59 us -> 1.11 us  [local(): pl.pallas_call(middle_grp_kernel, out_shape=(fluid_pad, fin_pad, fin_pad,...]
    ppermute x1, waiting for transfers between devices: 3.25 us -> 2.72 us  [local(): walls = [wall, lax.ppermute(wall, 'gx', mixed_with(2))]]
    pallas_call x1, Pallas kernels: 2.68 us -> 2.24 us  [local(): pl.pallas_call(end_kernel, out_shape=(fluid_pad, fin_pad, f32(depth, fin_...]
  transfers between devices with their start and end apart: 11 -> 11, of which waited for: 2 -> 2; matrix products, arithmetic and copies ran while one was open for 0% -> 0% of each run, Pallas kernels for 25% -> 26%
where the time goes in v4:
time: 28.5 us; the launch traced here: 28.4 us
  Pallas kernels  12.9 us (45%)
  starting transfers between devices  11.7 us (41%)
  waiting for transfers between devices  3.03 us (11%)
  between operations  0.76 us (3%)
    ppermute x3, starting transfers between devices, exchange(): paira = lax.ppermute(paira, axes, first)  5.76 us
    ppermute x1, starting transfers between devices, local(): gxa = lax.ppermute(gxa, 'gx', mixed_with(1))  3.03 us
    ppermute x1, waiting for transfers between devices, local(): walls = [wall, lax.ppermute(wall, 'gx', mixed_with(2))]  2.72 us
    pallas_call x1, Pallas kernels, local(): pl.pallas_call(end_fin_kernel, out_shape=(fin_rest, fluid_pad, f32(pairs,...  2.35 us
    pallas_call x1, Pallas kernels, local(): pl.pallas_call(end_kernel, out_shape=(fluid_pad, fin_pad, f32(depth, fin_...  2.24 us
    pallas_call x1, Pallas kernels, local(): pl.pallas_call(start_gx_kernel, out_shape=(f32(gx_rows, width), f32(gx_ro...  2.18 us
    pallas_call x1, Pallas kernels, local(): pl.pallas_call(middle_fin_kernel, out_shape=(fin_pad, f32(depth, fin_rows...  1.56 us
    ppermute x1, starting transfers between devices, local(): gxb = lax.ppermute(gxb, 'gx', mixed_with(3))  1.49 us
  transfers between devices with their start and end apart: 11, of which 2 were waited for; matrix products, arithmetic and copies ran while one was open for 0% of the time, Pallas kernels for 26%

profile of v4, /device:TPU:0, one launch (start us, length us, event | category | flops | bytes accessed | tf_op | source)
XLA Modules:
  0.0 28.4 jit_solution(15006101049974327932)
XLA Ops:
  0.6 0.0 copy-start.2
  0.6 0.0 copy-start.3
  0.7 2.2 %start_gx.1 = (f32[176,256]{1,0:T(8,128)S(1)}, f32[176,256]{1,0:T(8,128)S(1)}, f32[48,256]{1,0:T(8,128)S(1)}) custom-call(f32[16,128,256]{2,1,0:T(8,128)} %fluid_hbm.1, f32[64,32,256]{2,1,0:T(8,128)} %fin_hbm.1, s32[16,128]{1,0:T(8,128)} %bitcast.2, s32[16,128]{1,0:T(8,128)} %bitcast.3), custom_call_target="tpu_custom_call" | custom-call | tf_op jit(solution)/shard_map/start_gx/pallas_call | solution.py:375
  2.8 0.0 copy-start
  2.8 0.0 copy-start.1
  2.9 3.0 %collective-permute-start.3 = (f32[176,256]{1,0:T(8,128)S(1)}, f32[176,256]{1,0:T(8,128)S(1)}, u32[]{:S(2)}, u32[]{:S(2)}) collective-permute-start(f32[176,256]{1,0:T(8,128)S(1)} %get-tuple-element.44), channel_id=1, source_target_pairs={{0,2},{2,0},{4,6},{6,4},{1,3},{3,1},{5,7},{7,5},{8,10},{10,8},{12,... | collective-permute-start | bytes 540680 | tf_op jit(solution)/shard_map/ppermute | solution.py:440
  5.9 1.5 %collective-permute-start.4 = (f32[176,256]{1,0:T(8,128)S(1)}, f32[176,256]{1,0:T(8,128)S(1)}, u32[]{:S(2)}, u32[]{:S(2)}) collective-permute-start(f32[176,256]{1,0:T(8,128)S(1)} %get-tuple-element.45), channel_id=1, source_target_pairs={{0,6},{2,4},{4,2},{6,0},{1,7},{3,5},{5,3},{7,1},{8,14},{10,12},{12... | collective-permute-start | bytes 540680 | tf_op jit(solution)/shard_map/ppermute | solution.py:441
  7.4 0.0 copy-done.2
  7.4 0.0 copy-done.3
  7.4 1.1 %start_rest.1 = (f32[18,144,256]{2,1,0:T(8,128)S(1)}, f32[66,48,256]{2,1,0:T(8,128)S(1)}, f32[48,256]{1,0:T(8,128)S(1)}, f32[48,256]{1,0:T(8,128)S(1)}, f32[48,256]{1,0:T(8,128)S(1)}) custom-call(f32[16,128,256]{2,1,0:T(8,128)S(1)} %copy-done.2, f32[64,32,256]{2,1,0:T(8,128)S(1)} %copy-done.3), custom_call_target="tpu_custom_call" | custom-call | tf_op jit(solution)/shard_map/start_rest/pallas_call | solution.py:405
  8.5 0.1 collective-permute-start
  8.6 1.6 %collective-permute-start.1 = (f32[48,256]{1,0:T(8,128)S(1)}, f32[48,256]{1,0:T(8,128)S(1)}, u32[]{:S(2)}, u32[]{:S(2)}) collective-permute-start(f32[48,256]{1,0:T(8,128)S(1)} %get-tuple-element.38), channel_id=1, source_target_pairs={{0,8},{1,9},{8,0},{9,1},{16,24},{17,25},{24,16},{25,17},{2,10},{3,... | collective-permute-start | bytes 147464 | tf_op jit(solution)/shard_map/ppermute | solution.py:428
  10.2 0.2 collective-permute-start.2
  10.4 0.0 collective-permute-done.side
  10.4 0.5 %collective-permute-start.5 = (f32[48,256]{1,0:T(8,128)S(1)}, f32[48,256]{1,0:T(8,128)S(1)}, u32[]{:S(2)}, u32[]{:S(2)}) collective-permute-start(f32[48,256]{1,0:T(8,128)S(1)} %get-tuple-element.46.refs_9_), channel_id=1, source_target_pairs={{0,4},{2,6},{4,0},{6,2},{1,5},{3,7},{5,1},{7,3},{8,12},{10,14},{12... | collective-permute-start | bytes 147464 | tf_op jit(solution)/shard_map/ppermute | solution.py:439
  10.9 0.0 copy-done
  10.9 0.0 copy-done.1
  10.9 1.6 %middle_fin.1 = (f32[66,48,256]{2,1,0:T(8,128)S(1)}, f32[64,32,256]{2,1,0:T(8,128)S(1)}) custom-call(f32[66,48,256]{2,1,0:T(8,128)S(1)} %get-tuple-element.34.fin._1, f32[64,32,256]{2,1,0:T(8,128)S(1)} %copy-done.1, f32[48,256]{1,0:T(8,128)S(1)} %collective-permute-done.side, s32[16,128,256]{2,1,0:T(8,128)S(1)} %copy-done), custom_call_target="tpu_custom_call" | custom-call | tf_op jit(solution)/shard_map/middle_fin/pallas_call | solution.py:481
  12.4 0.3 collective-permute-done.1.paira.refs_7_
  12.7 0.0 collective-permute-done.2.pairb.refs_8_
  12.7 1.1 %middle_grp.1 = (f32[18,144,256]{2,1,0:T(8,128)S(1)}, f32[66,48,256]{2,1,0:T(8,128)S(1)}, f32[66,48,256]{2,1,0:T(8,128)S(1)}, f32[64,32,256]{2,1,0:T(8,128)S(1)}, f32[8,128,256]{2,1,0:T(8,128)S(1)}) custom-call(f32[18,144,256]{2,1,0:T(8,128)S(1)} %get-tuple-element.33._0, ...), custom_call_target="tpu_custom_call", output_to_operand_aliasing={{0}: (0, {}), {1}: (1, {}), {2}: (2, {}), {3}: (3, {})} | custom-call | tf_op jit(solution)/shard_map/middle_grp/pallas_call | solution.py:504
  13.8 2.7 %collective-permute-done.5.refs_10_ = f32[48,256]{1,0:T(8,128)S(1)} collective-permute-done((f32[48,256]{1,0:T(8,128)S(1)}, f32[48,256]{1,0:T(8,128)S(1)}, u32[]{:S(2)}, u32[]{:S(2)}) %collective-permute-start.5) | collective-permute-done | bytes 49184 | tf_op jit(solution)/shard_map/ppermute | solution.py:439
  16.6 0.0 collective-permute-done.3.refs_5_
  16.6 0.0 collective-permute-done.4.refs_6_
  16.6 1.1 %middle_gx.1 = (f32[18,144,256]{2,1,0:T(8,128)S(1)}, f32[66,48,256]{2,1,0:T(8,128)S(1)}, f32[64,32,256]{2,1,0:T(8,128)S(1)}, f32[16,128]{1,0:T(8,128)S(1)}, f32[...) custom-call(f32[18,144,256]{2,1,0:T(8,128)S(1)} %get-tuple-element.4, ...), custom_call_target="tpu_custom_call", output_to_operand_aliasing={{0}: (0, {}), {1}: (1, {}), {2}: (2, {})} | custom-call | tf_op jit(solution)/shard_map/middle_gx/pallas_call | solution.py:570
  17.7 1.5 %collective-permute-start.7 = (f32[128,256]{1,0:T(8,128)S(1)}, f32[128,256]{1,0:T(8,128)S(1)}, u32[]{:S(2)}, u32[]{:S(2)}) collective-permute-start(f32[128,256]{1,0:T(8,128)S(1)} %get-tuple-element.57), channel_id=1, source_target_pairs={{0,2},{1,3},{2,0},{3,1},{4,6},{5,7},{6,4},{7,5},{8,10},{9,11},{10,... | collective-permute-start | bytes 393224 | tf_op jit(solution)/shard_map/ppermute | solution.py:428
  19.2 0.0 collective-permute-start.8
  19.2 1.3 %middle_rest.1 = (f32[18,144,256]{2,1,0:T(8,128)S(1)}, f32[48,256]{1,0:T(8,128)S(1)}, f32[48,256]{1,0:T(8,128)S(1)}, f32[48,256]{1,0:T(8,128)S(1)}) custom-call(f32[18,144,256]{2,1,0:T(8,128)S(1)} %get-tuple-element.48._, s32[16,128,256]{2,1,0:T(8,128)S(1)} %copy-done, f32[128,128]{1,0:T(8,128)S(1)} %get-tuple-element.49.zedge, ...), custom_call_target="tpu_custom_call", output_to_operand_aliasing={{0}: (0, {})} | custom-call | tf_op jit(solution)/shard_map/middle_rest/pallas_call | solution.py:587
  20.5 0.6 %collective-permute-start.6 = (f32[48,256]{1,0:T(8,128)S(1)}, f32[48,256]{1,0:T(8,128)S(1)}, u32[]{:S(2)}, u32[]{:S(2)}) collective-permute-start(f32[48,256]{1,0:T(8,128)S(1)} %get-tuple-element.52), channel_id=1, source_target_pairs={{0,1},{1,0},{2,3},{3,2},{4,5},{5,4},{6,7},{7,6},{8,9},{9,8},{10,11... | collective-permute-start | bytes 147464 | tf_op jit(solution)/shard_map/ppermute | solution.py:433
  21.1 0.1 collective-permute-start.10
  21.2 2.6 %collective-permute-start.9 = (f32[48,256]{1,0:T(8,128)S(1)}, f32[48,256]{1,0:T(8,128)S(1)}, u32[]{:S(2)}, u32[]{:S(2)}) collective-permute-start(f32[48,256]{1,0:T(8,128)S(1)} %get-tuple-element.59), channel_id=1, source_target_pairs={{0,8},{1,9},{8,0},{9,1},{16,24},{17,25},{24,16},{25,17},{2,10},{3,... | collective-permute-start | bytes 147464 | tf_op jit(solution)/shard_map/ppermute | solution.py:428
  23.7 0.0 collective-permute-done.6.side
  23.7 2.4 %end_fin.1 = (f32[64,32,256]{2,1,0:T(8,128)S(1)}, f32[18,144,256]{2,1,0:T(8,128)S(1)}, f32[8,128,256]{2,1,0:T(8,128)S(1)}, f32[64,32,256]{2,1,0:T(8,128)}) custom-call(f32[64,32,256]{2,1,0:T(8,128)S(1)} %get-tuple-element.47._0, f32[18,144,256]{2,1,0:T(8,128)S(1)} %get-tuple-element.51._1, ...), custom_call_target="tpu_custom_call", output_to_operand_aliasing={{0}: (0, {}), {1}: (1, {})} | custom-call | tf_op jit(solution)/shard_map/end_fin/pallas_call | solution.py:612
  26.1 0.0 collective-permute-done.10.pairb
  26.1 0.0 collective-permute-done.9.paira
  26.1 0.0 collective-permute-done.7.gxa
  26.1 0.0 collective-permute-done.8.gxb
  26.2 2.2 %end.1 = (f32[18,144,256]{2,1,0:T(8,128)S(1)}, f32[66,48,256]{2,1,0:T(8,128)S(1)}, f32[64,32,256]{2,1,0:T(8,128)S(1)}, f32[16,128,256]{2,1,0:T(8,128)}, f32[64,32,256]{2,1,0:T(8,128)}) custom-call(f32[18,144,256]{2,1,0:T(8,128)S(1)} %get-tuple-element.53._0, ...), custom_call_target="tpu_custom_call", output_to_operand_aliasing={{0}: (0, {}), {1}: (1, {}), {2}: (2, {}), {4}: (3, {})} | custom-call | tf_op jit(solution)/shard_map/end/pallas_call | solution.py:665
Async XLA Ops:
  0.6 6.8 %copy-start.2 = (f32[16,128,256]{2,1,0:T(8,128)S(1)}, f32[16,128,256]{2,1,0:T(8,128)}, u32[]{:S(2)}) copy-start(f32[16,128,256]{2,1,0:T(8,128)} %fluid_hbm.1) | copy-start | bytes 6291460
  0.6 6.8 %copy-start.3 = (f32[64,32,256]{2,1,0:T(8,128)S(1)}, f32[64,32,256]{2,1,0:T(8,128)}, u32[]{:S(2)}) copy-start(f32[64,32,256]{2,1,0:T(8,128)} %fin_hbm.1) | copy-start | bytes 6291460
  2.8 8.0 %copy-start = (s32[16,128,256]{2,1,0:T(8,128)S(1)}, s32[16,128,256]{2,1,0:T(8,128)}, u32[]{:S(2)}) copy-start(s32[16,128,256]{2,1,0:T(8,128)} %act.3) | copy-start | bytes 6291460
  2.8 8.0 %copy-start.1 = (f32[64,32,256]{2,1,0:T(8,128)S(1)}, f32[64,32,256]{2,1,0:T(8,128)}, u32[]{:S(2)}) copy-start(f32[64,32,256]{2,1,0:T(8,128)} %src.3) | copy-start | bytes 6291460
  2.9 13.7 %collective-permute-start.3 = (f32[176,256]{1,0:T(8,128)S(1)}, f32[176,256]{1,0:T(8,128)S(1)}, u32[]{:S(2)}, u32[]{:S(2)}) collective-permute-start(f32[176,256]{1,0:T(8,128)S(1)} %get-tuple-element.44), channel_id=1, source_target_pairs={{0,2},{2,0},{4,6},{6,4},{1,3},{3,1},{5,7},{7,5},{8,10},{10,8},{12,... | collective-permute-start | bytes 540680 | tf_op jit(solution)/shard_map/ppermute | solution.py:440
  5.9 10.7 %collective-permute-start.4 = (f32[176,256]{1,0:T(8,128)S(1)}, f32[176,256]{1,0:T(8,128)S(1)}, u32[]{:S(2)}, u32[]{:S(2)}) collective-permute-start(f32[176,256]{1,0:T(8,128)S(1)} %get-tuple-element.45), channel_id=1, source_target_pairs={{0,6},{2,4},{4,2},{6,0},{1,7},{3,5},{5,3},{7,1},{8,14},{10,12},{12... | collective-permute-start | bytes 540680 | tf_op jit(solution)/shard_map/ppermute | solution.py:441
  8.5 1.9 %collective-permute-start = (f32[48,256]{1,0:T(8,128)S(1)}, f32[48,256]{1,0:T(8,128)S(1)}, u32[]{:S(2)}, u32[]{:S(2)}) collective-permute-start(f32[48,256]{1,0:T(8,128)S(1)} %get-tuple-element.35), channel_id=1, source_target_pairs={{0,1},{1,0},{2,3},{3,2},{4,5},{5,4},{6,7},{7,6},{8,9},{9,8},{10,11... | collective-permute-start | bytes 147464 | tf_op jit(solution)/shard_map/ppermute | solution.py:433
  8.6 4.2 %collective-permute-start.1 = (f32[48,256]{1,0:T(8,128)S(1)}, f32[48,256]{1,0:T(8,128)S(1)}, u32[]{:S(2)}, u32[]{:S(2)}) collective-permute-start(f32[48,256]{1,0:T(8,128)S(1)} %get-tuple-element.38), channel_id=1, source_target_pairs={{0,8},{1,9},{8,0},{9,1},{16,24},{17,25},{24,16},{25,17},{2,10},{3,... | collective-permute-start | bytes 147464 | tf_op jit(solution)/shard_map/ppermute | solution.py:428
  10.2 2.5 %collective-permute-start.2 = (f32[48,256]{1,0:T(8,128)S(1)}, f32[48,256]{1,0:T(8,128)S(1)}, u32[]{:S(2)}, u32[]{:S(2)}) collective-permute-start(f32[48,256]{1,0:T(8,128)S(1)} %get-tuple-element.39), channel_id=1, source_target_pairs={{0,1},{1,0},{8,16},{9,17},{16,8},{17,9},{24,25},{25,24},{2,3},{3,2... | collective-permute-start | bytes 147464 | tf_op jit(solution)/shard_map/ppermute | solution.py:429
  10.4 6.2 %collective-permute-start.5 = (f32[48,256]{1,0:T(8,128)S(1)}, f32[48,256]{1,0:T(8,128)S(1)}, u32[]{:S(2)}, u32[]{:S(2)}) collective-permute-start(f32[48,256]{1,0:T(8,128)S(1)} %get-tuple-element.46.refs_9_), channel_id=1, source_target_pairs={{0,4},{2,6},{4,0},{6,2},{1,5},{3,7},{5,1},{7,3},{8,12},{10,14},{12... | collective-permute-start | bytes 147464 | tf_op jit(solution)/shard_map/ppermute | solution.py:439
  17.7 8.4 %collective-permute-start.7 = (f32[128,256]{1,0:T(8,128)S(1)}, f32[128,256]{1,0:T(8,128)S(1)}, u32[]{:S(2)}, u32[]{:S(2)}) collective-permute-start(f32[128,256]{1,0:T(8,128)S(1)} %get-tuple-element.57), channel_id=1, source_target_pairs={{0,2},{1,3},{2,0},{3,1},{4,6},{5,7},{6,4},{7,5},{8,10},{9,11},{10,... | collective-permute-start | bytes 393224 | tf_op jit(solution)/shard_map/ppermute | solution.py:428
  19.2 6.9 %collective-permute-start.8 = (f32[128,256]{1,0:T(8,128)S(1)}, f32[128,256]{1,0:T(8,128)S(1)}, u32[]{:S(2)}, u32[]{:S(2)}) collective-permute-start(f32[128,256]{1,0:T(8,128)S(1)} %get-tuple-element.58), channel_id=1, source_target_pairs={{0,1},{1,0},{2,4},{3,5},{4,2},{5,3},{6,7},{7,6},{8,9},{9,8},{10,12... | collective-permute-start | bytes 393224 | tf_op jit(solution)/shard_map/ppermute | solution.py:429
  20.5 3.2 %collective-permute-start.6 = (f32[48,256]{1,0:T(8,128)S(1)}, f32[48,256]{1,0:T(8,128)S(1)}, u32[]{:S(2)}, u32[]{:S(2)}) collective-permute-start(f32[48,256]{1,0:T(8,128)S(1)} %get-tuple-element.52), channel_id=1, source_target_pairs={{0,1},{1,0},{2,3},{3,2},{4,5},{5,4},{6,7},{7,6},{8,9},{9,8},{10,11... | collective-permute-start | bytes 147464 | tf_op jit(solution)/shard_map/ppermute | solution.py:433
  21.1 5.0 %collective-permute-start.10 = (f32[48,256]{1,0:T(8,128)S(1)}, f32[48,256]{1,0:T(8,128)S(1)}, u32[]{:S(2)}, u32[]{:S(2)}) collective-permute-start(f32[48,256]{1,0:T(8,128)S(1)} %get-tuple-element.60), channel_id=1, source_target_pairs={{0,1},{1,0},{8,16},{9,17},{16,8},{17,9},{24,25},{25,24},{2,3},{3,2... | collective-permute-start | bytes 147464 | tf_op jit(solution)/shard_map/ppermute | solution.py:429
  21.2 5.0 %collective-permute-start.9 = (f32[48,256]{1,0:T(8,128)S(1)}, f32[48,256]{1,0:T(8,128)S(1)}, u32[]{:S(2)}, u32[]{:S(2)}) collective-permute-start(f32[48,256]{1,0:T(8,128)S(1)} %get-tuple-element.59), channel_id=1, source_target_pairs={{0,8},{1,9},{8,0},{9,1},{16,24},{17,25},{24,16},{25,17},{2,10},{3,... | collective-permute-start | bytes 147464 | tf_op jit(solution)/shard_map/ppermute | solution.py:428

commit v5 on v4

--- a/solution.py
+++ b/solution.py
@@ -467,11 +467,14 @@
         blocks = depth // 8
 
         def inner_blocks(body):
+            group = 2 if blocks % 2 == 0 else 1
+
             def step(k, carry):
-                body(k)
+                for u in range(group):
+                    body(1 + group * k + u)
                 return carry
 
-            lax.fori_loop(1, blocks - 1, step, 0)
+            lax.fori_loop(0, (blocks - 2) // group, step, 0)
 
         def middle_fin_kernel(fin, src, side, _, first, rest):
             hedge = side[cells : cells + fin_rows, 0:LANES]

time: 28.5 us -> 28.3 us (level)
  Pallas kernels: 12.9 us -> 12.5 us
  transfers between devices with their start and end apart: 11 -> 11, of which waited for: 2 -> 2; matrix products, arithmetic and copies ran while one was open for 0% -> 0% of each run, Pallas kernels for 26% -> 25%
where the time goes in v5:
time: 28.3 us; the launch traced here: 28.2 us
  Pallas kernels  12.5 us (44%)
  starting transfers between devices  11.7 us (41%)
  waiting for transfers between devices  3.23 us (11%)
  between operations  0.76 us (3%)
    ppermute x3, starting transfers between devices, exchange(): paira = lax.ppermute(paira, axes, first)  5.76 us
    ppermute x1, starting transfers between devices, local(): gxa = lax.ppermute(gxa, 'gx', mixed_with(1))  3.03 us
    ppermute x1, waiting for transfers between devices, local(): walls = [wall, lax.ppermute(wall, 'gx', mixed_with(2))]  2.72 us
    pallas_call x1, Pallas kernels, local(): pl.pallas_call(end_kernel, out_shape=(fluid_pad, fin_pad, f32(depth, fin_...  2.24 us
    pallas_call x1, Pallas kernels, local(): pl.pallas_call(start_gx_kernel, out_shape=(f32(gx_rows, width), f32(gx_ro...  2.18 us
    pallas_call x1, Pallas kernels, local(): pl.pallas_call(end_fin_kernel, out_shape=(fin_rest, fluid_pad, f32(pairs,...  2.14 us
    ppermute x1, starting transfers between devices, local(): gxb = lax.ppermute(gxb, 'gx', mixed_with(3))  1.49 us
    pallas_call x1, Pallas kernels, local(): pl.pallas_call(middle_fin_kernel, out_shape=(fin_pad, f32(depth, fin_rows...  1.35 us
  transfers between devices with their start and end apart: 11, of which 2 were waited for; matrix products, arithmetic and copies ran while one was open for 0% of the time, Pallas kernels for 25%

profile of v5, /device:TPU:0, one launch (start us, length us, event | category | flops | bytes accessed | tf_op | source)
XLA Modules:
  0.0 28.2 jit_solution(3857732906700481767)
XLA Ops:
  0.6 0.0 copy-start.2
  0.6 0.0 copy-start.3
  0.7 2.2 %start_gx.1 = (f32[176,256]{1,0:T(8,128)S(1)}, f32[176,256]{1,0:T(8,128)S(1)}, f32[48,256]{1,0:T(8,128)S(1)}) custom-call(f32[16,128,256]{2,1,0:T(8,128)} %fluid_hbm.1, f32[64,32,256]{2,1,0:T(8,128)} %fin_hbm.1, s32[16,128]{1,0:T(8,128)} %bitcast.2, s32[16,128]{1,0:T(8,128)} %bitcast.3), custom_call_target="tpu_custom_call" | custom-call | tf_op jit(solution)/shard_map/start_gx/pallas_call | solution.py:375
  2.8 0.0 copy-start
  2.8 0.0 copy-start.1
  2.9 3.0 %collective-permute-start.3 = (f32[176,256]{1,0:T(8,128)S(1)}, f32[176,256]{1,0:T(8,128)S(1)}, u32[]{:S(2)}, u32[]{:S(2)}) collective-permute-start(f32[176,256]{1,0:T(8,128)S(1)} %get-tuple-element.44), channel_id=1, source_target_pairs={{0,2},{2,0},{4,6},{6,4},{1,3},{3,1},{5,7},{7,5},{8,10},{10,8},{12,... | collective-permute-start | bytes 540680 | tf_op jit(solution)/shard_map/ppermute | solution.py:440
  5.9 1.5 %collective-permute-start.4 = (f32[176,256]{1,0:T(8,128)S(1)}, f32[176,256]{1,0:T(8,128)S(1)}, u32[]{:S(2)}, u32[]{:S(2)}) collective-permute-start(f32[176,256]{1,0:T(8,128)S(1)} %get-tuple-element.45), channel_id=1, source_target_pairs={{0,6},{2,4},{4,2},{6,0},{1,7},{3,5},{5,3},{7,1},{8,14},{10,12},{12... | collective-permute-start | bytes 540680 | tf_op jit(solution)/shard_map/ppermute | solution.py:441
  7.4 0.0 copy-done.2
  7.4 0.0 copy-done.3
  7.4 1.1 %start_rest.1 = (f32[18,144,256]{2,1,0:T(8,128)S(1)}, f32[66,48,256]{2,1,0:T(8,128)S(1)}, f32[48,256]{1,0:T(8,128)S(1)}, f32[48,256]{1,0:T(8,128)S(1)}, f32[48,256]{1,0:T(8,128)S(1)}) custom-call(f32[16,128,256]{2,1,0:T(8,128)S(1)} %copy-done.2, f32[64,32,256]{2,1,0:T(8,128)S(1)} %copy-done.3), custom_call_target="tpu_custom_call" | custom-call | tf_op jit(solution)/shard_map/start_rest/pallas_call | solution.py:405
  8.5 0.1 collective-permute-start
  8.6 1.6 %collective-permute-start.1 = (f32[48,256]{1,0:T(8,128)S(1)}, f32[48,256]{1,0:T(8,128)S(1)}, u32[]{:S(2)}, u32[]{:S(2)}) collective-permute-start(f32[48,256]{1,0:T(8,128)S(1)} %get-tuple-element.38), channel_id=1, source_target_pairs={{0,8},{1,9},{8,0},{9,1},{16,24},{17,25},{24,16},{25,17},{2,10},{3,... | collective-permute-start | bytes 147464 | tf_op jit(solution)/shard_map/ppermute | solution.py:428
  10.2 0.2 collective-permute-start.2
  10.4 0.0 collective-permute-done.side
  10.4 0.5 %collective-permute-start.5 = (f32[48,256]{1,0:T(8,128)S(1)}, f32[48,256]{1,0:T(8,128)S(1)}, u32[]{:S(2)}, u32[]{:S(2)}) collective-permute-start(f32[48,256]{1,0:T(8,128)S(1)} %get-tuple-element.46.refs_9_), channel_id=1, source_target_pairs={{0,4},{2,6},{4,0},{6,2},{1,5},{3,7},{5,1},{7,3},{8,12},{10,14},{12... | collective-permute-start | bytes 147464 | tf_op jit(solution)/shard_map/ppermute | solution.py:439
  10.9 0.0 copy-done
  10.9 0.0 copy-done.1
  10.9 1.3 %middle_fin.1 = (f32[66,48,256]{2,1,0:T(8,128)S(1)}, f32[64,32,256]{2,1,0:T(8,128)S(1)}) custom-call(f32[66,48,256]{2,1,0:T(8,128)S(1)} %get-tuple-element.34.fin._1, f32[64,32,256]{2,1,0:T(8,128)S(1)} %copy-done.1, f32[48,256]{1,0:T(8,128)S(1)} %collective-permute-done.side, s32[16,128,256]{2,1,0:T(8,128)S(1)} %copy-done), custom_call_target="tpu_custom_call" | custom-call | tf_op jit(solution)/shard_map/middle_fin/pallas_call | solution.py:484
  12.2 0.5 %collective-permute-done.1.paira.refs_7_ = f32[48,256]{1,0:T(8,128)S(1)} collective-permute-done((f32[48,256]{1,0:T(8,128)S(1)}, f32[48,256]{1,0:T(8,128)S(1)}, u32[]{:S(2)}, u32[]{:S(2)}) %collective-permute-start.1) | collective-permute-done | bytes 49184 | tf_op jit(solution)/shard_map/ppermute | solution.py:428
  12.7 0.0 collective-permute-done.2.pairb.refs_8_
  12.7 1.1 %middle_grp.1 = (f32[18,144,256]{2,1,0:T(8,128)S(1)}, f32[66,48,256]{2,1,0:T(8,128)S(1)}, f32[66,48,256]{2,1,0:T(8,128)S(1)}, f32[64,32,256]{2,1,0:T(8,128)S(1)}, f32[8,128,256]{2,1,0:T(8,128)S(1)}) custom-call(f32[18,144,256]{2,1,0:T(8,128)S(1)} %get-tuple-element.33._0, ...), custom_call_target="tpu_custom_call", output_to_operand_aliasing={{0}: (0, {}), {1}: (1, {}), {2}: (2, {}), {3}: (3, {})} | custom-call | tf_op jit(solution)/shard_map/middle_grp/pallas_call | solution.py:507
  13.8 2.7 %collective-permute-done.5.refs_10_ = f32[48,256]{1,0:T(8,128)S(1)} collective-permute-done((f32[48,256]{1,0:T(8,128)S(1)}, f32[48,256]{1,0:T(8,128)S(1)}, u32[]{:S(2)}, u32[]{:S(2)}) %collective-permute-start.5) | collective-permute-done | bytes 49184 | tf_op jit(solution)/shard_map/ppermute | solution.py:439
  16.6 0.0 collective-permute-done.3.refs_5_
  16.6 0.0 collective-permute-done.4.refs_6_
  16.6 1.1 %middle_gx.1 = (f32[18,144,256]{2,1,0:T(8,128)S(1)}, f32[66,48,256]{2,1,0:T(8,128)S(1)}, f32[64,32,256]{2,1,0:T(8,128)S(1)}, f32[16,128]{1,0:T(8,128)S(1)}, f32[...) custom-call(f32[18,144,256]{2,1,0:T(8,128)S(1)} %get-tuple-element.4, ...), custom_call_target="tpu_custom_call", output_to_operand_aliasing={{0}: (0, {}), {1}: (1, {}), {2}: (2, {})} | custom-call | tf_op jit(solution)/shard_map/middle_gx/pallas_call | solution.py:573
  17.7 1.5 %collective-permute-start.7 = (f32[128,256]{1,0:T(8,128)S(1)}, f32[128,256]{1,0:T(8,128)S(1)}, u32[]{:S(2)}, u32[]{:S(2)}) collective-permute-start(f32[128,256]{1,0:T(8,128)S(1)} %get-tuple-element.57), channel_id=1, source_target_pairs={{0,2},{1,3},{2,0},{3,1},{4,6},{5,7},{6,4},{7,5},{8,10},{9,11},{10,... | collective-permute-start | bytes 393224 | tf_op jit(solution)/shard_map/ppermute | solution.py:428
  19.2 0.0 collective-permute-start.8
  19.2 1.3 %middle_rest.1 = (f32[18,144,256]{2,1,0:T(8,128)S(1)}, f32[48,256]{1,0:T(8,128)S(1)}, f32[48,256]{1,0:T(8,128)S(1)}, f32[48,256]{1,0:T(8,128)S(1)}) custom-call(f32[18,144,256]{2,1,0:T(8,128)S(1)} %get-tuple-element.48._, s32[16,128,256]{2,1,0:T(8,128)S(1)} %copy-done, f32[128,128]{1,0:T(8,128)S(1)} %get-tuple-element.49.zedge, ...), custom_call_target="tpu_custom_call", output_to_operand_aliasing={{0}: (0, {})} | custom-call | tf_op jit(solution)/shard_map/middle_rest/pallas_call | solution.py:590
  20.5 0.6 %collective-permute-start.6 = (f32[48,256]{1,0:T(8,128)S(1)}, f32[48,256]{1,0:T(8,128)S(1)}, u32[]{:S(2)}, u32[]{:S(2)}) collective-permute-start(f32[48,256]{1,0:T(8,128)S(1)} %get-tuple-element.52), channel_id=1, source_target_pairs={{0,1},{1,0},{2,3},{3,2},{4,5},{5,4},{6,7},{7,6},{8,9},{9,8},{10,11... | collective-permute-start | bytes 147464 | tf_op jit(solution)/shard_map/ppermute | solution.py:433
  21.1 0.1 collective-permute-start.10
  21.2 2.6 %collective-permute-start.9 = (f32[48,256]{1,0:T(8,128)S(1)}, f32[48,256]{1,0:T(8,128)S(1)}, u32[]{:S(2)}, u32[]{:S(2)}) collective-permute-start(f32[48,256]{1,0:T(8,128)S(1)} %get-tuple-element.59), channel_id=1, source_target_pairs={{0,8},{1,9},{8,0},{9,1},{16,24},{17,25},{24,16},{25,17},{2,10},{3,... | collective-permute-start | bytes 147464 | tf_op jit(solution)/shard_map/ppermute | solution.py:428
  23.7 0.0 collective-permute-done.6.side
  23.7 2.1 %end_fin.1 = (f32[64,32,256]{2,1,0:T(8,128)S(1)}, f32[18,144,256]{2,1,0:T(8,128)S(1)}, f32[8,128,256]{2,1,0:T(8,128)S(1)}, f32[64,32,256]{2,1,0:T(8,128)}) custom-call(f32[64,32,256]{2,1,0:T(8,128)S(1)} %get-tuple-element.47._0, f32[18,144,256]{2,1,0:T(8,128)S(1)} %get-tuple-element.51._1, ...), custom_call_target="tpu_custom_call", output_to_operand_aliasing={{0}: (0, {}), {1}: (1, {})} | custom-call | tf_op jit(solution)/shard_map/end_fin/pallas_call | solution.py:615
  25.9 0.0 collective-permute-done.10.pairb
  25.9 0.0 collective-permute-done.9.paira
  25.9 0.0 collective-permute-done.7.gxa
  25.9 0.0 collective-permute-done.8.gxb
  25.9 2.2 %end.1 = (f32[18,144,256]{2,1,0:T(8,128)S(1)}, f32[66,48,256]{2,1,0:T(8,128)S(1)}, f32[64,32,256]{2,1,0:T(8,128)S(1)}, f32[16,128,256]{2,1,0:T(8,128)}, f32[64,32,256]{2,1,0:T(8,128)}) custom-call(f32[18,144,256]{2,1,0:T(8,128)S(1)} %get-tuple-element.53._0, ...), custom_call_target="tpu_custom_call", output_to_operand_aliasing={{0}: (0, {}), {1}: (1, {}), {2}: (2, {}), {4}: (3, {})} | custom-call | tf_op jit(solution)/shard_map/end/pallas_call | solution.py:668
Async XLA Ops:
  0.6 6.8 %copy-start.2 = (f32[16,128,256]{2,1,0:T(8,128)S(1)}, f32[16,128,256]{2,1,0:T(8,128)}, u32[]{:S(2)}) copy-start(f32[16,128,256]{2,1,0:T(8,128)} %fluid_hbm.1) | copy-start | bytes 6291460
  0.6 6.8 %copy-start.3 = (f32[64,32,256]{2,1,0:T(8,128)S(1)}, f32[64,32,256]{2,1,0:T(8,128)}, u32[]{:S(2)}) copy-start(f32[64,32,256]{2,1,0:T(8,128)} %fin_hbm.1) | copy-start | bytes 6291460
  2.8 8.0 %copy-start = (s32[16,128,256]{2,1,0:T(8,128)S(1)}, s32[16,128,256]{2,1,0:T(8,128)}, u32[]{:S(2)}) copy-start(s32[16,128,256]{2,1,0:T(8,128)} %act.3) | copy-start | bytes 6291460
  2.8 8.0 %copy-start.1 = (f32[64,32,256]{2,1,0:T(8,128)S(1)}, f32[64,32,256]{2,1,0:T(8,128)}, u32[]{:S(2)}) copy-start(f32[64,32,256]{2,1,0:T(8,128)} %src.3) | copy-start | bytes 6291460
  2.9 13.7 %collective-permute-start.3 = (f32[176,256]{1,0:T(8,128)S(1)}, f32[176,256]{1,0:T(8,128)S(1)}, u32[]{:S(2)}, u32[]{:S(2)}) collective-permute-start(f32[176,256]{1,0:T(8,128)S(1)} %get-tuple-element.44), channel_id=1, source_target_pairs={{0,2},{2,0},{4,6},{6,4},{1,3},{3,1},{5,7},{7,5},{8,10},{10,8},{12,... | collective-permute-start | bytes 540680 | tf_op jit(solution)/shard_map/ppermute | solution.py:440
  5.9 10.7 %collective-permute-start.4 = (f32[176,256]{1,0:T(8,128)S(1)}, f32[176,256]{1,0:T(8,128)S(1)}, u32[]{:S(2)}, u32[]{:S(2)}) collective-permute-start(f32[176,256]{1,0:T(8,128)S(1)} %get-tuple-element.45), channel_id=1, source_target_pairs={{0,6},{2,4},{4,2},{6,0},{1,7},{3,5},{5,3},{7,1},{8,14},{10,12},{12... | collective-permute-start | bytes 540680 | tf_op jit(solution)/shard_map/ppermute | solution.py:441
  8.5 1.9 %collective-permute-start = (f32[48,256]{1,0:T(8,128)S(1)}, f32[48,256]{1,0:T(8,128)S(1)}, u32[]{:S(2)}, u32[]{:S(2)}) collective-permute-start(f32[48,256]{1,0:T(8,128)S(1)} %get-tuple-element.35), channel_id=1, source_target_pairs={{0,1},{1,0},{2,3},{3,2},{4,5},{5,4},{6,7},{7,6},{8,9},{9,8},{10,11... | collective-permute-start | bytes 147464 | tf_op jit(solution)/shard_map/ppermute | solution.py:433
  8.6 4.2 %collective-permute-start.1 = (f32[48,256]{1,0:T(8,128)S(1)}, f32[48,256]{1,0:T(8,128)S(1)}, u32[]{:S(2)}, u32[]{:S(2)}) collective-permute-start(f32[48,256]{1,0:T(8,128)S(1)} %get-tuple-element.38), channel_id=1, source_target_pairs={{0,8},{1,9},{8,0},{9,1},{16,24},{17,25},{24,16},{25,17},{2,10},{3,... | collective-permute-start | bytes 147464 | tf_op jit(solution)/shard_map/ppermute | solution.py:428
  10.2 2.5 %collective-permute-start.2 = (f32[48,256]{1,0:T(8,128)S(1)}, f32[48,256]{1,0:T(8,128)S(1)}, u32[]{:S(2)}, u32[]{:S(2)}) collective-permute-start(f32[48,256]{1,0:T(8,128)S(1)} %get-tuple-element.39), channel_id=1, source_target_pairs={{0,1},{1,0},{8,16},{9,17},{16,8},{17,9},{24,25},{25,24},{2,3},{3,2... | collective-permute-start | bytes 147464 | tf_op jit(solution)/shard_map/ppermute | solution.py:429
  10.4 6.2 %collective-permute-start.5 = (f32[48,256]{1,0:T(8,128)S(1)}, f32[48,256]{1,0:T(8,128)S(1)}, u32[]{:S(2)}, u32[]{:S(2)}) collective-permute-start(f32[48,256]{1,0:T(8,128)S(1)} %get-tuple-element.46.refs_9_), channel_id=1, source_target_pairs={{0,4},{2,6},{4,0},{6,2},{1,5},{3,7},{5,1},{7,3},{8,12},{10,14},{12... | collective-permute-start | bytes 147464 | tf_op jit(solution)/shard_map/ppermute | solution.py:439
  17.7 8.2 %collective-permute-start.7 = (f32[128,256]{1,0:T(8,128)S(1)}, f32[128,256]{1,0:T(8,128)S(1)}, u32[]{:S(2)}, u32[]{:S(2)}) collective-permute-start(f32[128,256]{1,0:T(8,128)S(1)} %get-tuple-element.57), channel_id=1, source_target_pairs={{0,2},{1,3},{2,0},{3,1},{4,6},{5,7},{6,4},{7,5},{8,10},{9,11},{10,... | collective-permute-start | bytes 393224 | tf_op jit(solution)/shard_map/ppermute | solution.py:428
  19.2 6.7 %collective-permute-start.8 = (f32[128,256]{1,0:T(8,128)S(1)}, f32[128,256]{1,0:T(8,128)S(1)}, u32[]{:S(2)}, u32[]{:S(2)}) collective-permute-start(f32[128,256]{1,0:T(8,128)S(1)} %get-tuple-element.58), channel_id=1, source_target_pairs={{0,1},{1,0},{2,4},{3,5},{4,2},{5,3},{6,7},{7,6},{8,9},{9,8},{10,12... | collective-permute-start | bytes 393224 | tf_op jit(solution)/shard_map/ppermute | solution.py:429
  20.5 3.2 %collective-permute-start.6 = (f32[48,256]{1,0:T(8,128)S(1)}, f32[48,256]{1,0:T(8,128)S(1)}, u32[]{:S(2)}, u32[]{:S(2)}) collective-permute-start(f32[48,256]{1,0:T(8,128)S(1)} %get-tuple-element.52), channel_id=1, source_target_pairs={{0,1},{1,0},{2,3},{3,2},{4,5},{5,4},{6,7},{7,6},{8,9},{9,8},{10,11... | collective-permute-start | bytes 147464 | tf_op jit(solution)/shard_map/ppermute | solution.py:433
  21.1 4.8 %collective-permute-start.10 = (f32[48,256]{1,0:T(8,128)S(1)}, f32[48,256]{1,0:T(8,128)S(1)}, u32[]{:S(2)}, u32[]{:S(2)}) collective-permute-start(f32[48,256]{1,0:T(8,128)S(1)} %get-tuple-element.60), channel_id=1, source_target_pairs={{0,1},{1,0},{8,16},{9,17},{16,8},{17,9},{24,25},{25,24},{2,3},{3,2... | collective-permute-start | bytes 147464 | tf_op jit(solution)/shard_map/ppermute | solution.py:429
  21.2 4.7 %collective-permute-start.9 = (f32[48,256]{1,0:T(8,128)S(1)}, f32[48,256]{1,0:T(8,128)S(1)}, u32[]{:S(2)}, u32[]{:S(2)}) collective-permute-start(f32[48,256]{1,0:T(8,128)S(1)} %get-tuple-element.59), channel_id=1, source_target_pairs={{0,8},{1,9},{8,0},{9,1},{16,24},{17,25},{24,16},{25,17},{2,10},{3,... | collective-permute-start | bytes 147464 | tf_op jit(solution)/shard_map/ppermute | solution.py:428

commit v6 on v5

--- a/solution.py
+++ b/solution.py
@@ -304,6 +304,7 @@
         half = rows // 2
         pairs = cells // 2
         outer_group = max(g for g in (1, 2, 4) if pairs % g == 0)
+        sum_group = max(g for g in (1, 2, 4, 8) if pairs % g == 0)
         inner_group = max(g for g in (1, 2, 3) if (pairs - 2) % g == 0)
         face_rows = half + depth
         wall_rows = fin_rows + cells
@@ -497,19 +498,20 @@
             for block in (0, blocks - 1):
                 fin_first(fin, src, first, rest, hedge, block)
             unpack_lines(fluid, side, lax.axis_index("gy"), dims)
-            neighbour_sums(fluid, others, sums, 0, dims, all_pairs)
+            neighbour_sums(fluid, others, sums, 0, dims, sum_pairs)
 
         fin_rest = f32(depth, fin_rows, fin_width)
         other_buffer = lambda planes: buffer(planes, rows + 2 * PAD, width)
         outer_pairs = (0, pairs - 1, 1, 2)
         all_pairs = (0, 1, pairs // outer_group, outer_group)
+        sum_pairs = (0, 1, pairs // sum_group, sum_group)
         inner_pairs = (1, 1, (pairs - 2) // inner_group, inner_group)
         fluid0, _, first, rest, sums = pl.pallas_call(
             middle_grp_kernel,
             out_shape=(fluid_pad, fin_pad, fin_pad, fin_rest, f32(pairs, rows, width)),
             in_specs=[vmem] * 8,
             out_specs=(vmem,) * 5,
-            scratch_shapes=[other_buffer(outer_group)],
+            scratch_shapes=[other_buffer(sum_group)],
             input_output_aliases={0: 0, 1: 1, 2: 2, 3: 3},
             compiler_params=params,
             name="middle_grp",
@@ -605,7 +607,7 @@
             inner_blocks(lambda k: fin_second(first, rest, hedge, k))
             copy = fin_copy(rest, fin_new, sem.at[0], inner_depths, inner_rows)
             copy.start()
-            neighbour_sums(fluid, others, sums, 1, dims, all_pairs)
+            neighbour_sums(fluid, others, sums, 1, dims, sum_pairs)
             copy.wait()
 
         def fin_copy(rest, fin_new, sem, depths, lines):
@@ -617,7 +619,7 @@
             out_shape=(fin_rest, fluid_pad, f32(pairs, rows, width), fin_rest),
             in_specs=[vmem] * 4,
             out_specs=(vmem, vmem, vmem, hbm),
-            scratch_shapes=[other_buffer(outer_group), pltpu.SemaphoreType.DMA((1,))],
+            scratch_shapes=[other_buffer(sum_group), pltpu.SemaphoreType.DMA((1,))],
             input_output_aliases={0: 0, 1: 1},
             compiler_params=params,
             name="end_fin",

time: 28.3 us -> 28.3 us (level)
  transfers between devices with their start and end apart: 11 -> 11, of which waited for: 2 -> 2; matrix products, arithmetic and copies ran while one was open for 0% -> 0% of each run, Pallas kernels for 25% -> 24%
where the time goes in v6:
time: 28.3 us; the launch traced here: 28.2 us
  Pallas kernels  12.4 us (44%)
  starting transfers between devices  11.7 us (41%)
  waiting for transfers between devices  3.37 us (12%)
  between operations  0.76 us (3%)
    ppermute x3, starting transfers between devices, exchange(): paira = lax.ppermute(paira, axes, first)  5.76 us
    ppermute x1, starting transfers between devices, local(): gxa = lax.ppermute(gxa, 'gx', mixed_with(1))  3.03 us
    ppermute x1, waiting for transfers between devices, local(): walls = [wall, lax.ppermute(wall, 'gx', mixed_with(2))]  2.85 us
    pallas_call x1, Pallas kernels, local(): pl.pallas_call(end_kernel, out_shape=(fluid_pad, fin_pad, f32(depth, fin_...  2.24 us
    pallas_call x1, Pallas kernels, local(): pl.pallas_call(start_gx_kernel, out_shape=(f32(gx_rows, width), f32(gx_ro...  2.18 us
    pallas_call x1, Pallas kernels, local(): pl.pallas_call(end_fin_kernel, out_shape=(fin_rest, fluid_pad, f32(pairs,...  2.14 us
    ppermute x1, starting transfers between devices, local(): gxb = lax.ppermute(gxb, 'gx', mixed_with(3))  1.49 us
    pallas_call x1, Pallas kernels, local(): pl.pallas_call(middle_fin_kernel, out_shape=(fin_pad, f32(depth, fin_rows...  1.35 us
  transfers between devices with their start and end apart: 11, of which 2 were waited for; matrix products, arithmetic and copies ran while one was open for 0% of the time, Pallas kernels for 24%

profile of v6, /device:TPU:0, one launch (start us, length us, event | category | flops | bytes accessed | tf_op | source)
XLA Modules:
  0.0 28.2 jit_solution(7220837730940568605)
XLA Ops:
  0.6 0.0 copy-start.2
  0.6 0.0 copy-start.3
  0.7 2.2 %start_gx.1 = (f32[176,256]{1,0:T(8,128)S(1)}, f32[176,256]{1,0:T(8,128)S(1)}, f32[48,256]{1,0:T(8,128)S(1)}) custom-call(f32[16,128,256]{2,1,0:T(8,128)} %fluid_hbm.1, f32[64,32,256]{2,1,0:T(8,128)} %fin_hbm.1, s32[16,128]{1,0:T(8,128)} %bitcast.2, s32[16,128]{1,0:T(8,128)} %bitcast.3), custom_call_target="tpu_custom_call" | custom-call | tf_op jit(solution)/shard_map/start_gx/pallas_call | solution.py:376
  2.8 0.0 copy-start
  2.8 0.0 copy-start.1
  2.9 3.0 %collective-permute-start.3 = (f32[176,256]{1,0:T(8,128)S(1)}, f32[176,256]{1,0:T(8,128)S(1)}, u32[]{:S(2)}, u32[]{:S(2)}) collective-permute-start(f32[176,256]{1,0:T(8,128)S(1)} %get-tuple-element.44), channel_id=1, source_target_pairs={{0,2},{2,0},{4,6},{6,4},{1,3},{3,1},{5,7},{7,5},{8,10},{10,8},{12,... | collective-permute-start | bytes 540680 | tf_op jit(solution)/shard_map/ppermute | solution.py:441
  5.9 1.5 %collective-permute-start.4 = (f32[176,256]{1,0:T(8,128)S(1)}, f32[176,256]{1,0:T(8,128)S(1)}, u32[]{:S(2)}, u32[]{:S(2)}) collective-permute-start(f32[176,256]{1,0:T(8,128)S(1)} %get-tuple-element.45), channel_id=1, source_target_pairs={{0,6},{2,4},{4,2},{6,0},{1,7},{3,5},{5,3},{7,1},{8,14},{10,12},{12... | collective-permute-start | bytes 540680 | tf_op jit(solution)/shard_map/ppermute | solution.py:442
  7.4 0.0 copy-done.2
  7.4 0.0 copy-done.3
  7.4 1.1 %start_rest.1 = (f32[18,144,256]{2,1,0:T(8,128)S(1)}, f32[66,48,256]{2,1,0:T(8,128)S(1)}, f32[48,256]{1,0:T(8,128)S(1)}, f32[48,256]{1,0:T(8,128)S(1)}, f32[48,256]{1,0:T(8,128)S(1)}) custom-call(f32[16,128,256]{2,1,0:T(8,128)S(1)} %copy-done.2, f32[64,32,256]{2,1,0:T(8,128)S(1)} %copy-done.3), custom_call_target="tpu_custom_call" | custom-call | tf_op jit(solution)/shard_map/start_rest/pallas_call | solution.py:406
  8.5 0.1 collective-permute-start
  8.6 1.6 %collective-permute-start.1 = (f32[48,256]{1,0:T(8,128)S(1)}, f32[48,256]{1,0:T(8,128)S(1)}, u32[]{:S(2)}, u32[]{:S(2)}) collective-permute-start(f32[48,256]{1,0:T(8,128)S(1)} %get-tuple-element.38), channel_id=1, source_target_pairs={{0,8},{1,9},{8,0},{9,1},{16,24},{17,25},{24,16},{25,17},{2,10},{3,... | collective-permute-start | bytes 147464 | tf_op jit(solution)/shard_map/ppermute | solution.py:429
  10.2 0.2 collective-permute-start.2
  10.4 0.0 collective-permute-done.side
  10.4 0.5 %collective-permute-start.5 = (f32[48,256]{1,0:T(8,128)S(1)}, f32[48,256]{1,0:T(8,128)S(1)}, u32[]{:S(2)}, u32[]{:S(2)}) collective-permute-start(f32[48,256]{1,0:T(8,128)S(1)} %get-tuple-element.46.refs_9_), channel_id=1, source_target_pairs={{0,4},{2,6},{4,0},{6,2},{1,5},{3,7},{5,1},{7,3},{8,12},{10,14},{12... | collective-permute-start | bytes 147464 | tf_op jit(solution)/shard_map/ppermute | solution.py:440
  10.9 0.0 copy-done
  10.9 0.0 copy-done.1
  10.9 1.3 %middle_fin.1 = (f32[66,48,256]{2,1,0:T(8,128)S(1)}, f32[64,32,256]{2,1,0:T(8,128)S(1)}) custom-call(f32[66,48,256]{2,1,0:T(8,128)S(1)} %get-tuple-element.34.fin._1, f32[64,32,256]{2,1,0:T(8,128)S(1)} %copy-done.1, f32[48,256]{1,0:T(8,128)S(1)} %collective-permute-done.side, s32[16,128,256]{2,1,0:T(8,128)S(1)} %copy-done), custom_call_target="tpu_custom_call" | custom-call | tf_op jit(solution)/shard_map/middle_fin/pallas_call | solution.py:485
  12.2 0.5 %collective-permute-done.1.paira.refs_7_ = f32[48,256]{1,0:T(8,128)S(1)} collective-permute-done((f32[48,256]{1,0:T(8,128)S(1)}, f32[48,256]{1,0:T(8,128)S(1)}, u32[]{:S(2)}, u32[]{:S(2)}) %collective-permute-start.1) | collective-permute-done | bytes 49184 | tf_op jit(solution)/shard_map/ppermute | solution.py:429
  12.7 0.0 collective-permute-done.2.pairb.refs_8_
  12.7 1.0 %middle_grp.1 = (f32[18,144,256]{2,1,0:T(8,128)S(1)}, f32[66,48,256]{2,1,0:T(8,128)S(1)}, f32[66,48,256]{2,1,0:T(8,128)S(1)}, f32[64,32,256]{2,1,0:T(8,128)S(1)}, f32[8,128,256]{2,1,0:T(8,128)S(1)}) custom-call(f32[18,144,256]{2,1,0:T(8,128)S(1)} %get-tuple-element.33._0, ...), custom_call_target="tpu_custom_call", output_to_operand_aliasing={{0}: (0, {}), {1}: (1, {}), {2}: (2, {}), {3}: (3, {})} | custom-call | tf_op jit(solution)/shard_map/middle_grp/pallas_call | solution.py:509
  13.7 2.9 %collective-permute-done.5.refs_10_ = f32[48,256]{1,0:T(8,128)S(1)} collective-permute-done((f32[48,256]{1,0:T(8,128)S(1)}, f32[48,256]{1,0:T(8,128)S(1)}, u32[]{:S(2)}, u32[]{:S(2)}) %collective-permute-start.5) | collective-permute-done | bytes 49184 | tf_op jit(solution)/shard_map/ppermute | solution.py:440
  16.6 0.0 collective-permute-done.3.refs_5_
  16.6 0.0 collective-permute-done.4.refs_6_
  16.6 1.1 %middle_gx.1 = (f32[18,144,256]{2,1,0:T(8,128)S(1)}, f32[66,48,256]{2,1,0:T(8,128)S(1)}, f32[64,32,256]{2,1,0:T(8,128)S(1)}, f32[16,128]{1,0:T(8,128)S(1)}, f32[...) custom-call(f32[18,144,256]{2,1,0:T(8,128)S(1)} %get-tuple-element.4, ...), custom_call_target="tpu_custom_call", output_to_operand_aliasing={{0}: (0, {}), {1}: (1, {}), {2}: (2, {})} | custom-call | tf_op jit(solution)/shard_map/middle_gx/pallas_call | solution.py:575
  17.7 1.5 %collective-permute-start.7 = (f32[128,256]{1,0:T(8,128)S(1)}, f32[128,256]{1,0:T(8,128)S(1)}, u32[]{:S(2)}, u32[]{:S(2)}) collective-permute-start(f32[128,256]{1,0:T(8,128)S(1)} %get-tuple-element.57), channel_id=1, source_target_pairs={{0,2},{1,3},{2,0},{3,1},{4,6},{5,7},{6,4},{7,5},{8,10},{9,11},{10,... | collective-permute-start | bytes 393224 | tf_op jit(solution)/shard_map/ppermute | solution.py:429
  19.2 0.0 collective-permute-start.8
  19.2 1.3 %middle_rest.1 = (f32[18,144,256]{2,1,0:T(8,128)S(1)}, f32[48,256]{1,0:T(8,128)S(1)}, f32[48,256]{1,0:T(8,128)S(1)}, f32[48,256]{1,0:T(8,128)S(1)}) custom-call(f32[18,144,256]{2,1,0:T(8,128)S(1)} %get-tuple-element.48._, s32[16,128,256]{2,1,0:T(8,128)S(1)} %copy-done, f32[128,128]{1,0:T(8,128)S(1)} %get-tuple-element.49.zedge, ...), custom_call_target="tpu_custom_call", output_to_operand_aliasing={{0}: (0, {})} | custom-call | tf_op jit(solution)/shard_map/middle_rest/pallas_call | solution.py:592
  20.5 0.6 %collective-permute-start.6 = (f32[48,256]{1,0:T(8,128)S(1)}, f32[48,256]{1,0:T(8,128)S(1)}, u32[]{:S(2)}, u32[]{:S(2)}) collective-permute-start(f32[48,256]{1,0:T(8,128)S(1)} %get-tuple-element.52), channel_id=1, source_target_pairs={{0,1},{1,0},{2,3},{3,2},{4,5},{5,4},{6,7},{7,6},{8,9},{9,8},{10,11... | collective-permute-start | bytes 147464 | tf_op jit(solution)/shard_map/ppermute | solution.py:434
  21.1 0.1 collective-permute-start.10
  21.2 2.6 %collective-permute-start.9 = (f32[48,256]{1,0:T(8,128)S(1)}, f32[48,256]{1,0:T(8,128)S(1)}, u32[]{:S(2)}, u32[]{:S(2)}) collective-permute-start(f32[48,256]{1,0:T(8,128)S(1)} %get-tuple-element.59), channel_id=1, source_target_pairs={{0,8},{1,9},{8,0},{9,1},{16,24},{17,25},{24,16},{25,17},{2,10},{3,... | collective-permute-start | bytes 147464 | tf_op jit(solution)/shard_map/ppermute | solution.py:429
  23.7 0.0 collective-permute-done.6.side
  23.7 2.1 %end_fin.1 = (f32[64,32,256]{2,1,0:T(8,128)S(1)}, f32[18,144,256]{2,1,0:T(8,128)S(1)}, f32[8,128,256]{2,1,0:T(8,128)S(1)}, f32[64,32,256]{2,1,0:T(8,128)}) custom-call(f32[64,32,256]{2,1,0:T(8,128)S(1)} %get-tuple-element.47._0, f32[18,144,256]{2,1,0:T(8,128)S(1)} %get-tuple-element.51._1, ...), custom_call_target="tpu_custom_call", output_to_operand_aliasing={{0}: (0, {}), {1}: (1, {})} | custom-call | tf_op jit(solution)/shard_map/end_fin/pallas_call | solution.py:617
  25.9 0.0 collective-permute-done.10.pairb
  25.9 0.0 collective-permute-done.9.paira
  25.9 0.0 collective-permute-done.7.gxa
  25.9 0.0 collective-permute-done.8.gxb
  25.9 2.2 %end.1 = (f32[18,144,256]{2,1,0:T(8,128)S(1)}, f32[66,48,256]{2,1,0:T(8,128)S(1)}, f32[64,32,256]{2,1,0:T(8,128)S(1)}, f32[16,128,256]{2,1,0:T(8,128)}, f32[64,32,256]{2,1,0:T(8,128)}) custom-call(f32[18,144,256]{2,1,0:T(8,128)S(1)} %get-tuple-element.53._0, ...), custom_call_target="tpu_custom_call", output_to_operand_aliasing={{0}: (0, {}), {1}: (1, {}), {2}: (2, {}), {4}: (3, {})} | custom-call | tf_op jit(solution)/shard_map/end/pallas_call | solution.py:670
Async XLA Ops:
  0.6 6.8 %copy-start.2 = (f32[16,128,256]{2,1,0:T(8,128)S(1)}, f32[16,128,256]{2,1,0:T(8,128)}, u32[]{:S(2)}) copy-start(f32[16,128,256]{2,1,0:T(8,128)} %fluid_hbm.1) | copy-start | bytes 6291460
  0.6 6.8 %copy-start.3 = (f32[64,32,256]{2,1,0:T(8,128)S(1)}, f32[64,32,256]{2,1,0:T(8,128)}, u32[]{:S(2)}) copy-start(f32[64,32,256]{2,1,0:T(8,128)} %fin_hbm.1) | copy-start | bytes 6291460
  2.8 8.0 %copy-start = (s32[16,128,256]{2,1,0:T(8,128)S(1)}, s32[16,128,256]{2,1,0:T(8,128)}, u32[]{:S(2)}) copy-start(s32[16,128,256]{2,1,0:T(8,128)} %act.3) | copy-start | bytes 6291460
  2.8 8.0 %copy-start.1 = (f32[64,32,256]{2,1,0:T(8,128)S(1)}, f32[64,32,256]{2,1,0:T(8,128)}, u32[]{:S(2)}) copy-start(f32[64,32,256]{2,1,0:T(8,128)} %src.3) | copy-start | bytes 6291460
  2.9 13.7 %collective-permute-start.3 = (f32[176,256]{1,0:T(8,128)S(1)}, f32[176,256]{1,0:T(8,128)S(1)}, u32[]{:S(2)}, u32[]{:S(2)}) collective-permute-start(f32[176,256]{1,0:T(8,128)S(1)} %get-tuple-element.44), channel_id=1, source_target_pairs={{0,2},{2,0},{4,6},{6,4},{1,3},{3,1},{5,7},{7,5},{8,10},{10,8},{12,... | collective-permute-start | bytes 540680 | tf_op jit(solution)/shard_map/ppermute | solution.py:441
  5.9 10.7 %collective-permute-start.4 = (f32[176,256]{1,0:T(8,128)S(1)}, f32[176,256]{1,0:T(8,128)S(1)}, u32[]{:S(2)}, u32[]{:S(2)}) collective-permute-start(f32[176,256]{1,0:T(8,128)S(1)} %get-tuple-element.45), channel_id=1, source_target_pairs={{0,6},{2,4},{4,2},{6,0},{1,7},{3,5},{5,3},{7,1},{8,14},{10,12},{12... | collective-permute-start | bytes 540680 | tf_op jit(solution)/shard_map/ppermute | solution.py:442
  8.5 1.9 %collective-permute-start = (f32[48,256]{1,0:T(8,128)S(1)}, f32[48,256]{1,0:T(8,128)S(1)}, u32[]{:S(2)}, u32[]{:S(2)}) collective-permute-start(f32[48,256]{1,0:T(8,128)S(1)} %get-tuple-element.35), channel_id=1, source_target_pairs={{0,1},{1,0},{2,3},{3,2},{4,5},{5,4},{6,7},{7,6},{8,9},{9,8},{10,11... | collective-permute-start | bytes 147464 | tf_op jit(solution)/shard_map/ppermute | solution.py:434
  8.6 4.2 %collective-permute-start.1 = (f32[48,256]{1,0:T(8,128)S(1)}, f32[48,256]{1,0:T(8,128)S(1)}, u32[]{:S(2)}, u32[]{:S(2)}) collective-permute-start(f32[48,256]{1,0:T(8,128)S(1)} %get-tuple-element.38), channel_id=1, source_target_pairs={{0,8},{1,9},{8,0},{9,1},{16,24},{17,25},{24,16},{25,17},{2,10},{3,... | collective-permute-start | bytes 147464 | tf_op jit(solution)/shard_map/ppermute | solution.py:429
  10.2 2.5 %collective-permute-start.2 = (f32[48,256]{1,0:T(8,128)S(1)}, f32[48,256]{1,0:T(8,128)S(1)}, u32[]{:S(2)}, u32[]{:S(2)}) collective-permute-start(f32[48,256]{1,0:T(8,128)S(1)} %get-tuple-element.39), channel_id=1, source_target_pairs={{0,1},{1,0},{8,16},{9,17},{16,8},{17,9},{24,25},{25,24},{2,3},{3,2... | collective-permute-start | bytes 147464 | tf_op jit(solution)/shard_map/ppermute | solution.py:430
  10.4 6.2 %collective-permute-start.5 = (f32[48,256]{1,0:T(8,128)S(1)}, f32[48,256]{1,0:T(8,128)S(1)}, u32[]{:S(2)}, u32[]{:S(2)}) collective-permute-start(f32[48,256]{1,0:T(8,128)S(1)} %get-tuple-element.46.refs_9_), channel_id=1, source_target_pairs={{0,4},{2,6},{4,0},{6,2},{1,5},{3,7},{5,1},{7,3},{8,12},{10,14},{12... | collective-permute-start | bytes 147464 | tf_op jit(solution)/shard_map/ppermute | solution.py:440
  17.7 8.2 %collective-permute-start.7 = (f32[128,256]{1,0:T(8,128)S(1)}, f32[128,256]{1,0:T(8,128)S(1)}, u32[]{:S(2)}, u32[]{:S(2)}) collective-permute-start(f32[128,256]{1,0:T(8,128)S(1)} %get-tuple-element.57), channel_id=1, source_target_pairs={{0,2},{1,3},{2,0},{3,1},{4,6},{5,7},{6,4},{7,5},{8,10},{9,11},{10,... | collective-permute-start | bytes 393224 | tf_op jit(solution)/shard_map/ppermute | solution.py:429
  19.2 6.7 %collective-permute-start.8 = (f32[128,256]{1,0:T(8,128)S(1)}, f32[128,256]{1,0:T(8,128)S(1)}, u32[]{:S(2)}, u32[]{:S(2)}) collective-permute-start(f32[128,256]{1,0:T(8,128)S(1)} %get-tuple-element.58), channel_id=1, source_target_pairs={{0,1},{1,0},{2,4},{3,5},{4,2},{5,3},{6,7},{7,6},{8,9},{9,8},{10,12... | collective-permute-start | bytes 393224 | tf_op jit(solution)/shard_map/ppermute | solution.py:430
  20.5 3.2 %collective-permute-start.6 = (f32[48,256]{1,0:T(8,128)S(1)}, f32[48,256]{1,0:T(8,128)S(1)}, u32[]{:S(2)}, u32[]{:S(2)}) collective-permute-start(f32[48,256]{1,0:T(8,128)S(1)} %get-tuple-element.52), channel_id=1, source_target_pairs={{0,1},{1,0},{2,3},{3,2},{4,5},{5,4},{6,7},{7,6},{8,9},{9,8},{10,11... | collective-permute-start | bytes 147464 | tf_op jit(solution)/shard_map/ppermute | solution.py:434
  21.1 4.8 %collective-permute-start.10 = (f32[48,256]{1,0:T(8,128)S(1)}, f32[48,256]{1,0:T(8,128)S(1)}, u32[]{:S(2)}, u32[]{:S(2)}) collective-permute-start(f32[48,256]{1,0:T(8,128)S(1)} %get-tuple-element.60), channel_id=1, source_target_pairs={{0,1},{1,0},{8,16},{9,17},{16,8},{17,9},{24,25},{25,24},{2,3},{3,2... | collective-permute-start | bytes 147464 | tf_op jit(solution)/shard_map/ppermute | solution.py:430
  21.2 4.7 %collective-permute-start.9 = (f32[48,256]{1,0:T(8,128)S(1)}, f32[48,256]{1,0:T(8,128)S(1)}, u32[]{:S(2)}, u32[]{:S(2)}) collective-permute-start(f32[48,256]{1,0:T(8,128)S(1)} %get-tuple-element.59), channel_id=1, source_target_pairs={{0,8},{1,9},{8,0},{9,1},{16,24},{17,25},{24,16},{25,17},{2,10},{3,... | collective-permute-start | bytes 147464 | tf_op jit(solution)/shard_map/ppermute | solution.py:429
